TPU v7x, 32 devices: a whole 2x2x4 slice. The times are simulated.
32 devices in a mesh: dp: 16 (over z, y, core), tensor: 2 (over x).
Axes of the slice: x: 2, y: 2, z: 4, core: 2. Of those that a mesh axis runs over, the one named last changes fastest.
Arguments:
- tokens: bfloat16 [32, 2048, 1024], P('dp', 'tensor'), may hold values from -6 to 6
- gain_attn: bfloat16 [1024], P('dp'), may hold values from 0.5 to 1.5
- w_query: bfloat16 [1024, 1024], P('dp', 'tensor'), may hold values from -0.375 to 0.375
- w_key: bfloat16 [1024, 1024], P('dp', 'tensor'), may hold values from -0.1875 to 0.1875
- w_value: bfloat16 [1024, 1024], P('dp', 'tensor'), may hold values from -0.1875 to 0.1875
- w_out: bfloat16 [1024, 1024], P('tensor', 'dp'), may hold values from -1 to 1
- gain_ffn: bfloat16 [1024], P('dp'), may hold values from 0.5 to 1.5
- w_gate: bfloat16 [1024, 2816], P('dp', 'tensor'), may hold values from -0.1875 to 0.1875
- w_up: bfloat16 [1024, 2816], P('dp', 'tensor'), may hold values from -0.1875 to 0.1875
- w_down: bfloat16 [2816, 1024], P('tensor', 'dp'), may hold values from -0.21875 to 0.21875
- cache_keys: bfloat16 [32, 1024, 1024], P('dp', None, 'tensor'), may hold values from -6 to 6
- cache_values: bfloat16 [32, 1024, 1024], P('dp', None, 'tensor'), may hold values from -6 to 6
- prefix: int32 [32], P('dp'), may hold values from 204 to 1024, as said below
- partner: int32 [32], P('dp'), may hold values from 0 to 31, each once
- own_blocks: int32 [32, 16, 4], P('dp'), may hold values from 0 to 15, all different within a row
- partner_blocks: int32 [32, 16, 4], P('dp'), may hold values from 0 to 15, all different within a row
- grad_out: bfloat16 [32, 2048, 1024], P('dp', 'tensor'), may hold values from -6 to 6
Outputs:
- out: bfloat16 [32, 2048, 1024], P('dp', 'tensor')
- grad_tokens: float32 [32, 2048, 1024], P('dp', 'tensor')
- grad_gain_attn: float32 [1024], replicated
- grad_w_query: float32 [1024, 1024], P('dp', 'tensor')
- grad_w_key: float32 [1024, 1024], P('dp', 'tensor')
- grad_w_value: float32 [1024, 1024], P('dp', 'tensor')
- grad_w_out: float32 [1024, 1024], P('tensor', 'dp')
- grad_gain_ffn: float32 [1024], replicated
- grad_w_gate: float32 [1024, 2816], P('dp', 'tensor')
- grad_w_up: float32 [1024, 2816], P('dp', 'tensor')
- grad_w_down: float32 [2816, 1024], P('tensor', 'dp')
Inputs may be any that keep to these rules, and one draw needn't show every extreme that they name: prefix[s] leading positions of sequence s see each other both ways; both the smallest and the largest allowed value occur. `partner`: every sequence number occurs exactly once. `own_blocks`: the 4 block numbers of one query block are distinct. `partner_blocks`: the 4 block numbers of one query block are distinct.
All inputs are finite; a program needn't handle non-finite values.
Results may differ from a plain program's by a relative error of at most 0.02.
Values may be sent and summed in bfloat16 or wider, within the bound.
A program may use at most 384 MiB of HBM per device.

v0:
```python
import jax
import jax.numpy as jnp
from jax import lax
from jax.sharding import PartitionSpec as P

HD = 128
L = 2048
CACHE_LEN = 1024
QBLOCK = 128
CBLOCK = 64
KR = 4
QROWS = 512


EPS = 1e-05
NEGATIVE = -1e30


def norm_rows(values, gain):
    scale_rows = lax.rsqrt(jnp.mean(values * values, axis=-1, keepdims=True) + EPS)
    return (values * scale_rows * gain, scale_rows)


def norm_back(grad_normed, values, scale_rows, gain):
    unit = values * scale_rows
    grad_unit = grad_normed * gain
    grad_values = scale_rows * (
        grad_unit - unit * jnp.mean(grad_unit * unit, axis=-1, keepdims=True)
    )
    return (grad_values, jnp.sum(grad_normed * unit, axis=0))


def inner_rows(left, right):
    return lax.dot_general(
        left, right, (((0,), (0,)), ((), ())), preferred_element_type=jnp.float32
    )


def outer_cols(left, right):
    return lax.dot_general(
        left, right, (((1,), (1,)), ((), ())), preferred_element_type=jnp.float32
    )


def memory_rows(cache_one, chosen, width):
    shaped = cache_one.reshape(CACHE_LEN // CBLOCK, CBLOCK, width)
    return jnp.take(shaped, chosen, axis=0)


def block_scores(query_block, keys_part, mem_part, first_row, limit):
    rows_here, heads_here, size = query_block.shape
    extent = keys_part.shape[0]
    local = jnp.einsum(
        "qhd,khd->hqk", query_block, keys_part, preferred_element_type=jnp.float32
    ) * size ** (-0.5)
    row_ids = first_row + jnp.arange(rows_here, dtype=jnp.int32)[:, None]
    key_ids = jnp.arange(extent, dtype=jnp.int32)[None, :]
    allowed = (key_ids <= row_ids) | (row_ids < limit) & (key_ids < limit)
    local = jnp.where(allowed[None], local, NEGATIVE)
    groups = mem_part.shape[0]
    grouped = query_block.reshape(groups, rows_here // groups, heads_here, size)
    remote = jnp.einsum(
        "bqhd,bkhd->hbqk", grouped, mem_part, preferred_element_type=jnp.float32
    ) * size ** (-0.5)
    return (local, remote.reshape(heads_here, rows_here, -1))


def attention_forward(query, keys, values, mem_keys, mem_values, limit):
    groups = QROWS // QBLOCK
    heads_here = query.shape[1]
    context_parts = []
    lse_parts = []
    for index in range(L // QROWS):
        first = index * QROWS
        extent = max(first + QROWS, L // 2)
        query_block = query[first : first + QROWS]
        mem_k = mem_keys[index * groups : (index + 1) * groups]
        mem_v = mem_values[index * groups : (index + 1) * groups]
        local, remote = block_scores(query_block, keys[:extent], mem_k, first, limit)
        top = jnp.maximum(jnp.max(local, axis=-1), jnp.max(remote, axis=-1))
        e_local = jnp.exp(local - top[..., None])
        e_remote = jnp.exp(remote - top[..., None])
        total = jnp.sum(e_local, axis=-1) + jnp.sum(e_remote, axis=-1)
        p_local = (e_local / total[..., None]).astype(jnp.bfloat16)
        p_remote = (
            (e_remote / total[..., None])
            .astype(jnp.bfloat16)
            .reshape(heads_here, groups, QBLOCK, -1)
        )
        part = jnp.einsum(
            "hqk,khd->qhd", p_local, values[:extent], preferred_element_type=jnp.float32
        )
        extra = jnp.einsum("hbqk,bkhd->bqhd", p_remote, mem_v, preferred_element_type=jnp.float32)
        context_parts.append(part + extra.reshape(part.shape))
        lse_parts.append(top + jnp.log(total))
    return (jnp.concatenate(context_parts, axis=0), lse_parts)


def attention_backward(query, keys, values, mem_keys, mem_values, limit, lse_parts, grad_context):
    groups = QROWS // QBLOCK
    length, heads_here, size = query.shape
    scale = size ** (-0.5)
    grad_query_parts = []
    grad_keys = jnp.zeros(query.shape, jnp.float32)
    grad_values = jnp.zeros(query.shape, jnp.float32)
    for index in range(L // QROWS):
        first = index * QROWS
        extent = max(first + QROWS, L // 2)
        query_block = query[first : first + QROWS]
        mem_k = mem_keys[index * groups : (index + 1) * groups]
        mem_v = mem_values[index * groups : (index + 1) * groups]
        local, remote = block_scores(query_block, keys[:extent], mem_k, first, limit)
        lse_block = lse_parts[index][..., None]
        p_local = jnp.exp(local - lse_block)
        p_remote = jnp.exp(remote - lse_block)
        grad_block = grad_context[first : first + QROWS]
        grouped_grad = grad_block.reshape(groups, QBLOCK, heads_here, size)
        dp_local = jnp.einsum(
            "qhd,khd->hqk", grad_block, values[:extent], preferred_element_type=jnp.float32
        )
        dp_remote = jnp.einsum(
            "bqhd,bkhd->hbqk", grouped_grad, mem_v, preferred_element_type=jnp.float32
        )
        dp_remote = dp_remote.reshape(heads_here, QROWS, -1)
        delta = jnp.sum(p_local * dp_local, axis=-1) + jnp.sum(p_remote * dp_remote, axis=-1)
        ds_local = (p_local * (dp_local - delta[..., None])).astype(jnp.bfloat16)
        ds_remote = (p_remote * (dp_remote - delta[..., None])).astype(jnp.bfloat16)
        ds_remote = ds_remote.reshape(heads_here, groups, QBLOCK, -1)
        dq_block = jnp.einsum(
            "hqk,khd->qhd", ds_local, keys[:extent], preferred_element_type=jnp.float32
        )
        dq_extra = jnp.einsum(
            "hbqk,bkhd->bqhd", ds_remote, mem_k, preferred_element_type=jnp.float32
        )
        grad_query_parts.append((dq_block + dq_extra.reshape(dq_block.shape)) * scale)
        dk_part = (
            jnp.einsum("hqk,qhd->khd", ds_local, query_block, preferred_element_type=jnp.float32)
            * scale
        )
        dv_part = jnp.einsum(
            "hqk,qhd->khd",
            p_local.astype(jnp.bfloat16),
            grad_block,
            preferred_element_type=jnp.float32,
        )
        grad_keys = grad_keys.at[:extent].add(dk_part)
        grad_values = grad_values.at[:extent].add(dv_part)
    return (jnp.concatenate(grad_query_parts, axis=0), grad_keys, grad_values)


def body(
    tokens,
    gain_attn,
    w_query,
    w_key,
    w_value,
    w_out,
    gain_ffn,
    w_gate,
    w_up,
    w_down,
    cache_keys,
    cache_values,
    prefix,
    partner,
    own_blocks,
    partner_blocks,
    grad_out,
):
    micro, shard_len, width = tokens.shape
    cols = w_query.shape[1]
    heads_local = cols // HD
    qblocks = L // QBLOCK
    mem_len = 2 * KR * CBLOCK
    piece_keys = lax.all_gather(cache_keys, "dp", axis=0, tiled=True)
    piece_values = lax.all_gather(cache_values, "dp", axis=0, tiled=True)
    count = piece_keys.shape[0]
    onehot = (partner[:, None] == jnp.arange(count, dtype=jnp.int32)[None, :]).astype(jnp.bfloat16)
    add_keys = jnp.einsum("mn,nkc->mkc", onehot, piece_keys, preferred_element_type=jnp.float32)
    add_values = jnp.einsum("mn,nkc->mkc", onehot, piece_values, preferred_element_type=jnp.float32)
    fetched_keys = add_keys.astype(jnp.bfloat16)
    fetched_values = add_values.astype(jnp.bfloat16)
    totals = (
        jnp.zeros((width, cols), jnp.float32),
        jnp.zeros((width, cols), jnp.float32),
        jnp.zeros((width, cols), jnp.float32),
        jnp.zeros((cols, width), jnp.float32),
        jnp.zeros((width, w_gate.shape[1]), jnp.float32),
        jnp.zeros((width, w_gate.shape[1]), jnp.float32),
        jnp.zeros((w_gate.shape[1], width), jnp.float32),
    )
    shares = tuple(
        (
            jnp.zeros(w.shape, jnp.float32)
            for w in (w_query, w_key, w_value, w_out, w_gate, w_up, w_down)
        )
    )
    gain_total_attn = jnp.zeros((width,), jnp.float32)
    gain_total_ffn = jnp.zeros((width,), jnp.float32)
    out_rows = []
    grad_rows = []
    for step in range(micro):
        fwd = (
            lax.all_gather(gain_attn, "dp", axis=0, tiled=True),
            lax.all_gather(w_query, "dp", axis=0, tiled=True),
            lax.all_gather(w_key, "dp", axis=0, tiled=True),
            lax.all_gather(w_value, "dp", axis=0, tiled=True),
            lax.all_gather(w_out, "dp", axis=1, tiled=True),
            lax.all_gather(gain_ffn, "dp", axis=0, tiled=True),
            lax.all_gather(w_gate, "dp", axis=0, tiled=True),
            lax.all_gather(w_up, "dp", axis=0, tiled=True),
            lax.all_gather(w_down, "dp", axis=1, tiled=True),
        )
        g_attn, wq_full, wk_full, wv_full, wo_full, g_ffn, wg_full, wu_full, wd_full = fwd
        limit = prefix[step]
        own_k = memory_rows(cache_keys[step], own_blocks[step], cols)
        par_k = memory_rows(fetched_keys[step], partner_blocks[step], cols)
        own_v = memory_rows(cache_values[step], own_blocks[step], cols)
        par_v = memory_rows(fetched_values[step], partner_blocks[step], cols)
        mem_keys = jnp.concatenate([own_k, par_k], axis=1).reshape(
            qblocks, mem_len, heads_local, HD
        )
        mem_values = jnp.concatenate([own_v, par_v], axis=1).reshape(
            qblocks, mem_len, heads_local, HD
        )
        token_rows = tokens[step].astype(jnp.float32)
        normed, scale_one = norm_rows(token_rows, g_attn.astype(jnp.float32))
        normed_all = lax.all_gather(normed.astype(jnp.bfloat16), "tensor", axis=0, tiled=True)
        query = (
            jnp.dot(normed_all, wq_full, preferred_element_type=jnp.float32)
            .astype(jnp.bfloat16)
            .reshape(L, heads_local, HD)
        )
        keys = (
            jnp.dot(normed_all, wk_full, preferred_element_type=jnp.float32)
            .astype(jnp.bfloat16)
            .reshape(L, heads_local, HD)
        )
        values = (
            jnp.dot(normed_all, wv_full, preferred_element_type=jnp.float32)
            .astype(jnp.bfloat16)
            .reshape(L, heads_local, HD)
        )
        context_full, lse_parts = attention_forward(
            query, keys, values, mem_keys, mem_values, limit
        )
        context = context_full.reshape(L, cols).astype(jnp.bfloat16)
        mixed = token_rows + lax.psum_scatter(
            jnp.dot(context, wo_full, preferred_element_type=jnp.float32),
            "tensor",
            scatter_dimension=0,
            tiled=True,
        )
        normed_two, scale_two = norm_rows(mixed, g_ffn.astype(jnp.float32))
        normed_two_all = lax.all_gather(
            normed_two.astype(jnp.bfloat16), "tensor", axis=0, tiled=True
        )
        gate = jnp.dot(normed_two_all, wg_full, preferred_element_type=jnp.float32)
        upward = jnp.dot(normed_two_all, wu_full, preferred_element_type=jnp.float32)
        sigma = jax.nn.sigmoid(gate)
        silu_gate = gate * sigma
        hidden = (silu_gate * upward).astype(jnp.bfloat16)
        out_rows.append(
            (
                mixed
                + lax.psum_scatter(
                    jnp.dot(hidden, wd_full, preferred_element_type=jnp.float32).astype(
                        jnp.bfloat16
                    ),
                    "tensor",
                    scatter_dimension=0,
                    tiled=True,
                ).astype(jnp.float32)
            ).astype(jnp.bfloat16)
        )
        bwd = (
            lax.all_gather(gain_attn, "dp", axis=0, tiled=True),
            lax.all_gather(w_query, "dp", axis=0, tiled=True),
            lax.all_gather(w_key, "dp", axis=0, tiled=True),
            lax.all_gather(w_value, "dp", axis=0, tiled=True),
            lax.all_gather(w_out, "dp", axis=1, tiled=True),
            lax.all_gather(gain_ffn, "dp", axis=0, tiled=True),
            lax.all_gather(w_gate, "dp", axis=0, tiled=True),
            lax.all_gather(w_up, "dp", axis=0, tiled=True),
            lax.all_gather(w_down, "dp", axis=1, tiled=True),
        )
        g_attn, wq_full, wk_full, wv_full, wo_full, g_ffn, wg_full, wu_full, wd_full = bwd
        grad_here = grad_out[step]
        grad_all = lax.all_gather(grad_here, "tensor", axis=0, tiled=True)
        d_down = inner_rows(hidden, grad_all)
        grad_hidden = outer_cols(grad_all, wd_full)
        grad_gate = (grad_hidden * upward * sigma * (1.0 + gate * (1.0 - sigma))).astype(
            jnp.bfloat16
        )
        grad_up = (grad_hidden * silu_gate).astype(jnp.bfloat16)
        d_gate = inner_rows(normed_two_all, grad_gate)
        d_up = inner_rows(normed_two_all, grad_up)
        grad_normed_two = lax.psum_scatter(
            outer_cols(grad_gate, wg_full) + outer_cols(grad_up, wu_full),
            "tensor",
            scatter_dimension=0,
            tiled=True,
        )
        grad_mixed_norm, gain_part_ffn = norm_back(
            grad_normed_two, mixed, scale_two, g_ffn.astype(jnp.float32)
        )
        grad_mixed = grad_here.astype(jnp.float32) + grad_mixed_norm
        branch_all = lax.all_gather(grad_mixed.astype(jnp.bfloat16), "tensor", axis=0, tiled=True)
        d_out = inner_rows(context, branch_all)
        grad_context = (
            outer_cols(branch_all, wo_full).astype(jnp.bfloat16).reshape(L, heads_local, HD)
        )
        grad_query, grad_keys, grad_values = attention_backward(
            query, keys, values, mem_keys, mem_values, limit, lse_parts, grad_context
        )
        grad_query = grad_query.reshape(L, cols).astype(jnp.bfloat16)
        grad_keys = grad_keys.reshape(L, cols).astype(jnp.bfloat16)
        grad_values = grad_values.reshape(L, cols).astype(jnp.bfloat16)
        d_query = inner_rows(normed_all, grad_query)
        d_key = inner_rows(normed_all, grad_keys)
        d_value = inner_rows(normed_all, grad_values)
        grad_normed = lax.psum_scatter(
            (
                outer_cols(grad_query, wq_full)
                + outer_cols(grad_keys, wk_full)
                + outer_cols(grad_values, wv_full)
            ).astype(jnp.bfloat16),
            "tensor",
            scatter_dimension=0,
            tiled=True,
        ).astype(jnp.float32)
        grad_token_norm, gain_part_attn = norm_back(
            grad_normed, token_rows, scale_one, g_attn.astype(jnp.float32)
        )
        grad_rows.append(grad_mixed + grad_token_norm)
        gain_total_attn = gain_total_attn + gain_part_attn
        gain_total_ffn = gain_total_ffn + gain_part_ffn
        totals = tuple(
            (
                held + fresh
                for held, fresh in zip(
                    totals, (d_query, d_key, d_value, d_out, d_gate, d_up, d_down)
                )
            )
        )
    shares = (
        lax.psum_scatter(
            totals[0].astype(jnp.bfloat16), "dp", scatter_dimension=0, tiled=True
        ).astype(jnp.float32),
        lax.psum_scatter(
            totals[1].astype(jnp.bfloat16), "dp", scatter_dimension=0, tiled=True
        ).astype(jnp.float32),
        lax.psum_scatter(
            totals[2].astype(jnp.bfloat16), "dp", scatter_dimension=0, tiled=True
        ).astype(jnp.float32),
        lax.psum_scatter(
            totals[3].astype(jnp.bfloat16), "dp", scatter_dimension=1, tiled=True
        ).astype(jnp.float32),
        lax.psum_scatter(
            totals[4].astype(jnp.bfloat16), "dp", scatter_dimension=0, tiled=True
        ).astype(jnp.float32),
        lax.psum_scatter(
            totals[5].astype(jnp.bfloat16), "dp", scatter_dimension=0, tiled=True
        ).astype(jnp.float32),
        lax.psum_scatter(
            totals[6].astype(jnp.bfloat16), "dp", scatter_dimension=1, tiled=True
        ).astype(jnp.float32),
    )
    gain_attn_sum, gain_ffn_sum = lax.psum((gain_total_attn, gain_total_ffn), ("dp", "tensor"))
    return (
        jnp.stack(out_rows, axis=0),
        jnp.stack(grad_rows, axis=0),
        gain_attn_sum,
        shares[0],
        shares[1],
        shares[2],
        shares[3],
        gain_ffn_sum,
        shares[4],
        shares[5],
        shares[6],
    )


def solution(mesh):
    in_specs = (
        P("dp", "tensor", None),
        P("dp"),
        P("dp", "tensor"),
        P("dp", "tensor"),
        P("dp", "tensor"),
        P("tensor", "dp"),
        P("dp"),
        P("dp", "tensor"),
        P("dp", "tensor"),
        P("tensor", "dp"),
        P("dp", None, "tensor"),
        P("dp", None, "tensor"),
        P("dp"),
        P("dp"),
        P("dp", None, None),
        P("dp", None, None),
        P("dp", "tensor", None),
    )
    out_specs = (
        P("dp", "tensor", None),
        P("dp", "tensor", None),
        P(),
        P("dp", "tensor"),
        P("dp", "tensor"),
        P("dp", "tensor"),
        P("tensor", "dp"),
        P(),
        P("dp", "tensor"),
        P("dp", "tensor"),
        P("tensor", "dp"),
    )
    return jax.shard_map(body, mesh=mesh, in_specs=in_specs, out_specs=out_specs, check_vma=False)
```

profile of v0, /device:TPU:0, one launch (start us, length us, event | category | flops | bytes accessed | tf_op | source)
XLA Modules:
  0.0 2620.9 jit_solution(4970742204714353736)
XLA Ops:
  11.6 35.7 %all-reduce.7 = (bf16[1024]{0:T(1024)(128)(2,1)S(1)}, bf16[1024]{0:T(1024)(128)(2,1)}) all-reduce(bf16[1024]{0:T(1024)(128)(2,1)S(1)} %dynamic-update-slice.44, bf16[1024]{0:T(1024)(128)(2,1)S(1)} %dynamic-update-slice.45), channel_id=1, replica_groups=mesh['dp'=16,'tensor'=2] {'dp'}, use_global_device_ids=true, to_apply=%add.4 | all-reduce | flops 2048 | bytes 8192
  115.5 32.7 %all-gather.22.cloned.1.call-done = bf16[1024,512]{1,0:T(8,128)(2,1)} async-done(((bf16[64,512]{1,0:T(8,128)(2,1)}), bf16[1024,512]{1,0:T(8,128)(2,1)}) %all-gather.22.cloned.1.call-update) | async-done | bytes 1048592 | tf_op jit(solution)/shard_map/all_gather | solution.py:207
  156.1 49.3 %all-gather.20.cloned.1.call-done = bf16[2048,1024]{1,0:T(8,128)(2,1)} async-done(((bf16[1024,1024]{1,0:T(8,128)(2,1)}), bf16[2048,1024]{1,0:T(8,128)(2,1)}) %all-gather.20.cloned.1.call-update) | async-done | bytes 4194320 | tf_op jit(solution)/shard_map/all_gather | solution.py:228
  219.8 25.6 all-gather.24.cloned.1.call-done
  245.3 18.4 convolution_convert_fusion.5
  331.1 9.9 fusion.413
  350.6 63.2 %all-gather.30.cloned.1.call-done = bf16[32,1024,512]{2,1,0:T(8,128)(2,1)} async-done(((bf16[2,1024,512]{2,1,0:T(8,128)(2,1)}), bf16[32,1024,512]{2,1,0:T(8,128)(2,1)}) %all-gather.30.cloned.1.call-update) | async-done | bytes 33554448 | tf_op jit(solution)/shard_map/all_gather | solution.py:176
  413.8 32.3 %fusion.102 = bf16[2,1024,512]{2,0,1:T(2,128)(2,1)S(1)} fusion(bf16[32,1024,512]{2,1,0:T(8,128)(2,1)} %all-gather.30.cloned.1.call-done, s32[2]{0:T(128)S(1)} %copy-done.190), kind=kOutput, calls=%fused_computation.264 | convolution fusion | flops 68157504 | bytes 35651592 | tf_op jit(solution)/shard_map/mn,nkc->mkc/dot_general | solution.py:180
  449.7 133.8 %all-gather.28.cloned.1.call-done = bf16[32,1024,512]{2,1,0:T(8,128)(2,1)} async-done(((bf16[2,1024,512]{2,1,0:T(8,128)(2,1)}), bf16[32,1024,512]{2,1,0:T(8,128)(2,1)}) %all-gather.28.cloned.1.call-update) | async-done | bytes 33554448 | tf_op jit(solution)/shard_map/all_gather | solution.py:175
  583.5 33.3 %fusion.99 = bf16[2,1024,512]{2,0,1:T(2,128)(2,1)} fusion(bf16[32,1024,512]{2,1,0:T(8,128)(2,1)} %all-gather.28.cloned.1.call-done, s32[2]{0:T(128)S(1)} %copy-done.190), kind=kOutput, calls=%fused_computation.263 | convolution fusion | flops 68157504 | bytes 35651592 | tf_op jit(solution)/shard_map/mn,nkc->mkc/dot_general | solution.py:179
  962.8 98.6 %reduce-scatter.20.cloned.1.call-done = f32[1024,1024]{1,0:T(8,128)} async-done(((f32[2048,1024]{1,0:T(8,128)}), f32[1024,1024]{1,0:T(8,128)}) %reduce-scatter.20.cloned.1.call-update) | async-done | bytes 4194320 | tf_op jit(solution)/shard_map/reduce_scatter | solution.py:248
  1078.9 29.2 %all-gather.38.cloned.1.call-done = bf16[1024,1408]{1,0:T(8,128)(2,1)} async-done(((bf16[64,1408]{1,0:T(8,128)(2,1)}), bf16[1024,1408]{1,0:T(8,128)(2,1)}) %all-gather.38.cloned.1.call-update) | async-done | bytes 2883600 | tf_op jit(solution)/shard_map/all_gather | solution.py:211
  1108.1 56.5 %all-gather.34.cloned.1.call-done = bf16[2048,1024]{1,0:T(8,128)(2,1)} async-done(((bf16[1024,1024]{1,0:T(8,128)(2,1)}), bf16[2048,1024]{1,0:T(8,128)(2,1)}) %all-gather.34.cloned.1.call-update) | async-done | bytes 4194320 | tf_op jit(solution)/shard_map/all_gather | solution.py:255
  1164.6 11.8 fusion.423
  1176.4 34.9 %all-gather.36.cloned.1.call-done = bf16[1024,1408]{1,0:T(8,128)(2,1)} async-done(((bf16[64,1408]{1,0:T(8,128)(2,1)}), bf16[1024,1408]{1,0:T(8,128)(2,1)}) %all-gather.36.cloned.1.call-update) | async-done | bytes 2883600 | tf_op jit(solution)/shard_map/all_gather | solution.py:210
  1211.3 11.8 fusion.422
  1223.1 44.7 %all-gather.50.cloned.1.call-done = bf16[1,2048,1024]{2,1,0:T(8,128)(2,1)} async-done(((bf16[1,1024,1024]{2,1,0:T(8,128)(2,1)}), bf16[1,2048,1024]{2,1,0:T(8,128)(2,1)}) %all-gather.50.cloned.1.call-update) | async-done | bytes 4194320 | tf_op jit(solution)/shard_map/all_gather | solution.py:289
  1267.8 46.5 %all-gather.40.cloned.1.call-done = bf16[1408,1024]{0,1:T(8,128)(2,1)} async-done(((bf16[1408,64]{0,1:T(8,128)(2,1)}), bf16[1408,1024]{0,1:T(8,128)(2,1)}) %all-gather.40.cloned.1.call-update) | async-done | bytes 2883600 | tf_op jit(solution)/shard_map/all_gather | solution.py:212
  1314.3 21.4 multiply_convert_fusion.6
  1335.8 9.7 fusion.427
  1354.8 97.6 %reduce-scatter.24.cloned.1.call-done = f32[1024,1024]{1,0:T(8,128)} async-done(((f32[2048,1024]{1,0:T(8,128)}), f32[1024,1024]{1,0:T(8,128)}) %reduce-scatter.24.cloned.1.call-update) | async-done | bytes 4194320 | tf_op jit(solution)/shard_map/reduce_scatter | solution.py:298
  1460.2 56.3 %all-gather.44.cloned.1.call-done = bf16[2048,1024]{1,0:T(8,128)(2,1)} async-done(((bf16[1024,1024]{1,0:T(8,128)(2,1)}), bf16[2048,1024]{1,0:T(8,128)(2,1)}) %all-gather.44.cloned.1.call-update) | async-done | bytes 4194320 | tf_op jit(solution)/shard_map/all_gather | solution.py:255
  1516.5 11.2 fusion.426
  1537.2 37.6 %all-gather.52.cloned.1.call-done = bf16[1,2048,1024]{2,1,0:T(8,128)(2,1)} async-done(((bf16[1,1024,1024]{2,1,0:T(8,128)(2,1)}), bf16[1,2048,1024]{2,1,0:T(8,128)(2,1)}) %all-gather.52.cloned.1.call-update) | async-done | bytes 4194320 | tf_op jit(solution)/shard_map/all_gather | solution.py:289
  1574.8 20.2 multiply_convert_fusion.4
  1614.0 11.0 convolution_convert_fusion
  1625.1 88.2 %reduce-scatter.28.cloned.1.call-done = f32[1024,1024]{1,0:T(8,128)} async-done(((f32[2048,1024]{1,0:T(8,128)}), f32[1024,1024]{1,0:T(8,128)}) %reduce-scatter.28.cloned.1.call-update) | async-done | bytes 4194320 | tf_op jit(solution)/shard_map/reduce_scatter | solution.py:298
  1718.5 51.3 %reduce-scatter.22.cloned.1.call-done = bf16[1024,1024]{1,0:T(8,128)(2,1)} async-done(((bf16[2048,1024]{1,0:T(8,128)(2,1)}), bf16[1024,1024]{1,0:T(8,128)(2,1)}) %reduce-scatter.22.cloned.1.call-update) | async-done | bytes 2097168 | tf_op jit(solution)/shard_map/reduce_scatter | solution.py:266
  1769.8 11.6 fusion.401
  1782.3 10.8 fusion.77
  1801.6 11.0 fusion.437
  1812.6 11.0 add_convert_fusion.4
  1823.7 10.6 fusion.438
  1834.3 11.1 add_convert_fusion.3
  1864.5 32.2 %all-gather.46.cloned.1.call-done = bf16[2048,1024]{1,0:T(8,128)(2,1)} async-done(((bf16[1024,1024]{1,0:T(8,128)(2,1)}), bf16[2048,1024]{1,0:T(8,128)(2,1)}) %all-gather.46.cloned.1.call-update) | async-done | bytes 4194320 | tf_op jit(solution)/shard_map/all_gather | solution.py:308
  2063.4 11.7 multiply_reduce_fusion
  2075.2 11.1 multiply_reduce_fusion.1
  2162.6 9.8 fusion.124
  2178.4 11.4 fusion.70
  2198.1 10.1 multiply_convert_fusion.2
  2210.9 15.9 multiply_convert_fusion
  2234.1 11.0 multiply_convert_fusion.1
  2310.2 10.9 convolution_convert_fusion.1
  2329.3 38.6 %reduce-scatter.32.cloned.1.call-done = bf16[64,512]{1,0:T(8,128)(2,1)} async-done(((bf16[1024,512]{1,0:T(8,128)(2,1)}), bf16[64,512]{1,0:T(8,128)(2,1)}) %reduce-scatter.32.cloned.1.call-update) | async-done | bytes 65552 | tf_op jit(solution)/shard_map/reduce_scatter | solution.py:347
  2369.3 59.1 %reduce-scatter.34.cloned.1.call-done = bf16[64,512]{1,0:T(8,128)(2,1)} async-done(((bf16[1024,512]{1,0:T(8,128)(2,1)}), bf16[64,512]{1,0:T(8,128)(2,1)}) %reduce-scatter.34.cloned.1.call-update) | async-done | bytes 65552 | tf_op jit(solution)/shard_map/reduce_scatter | solution.py:350
  2429.9 54.5 %reduce-scatter.30.cloned.1.call-done = bf16[1024,1024]{1,0:T(8,128)(2,1)} async-done(((bf16[2048,1024]{1,0:T(8,128)(2,1)}), bf16[1024,1024]{1,0:T(8,128)(2,1)}) %reduce-scatter.30.cloned.1.call-update) | async-done | bytes 2097168 | tf_op jit(solution)/shard_map/reduce_scatter | solution.py:322
  2484.4 57.3 %reduce-scatter.26.cloned.1.call-done = bf16[1024,1024]{1,0:T(8,128)(2,1)} async-done(((bf16[2048,1024]{1,0:T(8,128)(2,1)}), bf16[1024,1024]{1,0:T(8,128)(2,1)}) %reduce-scatter.26.cloned.1.call-update) | async-done | bytes 2097168 | tf_op jit(solution)/shard_map/reduce_scatter | solution.py:322
  2546.9 40.0 %all-reduce.6 = (f32[1024]{0:T(1024)}, f32[1024]{0:T(1024)}) all-reduce(f32[1024]{0:T(1024)S(1)} %add.769, f32[1024]{0:T(1024)S(1)} %add.774), channel_id=1, replica_groups=mesh['dp'=16,'tensor'=2] {'dp','tensor'}, use_global_device_ids=true, to_apply=%region_66.68 | all-reduce | flops 2048 | bytes 16384 | tf_op jit(solution)/shard_map/psum | solution.py:369
  (976 shorter events, 989.9 us)
Async XLA Ops:
  7.2 97.3 %all-gather.26.cloned.1.call-start = ((), (), s32[]{:S(2)}) async-start(), calls=%async_computation.18 | async-start | bytes 1114112 | tf_op jit(solution)/shard_map/all_gather | solution.py:206
  7.9 100.2 %all-gather.42.cloned.1.call-start = ((), (), s32[]{:S(2)}) async-start(), calls=%async_computation.28 | async-start | bytes 6291456 | tf_op jit(solution)/shard_map/all_gather | solution.py:228
  53.4 94.8 %all-gather.22.cloned.1.call-start = ((), (), s32[]{:S(2)}) async-start(), calls=%async_computation.16 | async-start | bytes 1114112 | tf_op jit(solution)/shard_map/all_gather | solution.py:207
  54.2 151.2 %all-gather.20.cloned.1.call-start = ((), (), s32[]{:S(2)}) async-start(), calls=%async_computation.15 | async-start | bytes 6291456 | tf_op jit(solution)/shard_map/all_gather | solution.py:228
  54.7 190.6 %all-gather.24.cloned.1.call-start = ((), (), s32[]{:S(2)}) async-start(), calls=%async_computation.17 | async-start | bytes 1114112 | tf_op jit(solution)/shard_map/all_gather | solution.py:205
  55.3 358.5 %all-gather.30.cloned.1.call-start = ((), (), s32[]{:S(2)}) async-start(), calls=%async_computation.20 | async-start | bytes 35651584 | tf_op jit(solution)/shard_map/all_gather | solution.py:176
  55.9 527.6 %all-gather.28.cloned.1.call-start = ((), (), s32[]{:S(2)}) async-start(), calls=%async_computation.19 | async-start | bytes 35651584 | tf_op jit(solution)/shard_map/all_gather | solution.py:175
  56.7 766.8 %all-gather.32.cloned.1.call-start = ((), (), s32[]{:S(2)}) async-start(), calls=%async_computation.21 | async-start | bytes 1114112 | tf_op jit(solution)/shard_map/all_gather | solution.py:208
  57.4 905.4 %reduce-scatter.16.cloned.1.call-start = ((), (), s32[]{:S(2)}) async-start(), calls=%async_computation.22 | async-start | bytes 12582912 | tf_op jit(solution)/shard_map/reduce_scatter | solution.py:248
  113.0 228.0 %copy-start.25 = (bf16[2048,512]{0,1:T(8,128)(2,1)}, bf16[2048,512]{0,1:T(8,128)(2,1)S(1)}, u32[]{:S(2)}) copy-start(bf16[2048,512]{0,1:T(8,128)(2,1)S(1)} %convolution_convert_fusion.4) | copy-start | bytes 6291460
  210.1 83.5 %copy-start.29 = (bf16[1024,512]{0,1:T(8,128)(2,1)}, bf16[1024,512]{0,1:T(8,128)(2,1)S(1)}, u32[]{:S(2)}) copy-start(bf16[1024,512]{0,1:T(8,128)(2,1)S(1)} %slice.808) | copy-start | bytes 3145732
  341.0 72.8 %copy-start.190 = (s32[2]{0:T(128)S(1)}, s32[2]{0:T(128)}, u32[]{:S(2)}) copy-start(s32[2]{0:T(128)} %param.72) | copy-start | bytes 28
  350.0 96.1 %copy-start.160 = (f32[4,512]{1,0:T(4,128)}, f32[4,512]{1,0:T(4,128)S(1)}, u32[]{:S(2)}) copy-start(f32[4,512]{1,0:T(4,128)S(1)} %get-tuple-element.388) | copy-start | bytes 24580
  667.4 108.7 %copy-start.38 = (bf16[4,512,4,128]{3,2,1,0:T(4,128)(2,1)}, bf16[4,512,4,128]{3,2,1,0:T(4,128)(2,1)S(1)}, u32[]{:S(2)}) copy-start(bf16[4,512,4,128]{3,2,1,0:T(4,128)(2,1)S(1)} %slice.725) | copy-start | bytes 6291460
  831.2 230.3 %reduce-scatter.20.cloned.1.call-start = ((), (), s32[]{:S(2)}) async-start(), calls=%async_computation.29 | async-start | bytes 12582912 | tf_op jit(solution)/shard_map/reduce_scatter | solution.py:248
  962.0 146.1 %all-gather.38.cloned.1.call-start = ((), (), s32[]{:S(2)}) async-start(), calls=%async_computation.25 | async-start | bytes 3063808 | tf_op jit(solution)/shard_map/all_gather | solution.py:211
  962.7 201.9 %all-gather.34.cloned.1.call-start = ((), (), s32[]{:S(2)}) async-start(), calls=%async_computation.23 | async-start | bytes 6291456 | tf_op jit(solution)/shard_map/all_gather | solution.py:255
  962.8 807.1 %copy-start.145 = (f32[1024]{0:T(1024)}, f32[1024]{0:T(1024)S(1)}, u32[]{:S(2)}) copy-start(f32[1024]{0:T(1024)S(1)} %convert_element_type.363) | copy-start | bytes 12292
  1068.6 701.3 %copy-start.155 = (f32[1024]{0:T(1024)}, f32[1024]{0:T(1024)S(1)}, u32[]{:S(2)}) copy-start(f32[1024]{0:T(1024)S(1)} %add_rsqrt_fusion.2) | copy-start | bytes 12292
  1072.3 139.0 %all-gather.36.cloned.1.call-start = ((), (), s32[]{:S(2)}) async-start(), calls=%async_computation.24 | async-start | bytes 3063808 | tf_op jit(solution)/shard_map/all_gather | solution.py:210
  1073.1 194.8 %all-gather.50.cloned.1.call-start = ((), (), s32[]{:S(2)}) async-start(), calls=%async_computation.45 | async-start | bytes 6291456 | tf_op jit(solution)/shard_map/all_gather | solution.py:289
  1078.3 236.1 %all-gather.40.cloned.1.call-start = ((), (), s32[]{:S(2)}) async-start(), calls=%async_computation.26 | async-start | bytes 3063808 | tf_op jit(solution)/shard_map/all_gather | solution.py:212
  1078.8 373.6 %reduce-scatter.24.cloned.1.call-start = ((), (), s32[]{:S(2)}) async-start(), calls=%async_computation.32 | async-start | bytes 12582912 | tf_op jit(solution)/shard_map/reduce_scatter | solution.py:298
  1354.8 161.7 %all-gather.44.cloned.1.call-start = ((), (), s32[]{:S(2)}) async-start(), calls=%async_computation.30 | async-start | bytes 6291456 | tf_op jit(solution)/shard_map/all_gather | solution.py:255
  1354.8 415.0 %copy-start.157 = (f32[1024]{0:T(1024)}, f32[1024]{0:T(1024)S(1)}, u32[]{:S(2)}) copy-start(f32[1024]{0:T(1024)S(1)} %add_rsqrt_fusion) | copy-start | bytes 12292
  1459.6 115.2 %all-gather.52.cloned.1.call-start = ((), (), s32[]{:S(2)}) async-start(), calls=%async_computation.46 | async-start | bytes 6291456 | tf_op jit(solution)/shard_map/all_gather | solution.py:289
  1460.2 253.2 %reduce-scatter.28.cloned.1.call-start = ((), (), s32[]{:S(2)}) async-start(), calls=%async_computation.35 | async-start | bytes 12582912 | tf_op jit(solution)/shard_map/reduce_scatter | solution.py:298
  1614.0 155.9 %reduce-scatter.22.cloned.1.call-start = ((), (), s32[]{:S(2)}) async-start(), calls=%async_computation.31 | async-start | bytes 6291456 | tf_op jit(solution)/shard_map/reduce_scatter | solution.py:266
  1625.1 220.4 %all-gather.48.cloned.1.call-start = ((), (), s32[]{:S(2)}) async-start(), calls=%async_computation.36 | async-start | bytes 6291456 | tf_op jit(solution)/shard_map/all_gather | solution.py:308
  1625.1 144.7 %copy-start.178 = (f32[1024]{0:T(1024)}, f32[1024]{0:T(1024)S(1)}, u32[]{:S(2)}) copy-start(f32[1024]{0:T(1024)S(1)} %broadcast_multiply_fusion.3) | copy-start | bytes 12292
  1781.5 115.3 %all-gather.46.cloned.1.call-start = ((), (), s32[]{:S(2)}) async-start(), calls=%async_computation.33 | async-start | bytes 6291456 | tf_op jit(solution)/shard_map/all_gather | solution.py:308
  1782.2 538.9 %reduce-scatter.44.cloned.1.call-start = ((), (), s32[]{:S(2)}) async-start(), calls=%async_computation.44 | async-start | bytes 3063808 | tf_op jit(solution)/shard_map/reduce_scatter | solution.py:365
  1801.6 521.3 %reduce-scatter.40.cloned.1.call-start = ((), (), s32[]{:S(2)}) async-start(), calls=%async_computation.42 | async-start | bytes 3063808 | tf_op jit(solution)/shard_map/reduce_scatter | solution.py:359
  1823.6 500.9 %reduce-scatter.42.cloned.1.call-start = ((), (), s32[]{:S(2)}) async-start(), calls=%async_computation.43 | async-start | bytes 3063808 | tf_op jit(solution)/shard_map/reduce_scatter | solution.py:362
  1845.4 480.9 %reduce-scatter.38.cloned.1.call-start = ((), (), s32[]{:S(2)}) async-start(), calls=%async_computation.41 | async-start | bytes 1114112 | tf_op jit(solution)/shard_map/reduce_scatter | solution.py:356
  2189.8 137.9 %reduce-scatter.36.cloned.1.call-start = ((), (), s32[]{:S(2)}) async-start(), calls=%async_computation.40 | async-start | bytes 1114112 | tf_op jit(solution)/shard_map/reduce_scatter | solution.py:353
  2198.1 169.8 %reduce-scatter.32.cloned.1.call-start = ((), (), s32[]{:S(2)}) async-start(), calls=%async_computation.38 | async-start | bytes 1114112 | tf_op jit(solution)/shard_map/reduce_scatter | solution.py:347
  2265.0 163.4 %reduce-scatter.34.cloned.1.call-start = ((), (), s32[]{:S(2)}) async-start(), calls=%async_computation.39 | async-start | bytes 1114112 | tf_op jit(solution)/shard_map/reduce_scatter | solution.py:350
  2282.9 201.5 %reduce-scatter.30.cloned.1.call-start = ((), (), s32[]{:S(2)}) async-start(), calls=%async_computation.37 | async-start | bytes 6291456 | tf_op jit(solution)/shard_map/reduce_scatter | solution.py:322
  2296.3 245.4 %reduce-scatter.26.cloned.1.call-start = ((), (), s32[]{:S(2)}) async-start(), calls=%async_computation.34 | async-start | bytes 6291456 | tf_op jit(solution)/shard_map/reduce_scatter | solution.py:322
  2308.4 291.4 %reduce-scatter.18.cloned.1.call-start = ((), (), s32[]{:S(2)}) async-start(), calls=%async_computation.27 | async-start | bytes 6291456 | tf_op jit(solution)/shard_map/reduce_scatter | solution.py:266
  2321.1 220.7 %copy-start.154 = (f32[1024]{0:T(1024)S(1)}, f32[1024]{0:T(1024)}, u32[]{:S(2)}) copy-start(f32[1024]{0:T(1024)} %copy-done.153) | copy-start | bytes 12292
  2321.1 220.7 %copy-start.175 = (f32[1024]{0:T(1024)S(1)}, f32[1024]{0:T(1024)}, u32[]{:S(2)}) copy-start(f32[1024]{0:T(1024)} %copy-done.174) | copy-start | bytes 12292
  2321.1 220.7 %copy-start.177 = (f32[1024]{0:T(1024)S(1)}, f32[1024]{0:T(1024)}, u32[]{:S(2)}) copy-start(f32[1024]{0:T(1024)} %copy-done.176) | copy-start | bytes 12292
  2429.9 157.0 %copy-start.146 = (f32[1024]{0:T(1024)S(1)}, f32[1024]{0:T(1024)}, u32[]{:S(2)}) copy-start(f32[1024]{0:T(1024)} %copy-done.145) | copy-start | bytes 12292
  2429.9 157.0 %copy-start.158 = (f32[1024]{0:T(1024)S(1)}, f32[1024]{0:T(1024)}, u32[]{:S(2)}) copy-start(f32[1024]{0:T(1024)} %copy-done.157) | copy-start | bytes 12292
  2429.9 157.0 %copy-start.181 = (f32[1024]{0:T(1024)S(1)}, f32[1024]{0:T(1024)}, u32[]{:S(2)}) copy-start(f32[1024]{0:T(1024)} %copy-done.180) | copy-start | bytes 12292
  2484.4 102.5 %copy-start.77 = (bf16[1024,1024]{1,0:T(8,128)(2,1)S(1)}, bf16[1024,1024]{1,0:T(8,128)(2,1)}, u32[]{:S(2)}) copy-start(bf16[1024,1024]{1,0:T(8,128)(2,1)} %reduce-scatter.30.cloned.1.call-done) | copy-start | bytes 6291460
  (241 other events, 1803.5 us)
Sparse Core Ops, SparseCore 0:
  10.2 40.5 all-gather.25
  53.5 54.5 all-gather.41
  110.3 37.9 all-gather.21
  149.7 55.6 all-gather.19
  207.4 37.9 all-gather.23
  246.8 166.9 all-gather.29
  415.4 168.0 all-gather.27
  585.7 37.9 all-gather.31
  831.3 99.2 reduce-scatter.15
  962.1 99.2 reduce-scatter.19
  1063.7 44.3 all-gather.37
  1109.5 55.0 all-gather.33
  1166.9 44.3 all-gather.35
  1212.7 55.0 all-gather.49
  1269.9 44.3 all-gather.39
  1354.9 97.5 reduce-scatter.23
  1459.7 56.7 all-gather.43
  1518.0 56.7 all-gather.51
  1614.1 99.2 reduce-scatter.27
  1715.5 54.2 reduce-scatter.21
  1781.6 56.7 all-gather.47
  1840.0 56.7 all-gather.45
  1901.0 65.0 reduce-scatter.43
  1969.8 63.9 reduce-scatter.39
  2038.1 63.9 reduce-scatter.41
  2190.0 57.3 reduce-scatter.37
  2251.3 56.4 reduce-scatter.35
  2311.4 56.4 reduce-scatter.31
  2371.9 56.4 reduce-scatter.33
  2431.1 53.3 reduce-scatter.29
  2487.4 54.2 reduce-scatter.25
  2544.0 55.7 reduce-scatter.17
where the time goes:
time: 2630 us; the launch traced here: 2620 us
  waiting for transfers between devices  1200 us (46%)
  matrix products  783 us (30%)
  other arithmetic  280 us (11%)
  local copies, waits for them, and re-layouts  256 us (10%)
  blocking collectives  75.7 us (3%)
    reduce_scatter x2, waiting for transfers between devices, body(): lax.psum_scatter(outer_cols(grad_gate, wg_full) + outer_cols(grad_up, wu_...  186 us
    all_gather x1, waiting for transfers between devices, body(): piece_keys = lax.all_gather(cache_keys, 'dp', axis=0, tiled=True)  134 us
    dot_general x14, matrix products, outer_cols(): lax.dot_general(left, right, (((1,), (1,)), ((), ())), preferred_element_...  114 us
    all_gather x2, waiting for transfers between devices, body(): lax.all_gather(normed_two.astype(jnp.bfloat16), 'tensor', axis=0, tiled=T...  113 us
    reduce_scatter x2, waiting for transfers between devices, body(): lax.psum_scatter((outer_cols(grad_query, wq_full) + outer_cols(grad_keys,...  112 us
    reduce_scatter x2, waiting for transfers between devices, body(): lax.psum_scatter(jnp.dot(context, wo_full, preferred_element_type=jnp.flo...  98.6 us
    dot_general x14, matrix products, inner_rows(): lax.dot_general(left, right, (((0,), (0,)), ((), ())), preferred_element_...  91.2 us
    all_gather x2, waiting for transfers between devices, body(): grad_all = lax.all_gather(grad_here, 'tensor', axis=0, tiled=True)  82.3 us
  transfers between devices with their start and end apart: 32, of which 23 were waited for; matrix products, arithmetic and copies ran while one was open for 44% of the time, Pallas kernels for 0%

commit v1 on v0

--- a/solution.py
+++ b/solution.py
@@ -1,6 +1,10 @@
+import functools
+
 import jax
 import jax.numpy as jnp
 from jax import lax
+from jax.experimental import pallas as pl
+from jax.experimental.pallas import tpu as pltpu
 from jax.sharding import PartitionSpec as P
 
 HD = 128
@@ -148,7 +152,7 @@
     return (jnp.concatenate(grad_query_parts, axis=0), grad_keys, grad_values)
 
 
-def body(
+def tensor_body(
     tokens,
     gain_attn,
     w_query,
@@ -382,6 +386,580 @@
     )
 
 
+TQ = 512
+TK = 512
+ROWS = 512
+HT = 256
+SCALE = HD**-0.5
+EXP_SCALE = SCALE * 1.4426950408889634
+LOG2E = 1.4426950408889634
+NT = (((1,), (1,)), ((), ()))
+TN = (((0,), (0,)), ((), ()))
+F32 = jnp.float32
+BF16 = jnp.bfloat16
+MIB = 1 << 20
+
+
+def mm(left, right, dims=(((1,), (0,)), ((), ()))):
+    return lax.dot_general(left, right, dims, preferred_element_type=F32)
+
+
+def fold_max(values):
+    best = values[:, :HD]
+    for i in range(1, values.shape[1] // HD):
+        best = jnp.maximum(best, values[:, i * HD : (i + 1) * HD])
+    return best
+
+
+def fold_sum(values):
+    total = values[:, :HD]
+    for i in range(1, values.shape[1] // HD):
+        total = total + values[:, i * HD : (i + 1) * HD]
+    return total
+
+
+def reach_mask(first, tile, limit):
+    rows = first + lax.broadcasted_iota(jnp.int32, (TQ, 1), 0)
+    keys = tile * TK + lax.broadcasted_iota(jnp.int32, (1, TK), 1)
+    reach = jnp.where(rows < limit, jnp.maximum(rows, limit - 1), rows)
+    return keys <= reach
+
+
+def pick_blocks(meta, block, own, other, buf):
+    for i in range(KR):
+        c = meta[2 + block * KR + i]
+        buf[pl.ds(i * CBLOCK, CBLOCK), :] = own[0, pl.ds(pl.multiple_of(c * CBLOCK, CBLOCK), CBLOCK), :]
+        d = meta[2 + (L // QBLOCK) * KR + block * KR + i]
+        buf[pl.ds((KR + i) * CBLOCK, CBLOCK), :] = other[d, 0, 0]
+
+
+def attend_kernel(
+    meta, q_ref, k_ref, v_ref, ok_ref, ov_ref, pk_ref, pv_ref, ctx_ref, lse_ref, kbuf, vbuf, sbuf, smem, *, pair
+):
+    step = pl.program_id(1)
+    limit = meta[0]
+    first = step * TQ
+    free = jnp.where(first < limit, (limit + TK - 1) // TK, 0)
+    tiles = jnp.maximum(step + 1, free)
+    blocks = TQ // QBLOCK
+    for b in range(blocks):
+        pick_blocks(meta, step * blocks + b, ok_ref, pk_ref, kbuf.at[b])
+        pick_blocks(meta, step * blocks + b, ov_ref, pv_ref, vbuf.at[b])
+    state = []
+    for h in range(pair):
+        cs = pl.ds(h * HD, HD)
+        best = []
+        for b in range(blocks):
+            s = mm(q_ref[pl.ds(b * QBLOCK, QBLOCK), cs], kbuf[b, :, cs], NT)
+            smem[h, pl.ds(b * QBLOCK, QBLOCK), :] = s
+            best.append(fold_max(s))
+        state.append(jnp.concatenate(best, 0))
+
+    def scores(tile, state, masked):
+        ks = pl.ds(pl.multiple_of(tile * TK, TK), TK)
+        if masked:
+            allowed = reach_mask(first, tile, limit)
+        new = []
+        for h in range(pair):
+            cs = pl.ds(h * HD, HD)
+            s = mm(q_ref[:, cs], k_ref[ks, cs], NT)
+            if masked:
+                s = jnp.where(allowed, s, NEGATIVE)
+            sbuf[h, tile] = s
+            new.append(jnp.maximum(state[h], fold_max(s)))
+        return tuple(new)
+
+    state = lax.fori_loop(0, step, lambda tile, s: scores(tile, s, False), tuple(state))
+    state = lax.fori_loop(step, tiles, lambda tile, s: scores(tile, s, True), state)
+    tops = [jnp.max(s, axis=1, keepdims=True) for s in state]
+    state = []
+    for h in range(pair):
+        cs = pl.ds(h * HD, HD)
+        p = jnp.exp2((smem[h] - tops[h]) * EXP_SCALE)
+        low = p.astype(BF16)
+        parts = [mm(low[b * QBLOCK : (b + 1) * QBLOCK], vbuf[b, :, cs]) for b in range(blocks)]
+        state.append((fold_sum(p), jnp.concatenate(parts, 0)))
+
+    def weigh(tile, state):
+        ks = pl.ds(pl.multiple_of(tile * TK, TK), TK)
+        new = []
+        for h in range(pair):
+            total, acc = state[h]
+            p = jnp.exp2((sbuf[h, tile] - tops[h]) * EXP_SCALE)
+            new.append((total + fold_sum(p), acc + mm(p.astype(BF16), v_ref[ks, pl.ds(h * HD, HD)])))
+        return tuple(new)
+
+    state = lax.fori_loop(0, tiles, weigh, tuple(state))
+    for h in range(pair):
+        cs = pl.ds(h * HD, HD)
+        total = jnp.sum(state[h][0], axis=1, keepdims=True)
+        ctx_ref[:, cs] = (state[h][1] / total).astype(BF16)
+        lse_ref[:, cs] = jnp.broadcast_to(tops[h] * SCALE + jnp.log(total), (TQ, HD))
+
+
+def attend_back_kernel(
+    meta, q_ref, k_ref, v_ref, ok_ref, ov_ref, pk_ref, pv_ref, do_ref, ctx_ref, lse_ref,
+    dq_ref, dk_ref, dv_ref, kbuf, vbuf, dks, dvs, *, pair
+):
+    step = pl.program_id(1)
+    limit = meta[0]
+    first = step * TQ
+    free = jnp.where(first < limit, (limit + TK - 1) // TK, 0)
+    tiles = jnp.maximum(step + 1, free)
+    blocks = TQ // QBLOCK
+
+    @pl.when(step == 0)
+    def _():
+        dks[...] = jnp.zeros_like(dks)
+        dvs[...] = jnp.zeros_like(dvs)
+
+    for b in range(blocks):
+        pick_blocks(meta, step * blocks + b, ok_ref, pk_ref, kbuf.at[b])
+        pick_blocks(meta, step * blocks + b, ov_ref, pv_ref, vbuf.at[b])
+    state = []
+    aux = []
+    for h in range(pair):
+        cs = pl.ds(h * HD, HD)
+        delta = jnp.sum(do_ref[:, cs].astype(F32) * ctx_ref[:, cs].astype(F32), axis=1, keepdims=True)
+        lse2 = lse_ref[:, cs][:, :1] * LOG2E
+        aux.append((lse2, delta))
+        parts = []
+        for b in range(blocks):
+            rs = pl.ds(b * QBLOCK, QBLOCK)
+            s = mm(q_ref[rs, cs], kbuf[b, :, cs], NT)
+            p = jnp.exp2(s * EXP_SCALE - lse2[b * QBLOCK : (b + 1) * QBLOCK])
+            dp = mm(do_ref[rs, cs], vbuf[b, :, cs], NT)
+            ds = (p * (dp - delta[b * QBLOCK : (b + 1) * QBLOCK])).astype(BF16)
+            parts.append(mm(ds, kbuf[b, :, cs]))
+        state.append(jnp.concatenate(parts, 0))
+
+    def grads(tile, state, masked):
+        ks = pl.ds(pl.multiple_of(tile * TK, TK), TK)
+        if masked:
+            allowed = reach_mask(first, tile, limit)
+        new = []
+        for h in range(pair):
+            cs = pl.ds(h * HD, HD)
+            lse2, delta = aux[h]
+            s = mm(q_ref[:, cs], k_ref[ks, cs], NT)
+            p = jnp.exp2(s * EXP_SCALE - lse2)
+            if masked:
+                p = jnp.where(allowed, p, 0.0)
+            dp = mm(do_ref[:, cs], v_ref[ks, cs], NT)
+            ds = (p * (dp - delta)).astype(BF16)
+            dvs[ks, cs] += mm(p.astype(BF16), do_ref[:, cs], TN)
+            dks[ks, cs] += mm(ds, q_ref[:, cs], TN)
+            new.append(state[h] + mm(ds, k_ref[ks, cs]))
+        return tuple(new)
+
+    state = lax.fori_loop(0, step, lambda tile, s: grads(tile, s, False), tuple(state))
+    state = lax.fori_loop(step, tiles, lambda tile, s: grads(tile, s, True), state)
+    for h in range(pair):
+        dq_ref[:, pl.ds(h * HD, HD)] = (state[h] * SCALE).astype(BF16)
+
+    @pl.when(step == L // TQ - 1)
+    def _():
+        dk_ref[...] = (dks[...] * SCALE).astype(BF16)
+        dv_ref[...] = dvs[...].astype(BF16)
+
+
+def attention_specs(heads, pair):
+    wide = pair * HD
+    per = heads // 2 // pair
+    groups = heads // pair
+    return [
+        pl.BlockSpec((TQ, wide), lambda h, i, meta: (i, h)),
+        pl.BlockSpec((L, wide), lambda h, i, meta: (0, groups + h)),
+        pl.BlockSpec((L, wide), lambda h, i, meta: (0, 2 * groups + h)),
+        pl.BlockSpec((1, CACHE_LEN, wide), lambda h, i, meta: ((h // per) ^ meta[1], 0, h % per)),
+        pl.BlockSpec((1, CACHE_LEN, wide), lambda h, i, meta: ((h // per) ^ meta[1], 0, h % per)),
+        pl.BlockSpec(
+            (CACHE_LEN // CBLOCK, 1, 1, CBLOCK, wide),
+            lambda h, i, meta: (0, (h // per) ^ meta[1], 0, 0, h % per),
+        ),
+        pl.BlockSpec(
+            (CACHE_LEN // CBLOCK, 1, 1, CBLOCK, wide),
+            lambda h, i, meta: (0, (h // per) ^ meta[1], 1, 0, h % per),
+        ),
+    ]
+
+
+def attend(meta, qkv, own_k, own_v, fetched, pair=2):
+    width = qkv.shape[1] // 3
+    heads = width // HD
+    wide = pair * HD
+    row = pl.BlockSpec((TQ, wide), lambda h, i, meta: (i, h))
+    area = L * 1900 * width
+    return pl.pallas_call(
+        functools.partial(attend_kernel, pair=pair),
+        grid_spec=pltpu.PrefetchScalarGridSpec(
+            num_scalar_prefetch=1,
+            grid=(heads // pair, L // TQ),
+            in_specs=attention_specs(heads, pair),
+            out_specs=[row, row],
+            scratch_shapes=[pltpu.VMEM((TQ // QBLOCK, 2 * KR * CBLOCK, wide), BF16)] * 2
+            + [pltpu.VMEM((pair, L // TK, TQ, TK), F32), pltpu.VMEM((pair, TQ, 2 * KR * CBLOCK), F32)],
+        ),
+        out_shape=[jax.ShapeDtypeStruct((L, width), BF16), jax.ShapeDtypeStruct((L, width), F32)],
+        compiler_params=pltpu.CompilerParams(vmem_limit_bytes=40 * MIB),
+        cost_estimate=pl.CostEstimate(flops=8 * area, bytes_accessed=30 * MIB, transcendentals=area // HD),
+        name="attend",
+    )(meta, qkv, qkv, qkv, own_k, own_v, fetched, fetched)
+
+
+def attend_back(meta, qkv, own_k, own_v, fetched, grad_context, context, lse, pair=2):
+    width = context.shape[1]
+    heads = width // HD
+    wide = pair * HD
+    row = pl.BlockSpec((TQ, wide), lambda h, i, meta: (i, h))
+    col = pl.BlockSpec((L, wide), lambda h, i, meta: (0, h))
+    area = L * 1900 * width
+    return pl.pallas_call(
+        functools.partial(attend_back_kernel, pair=pair),
+        grid_spec=pltpu.PrefetchScalarGridSpec(
+            num_scalar_prefetch=1,
+            grid=(heads // pair, L // TQ),
+            in_specs=attention_specs(heads, pair) + [row, row, row],
+            out_specs=[row, col, col],
+            scratch_shapes=[pltpu.VMEM((TQ // QBLOCK, 2 * KR * CBLOCK, wide), BF16)] * 2
+            + [pltpu.VMEM((L, wide), F32)] * 2,
+        ),
+        out_shape=[jax.ShapeDtypeStruct((L, width), BF16)] * 3,
+        compiler_params=pltpu.CompilerParams(vmem_limit_bytes=48 * MIB),
+        cost_estimate=pl.CostEstimate(flops=12 * area, bytes_accessed=40 * MIB, transcendentals=area // HD),
+        name="attend_back",
+    )(meta, qkv, qkv, qkv, own_k, own_v, fetched, fetched, grad_context, context, lse)
+
+
+def project_kernel(x_ref, gain_ref, w_ref, normed_ref, qkv_ref):
+    rows = x_ref[...].astype(F32)
+    scale = lax.rsqrt(jnp.mean(rows * rows, axis=1, keepdims=True) + EPS)
+    normed_ref[...] = (rows * scale * gain_ref[...]).astype(BF16)
+    left = normed_ref[...]
+
+    def chunk(c, carry):
+        cs = pl.ds(pl.multiple_of(c * 512, 512), 512)
+        qkv_ref[:, cs] = mm(left, w_ref[:, cs]).astype(BF16)
+        return carry
+
+    lax.fori_loop(0, qkv_ref.shape[1] // 512, chunk, 0)
+
+
+def project(x, gain, weights):
+    width = x.shape[1]
+    cols = 3 * width
+    row = lambda n: pl.BlockSpec((ROWS, n), lambda i: (i, 0))
+    whole = lambda n: pl.BlockSpec((width, n), lambda i: (0, 0))
+    return pl.pallas_call(
+        project_kernel,
+        grid=(L // ROWS,),
+        in_specs=[row(width), pl.BlockSpec((1, width), lambda i: (0, 0)), whole(cols)],
+        out_specs=[row(width), row(cols)],
+        out_shape=[jax.ShapeDtypeStruct((L, width), BF16), jax.ShapeDtypeStruct((L, cols), BF16)],
+        compiler_params=pltpu.CompilerParams(vmem_limit_bytes=40 * MIB),
+        cost_estimate=pl.CostEstimate(flops=2 * L * width * cols, bytes_accessed=26 * MIB, transcendentals=0),
+        name="project",
+    )(x, gain, weights)
+
+
+def mix_kernel(x_ref, ctx_ref, gain_ref, w_ref, mixed_ref, normed_ref):
+    mixed = x_ref[...].astype(F32) + mm(ctx_ref[...], w_ref[...], NT)
+    mixed_ref[...] = mixed
+    scale = lax.rsqrt(jnp.mean(mixed * mixed, axis=1, keepdims=True) + EPS)
+    normed_ref[...] = (mixed * scale * gain_ref[...]).astype(BF16)
+
+
+def mix(x, context, gain, weights):
+    width = x.shape[1]
+    row = pl.BlockSpec((ROWS, width), lambda i: (i, 0))
+    return pl.pallas_call(
+        mix_kernel,
+        grid=(L // ROWS,),
+        in_specs=[row, row, pl.BlockSpec((1, width), lambda i: (0, 0)), pl.BlockSpec((width, width), lambda i: (0, 0))],
+        out_specs=[row, row],
+        out_shape=[jax.ShapeDtypeStruct((L, width), F32), jax.ShapeDtypeStruct((L, width), BF16)],
+        compiler_params=pltpu.CompilerParams(vmem_limit_bytes=32 * MIB),
+        cost_estimate=pl.CostEstimate(flops=2 * L * width * width, bytes_accessed=22 * MIB, transcendentals=0),
+        name="mix",
+    )(x, context, gain, weights)
+
+
+def ffn_kernel(n_ref, g_ref, wg_ref, wu_ref, wd_ref, out_ref, gn_ref, dg_ref, du_ref, dd_ref, acc, ag, au, ad):
+    tile = pl.program_id(0)
+    last = pl.num_programs(0) - 1
+
+    @pl.when(tile == 0)
+    def _():
+        acc[...] = jnp.zeros_like(acc)
+        gn_ref[...] = jnp.zeros_like(gn_ref)
+
+    ag[...] = jnp.zeros_like(ag)
+    au[...] = jnp.zeros_like(au)
+    ad[...] = jnp.zeros_like(ad)
+
+    def chunk(r, carry):
+        rs = pl.ds(pl.multiple_of(r * ROWS, ROWS), ROWS)
+        rows = n_ref[rs, :]
+        cotangent = g_ref[rs, :]
+        gate = mm(rows, wg_ref[...])
+        up = mm(rows, wu_ref[...])
+        grad_hidden = mm(cotangent, wd_ref[...])
+        sigma = 1.0 / (1.0 + jnp.exp(-gate))
+        silu = gate * sigma
+        hidden = (silu * up).astype(BF16)
+        grad_gate = (grad_hidden * up * (sigma * (1.0 + gate * (1.0 - sigma)))).astype(BF16)
+        grad_up = (grad_hidden * silu).astype(BF16)
+        acc[rs, :] += mm(hidden, wd_ref[...], NT)
+        gn_ref[rs, :] += mm(grad_gate, wg_ref[...], NT) + mm(grad_up, wu_ref[...], NT)
+        ag[...] += mm(rows, grad_gate, TN)
+        au[...] += mm(rows, grad_up, TN)
+        ad[...] += mm(cotangent, hidden, TN)
+        return carry
+
+    lax.fori_loop(0, L // ROWS, chunk, 0)
+    dg_ref[...] = ag[...].astype(BF16)
+    du_ref[...] = au[...].astype(BF16)
+    dd_ref[...] = ad[...].astype(BF16)
+
+    @pl.when(tile == last)
+    def _():
+        out_ref[...] = acc[...].astype(BF16)
+
+
+def ffn(normed, cotangent, weights, width, hidden):
+    once = pl.Buffered(1)
+    tiles = hidden // HT
+    lead = width // HT
+    part = lambda k: pl.BlockSpec((width, HT), lambda j: (0, lead + k * tiles + j))
+    whole = pl.BlockSpec((L, width), lambda j: (0, 0), pipeline_mode=once)
+    grad = pl.BlockSpec((width, HT), lambda j: (0, j))
+    return pl.pallas_call(
+        ffn_kernel,
+        grid=(tiles,),
+        in_specs=[whole, whole, part(0), part(1), part(2)],
+        out_specs=[whole, whole, grad, grad, grad],
+        out_shape=[jax.ShapeDtypeStruct((L, width), BF16), jax.ShapeDtypeStruct((L, width), F32)]
+        + [jax.ShapeDtypeStruct((width, hidden), BF16)] * 3,
+        scratch_shapes=[pltpu.VMEM((L, width), F32)] + [pltpu.VMEM((width, HT), F32)] * 3,
+        compiler_params=pltpu.CompilerParams(vmem_limit_bytes=56 * MIB),
+        cost_estimate=pl.CostEstimate(
+            flops=18 * L * width * hidden, bytes_accessed=60 * MIB, transcendentals=L * hidden
+        ),
+        name="ffn",
+    )(normed, cotangent, weights, weights, weights)
+
+
+def unmix_kernel(mixed_ref, gn_ref, ffn_ref, g_ref, gain_ref, w_ref, out_ref, gm_ref, br_ref, gc_ref, gg_ref):
+    mixed = mixed_ref[...]
+    grad = gn_ref[...]
+    scale = lax.rsqrt(jnp.mean(mixed * mixed, axis=1, keepdims=True) + EPS)
+    unit = mixed * scale
+    inner = grad * gain_ref[...]
+    grad_mixed = g_ref[...].astype(F32) + scale * (inner - unit * jnp.mean(inner * unit, axis=1, keepdims=True))
+    out_ref[...] = (mixed + ffn_ref[...].astype(F32)).astype(BF16)
+    gm_ref[...] = grad_mixed
+    branch = grad_mixed.astype(BF16)
+    br_ref[...] = branch
+    gc_ref[...] = mm(branch, w_ref[...]).astype(BF16)
+
+    @pl.when(pl.program_id(0) == 0)
+    def _():
+        gg_ref[...] = jnp.zeros_like(gg_ref)
+
+    gg_ref[...] += jnp.sum(grad * unit, axis=0, keepdims=True)
+
+
+def unmix(mixed, grad_normed, ffn_out, cotangent, gain, weights):
+    width = mixed.shape[1]
+    rows = ROWS // 2
+    row = pl.BlockSpec((rows, width), lambda i: (i, 0))
+    one = pl.BlockSpec((1, width), lambda i: (0, 0))
+    return pl.pallas_call(
+        unmix_kernel,
+        grid=(L // rows,),
+        in_specs=[row, row, row, row, one, pl.BlockSpec((width, width), lambda i: (0, 0))],
+        out_specs=[row, row, row, row, one],
+        out_shape=[
+            jax.ShapeDtypeStruct((L, width), BF16),
+            jax.ShapeDtypeStruct((L, width), F32),
+            jax.ShapeDtypeStruct((L, width), BF16),
+            jax.ShapeDtypeStruct((L, width), BF16),
+            jax.ShapeDtypeStruct((1, width), F32),
+        ],
+        compiler_params=pltpu.CompilerParams(vmem_limit_bytes=40 * MIB),
+        cost_estimate=pl.CostEstimate(flops=2 * L * width * width, bytes_accessed=46 * MIB, transcendentals=0),
+        name="unmix",
+    )(mixed, grad_normed, ffn_out, cotangent, gain, weights)
+
+
+def finish_kernel(x_ref, gm_ref, dq_ref, dk_ref, dv_ref, gain_ref, w_ref, gt_ref, gg_ref):
+    width = x_ref.shape[1]
+    grad = mm(dq_ref[...], w_ref[:, :width], NT)
+    grad += mm(dk_ref[...], w_ref[:, width : 2 * width], NT)
+    grad += mm(dv_ref[...], w_ref[:, 2 * width : 3 * width], NT)
+    rows = x_ref[...].astype(F32)
+    scale = lax.rsqrt(jnp.mean(rows * rows, axis=1, keepdims=True) + EPS)
+    unit = rows * scale
+    inner = grad * gain_ref[...]
+    back = scale * (inner - unit * jnp.mean(inner * unit, axis=1, keepdims=True))
+    gt_ref[...] = (gm_ref[...] + back).astype(BF16)
+
+    @pl.when(pl.program_id(0) == 0)
+    def _():
+        gg_ref[...] = jnp.zeros_like(gg_ref)
+
+    gg_ref[...] += jnp.sum(grad * unit, axis=0, keepdims=True)
+
+
+def finish(x, grad_mixed, dq, dk, dv, gain, weights):
+    width = x.shape[1]
+    row = pl.BlockSpec((ROWS, width), lambda i: (i, 0))
+    one = pl.BlockSpec((1, width), lambda i: (0, 0))
+    return pl.pallas_call(
+        finish_kernel,
+        grid=(L // ROWS,),
+        in_specs=[row, row, row, row, row, one, pl.BlockSpec((width, 3 * width), lambda i: (0, 0))],
+        out_specs=[row, one],
+        out_shape=[jax.ShapeDtypeStruct((L, width), BF16), jax.ShapeDtypeStruct((1, width), F32)],
+        compiler_params=pltpu.CompilerParams(vmem_limit_bytes=48 * MIB),
+        cost_estimate=pl.CostEstimate(flops=6 * L * width * width, bytes_accessed=40 * MIB, transcendentals=0),
+        name="finish",
+    )(x, grad_mixed, dq, dk, dv, gain, weights)
+
+
+def pick_kernel(table, held_ref, sent_ref, sems):
+    def copy(i):
+        return pltpu.make_async_copy(held_ref.at[table[i]], sent_ref.at[i], sems.at[i])
+
+    for i in range(sent_ref.shape[0]):
+        copy(i).start()
+    for i in range(sent_ref.shape[0]):
+        copy(i).wait()
+
+
+def pick_rows(table, held):
+    count = held.shape[0]
+    return pl.pallas_call(
+        pick_kernel,
+        grid_spec=pltpu.PrefetchScalarGridSpec(
+            num_scalar_prefetch=1,
+            grid=(),
+            in_specs=[pl.BlockSpec(memory_space=pl.ANY)],
+            out_specs=pl.BlockSpec(memory_space=pl.ANY),
+            scratch_shapes=[pltpu.SemaphoreType.DMA((count,))],
+        ),
+        out_shape=jax.ShapeDtypeStruct(held.shape, held.dtype),
+        cost_estimate=pl.CostEstimate(flops=0, bytes_accessed=2 * held.size * 2, transcendentals=0),
+        name="pick_rows",
+    )(table, held)
+
+
+def swap(values):
+    return lax.ppermute(values, "tensor", [(0, 1), (1, 0)])
+
+
+def sequence_body(
+    tokens, gain_attn, w_query, w_key, w_value, w_out, gain_ffn, w_gate, w_up, w_down,
+    cache_keys, cache_values, prefix, partner, own_blocks, partner_blocks, grad_out,
+):
+    micro, shard_len, width = tokens.shape
+    devices = lax.axis_size("dp")
+    seqs = micro * devices
+    rows_held, cols = w_query.shape
+    hidden_held = w_gate.shape[1]
+    hidden = 2 * hidden_held
+    spot = lax.axis_index("tensor")
+    exchange = functools.partial(lax.all_to_all, axis_name="tensor", split_axis=0, concat_axis=0, tiled=True)
+    chunks = CACHE_LEN // CBLOCK
+
+    small = jnp.concatenate([w_query, w_key, w_value], axis=1)
+    small_other = swap(small)
+    partner_column = jnp.zeros((rows_held, 1), BF16).at[:micro, 0].set(partner.astype(BF16))
+    extra = jnp.concatenate(
+        [gain_attn[:, None], gain_ffn[:, None], partner_column, jnp.zeros((rows_held, HD - 3), BF16)], axis=1
+    )
+    first_rows = jnp.concatenate(
+        [
+            w_query, small_other[:, :cols], w_key, small_other[:, cols : 2 * cols],
+            w_value, small_other[:, 2 * cols :], extra,
+        ],
+        axis=1,
+    )
+    first_all = lax.all_gather(first_rows, "dp", axis=0, tiled=True)
+    x = exchange(tokens).reshape(L, width)
+    cotangent = exchange(grad_out).reshape(L, width)
+    own_k = exchange(cache_keys)
+    own_v = exchange(cache_values)
+
+    spread = jnp.stack(
+        [cache_keys.reshape(micro, chunks, CBLOCK, cols), cache_values.reshape(micro, chunks, CBLOCK, cols)], axis=2
+    ).swapaxes(0, 1)
+    per = chunks // devices
+    held = lax.all_to_all(
+        spread.reshape(chunks, micro * 2 * CBLOCK, cols), "dp", split_axis=0, concat_axis=0, tiled=True
+    )
+
+    big = jnp.concatenate([w_out.T, w_gate, w_up, w_down.T], axis=1)
+    big_other = swap(big)
+    a, b, c = cols, cols + hidden_held, cols + 2 * hidden_held
+    second_rows = jnp.concatenate(
+        [
+            big[:, :a], big_other[:, :a], big[:, a:b], big_other[:, a:b],
+            big[:, b:c], big_other[:, b:c], big[:, c:], big_other[:, c:],
+        ],
+        axis=1,
+    )
+    second_all = lax.all_gather(second_rows, "dp", axis=0, tiled=True)
+
+    tail = first_all[:, 3 * width :]
+    gains = tail[:, :2].astype(F32).T
+    gain_one, gain_two = gains[:1], gains[1:]
+    table = tail[:, 2].reshape(devices, rows_held)[:, :micro].reshape(seqs).astype(jnp.int32)
+    sent = pick_rows(table, held.reshape(seqs, 2 * CBLOCK, cols))
+    fetched = lax.all_to_all(sent, ("dp", "tensor"), split_axis=0, concat_axis=0, tiled=True)
+    fetched = fetched.reshape(chunks, 2, 2, CBLOCK, cols)
+
+    meta = jnp.concatenate(
+        [
+            prefix[spot][None], spot[None].astype(jnp.int32),
+            own_blocks[spot].reshape(-1), partner_blocks[spot].reshape(-1),
+        ]
+    )
+    normed, qkv = project(x, gain_one, first_all)
+    context, lse = attend(meta, qkv, own_k, own_v, fetched)
+    mixed, normed_two = mix(x, context, gain_two, second_all)
+    ffn_out, grad_normed_two, d_gate, d_up, d_down = ffn(normed_two, cotangent, second_all, width, hidden)
+    share = functools.partial(lax.psum_scatter, axis_name="dp", scatter_dimension=0, tiled=True)
+    ffn_share = share(jnp.concatenate([d_gate, d_up, d_down], axis=1))
+    out, grad_mixed, branch, grad_context, gain_part_two = unmix(
+        mixed, grad_normed_two, ffn_out, cotangent, gain_two, second_all
+    )
+    out = exchange(out.reshape(2, shard_len, width))
+    d_out = inner_rows(branch, context).astype(BF16)
+    dq, dk, dv = attend_back(meta, qkv, own_k, own_v, fetched, grad_context, context, lse)
+    d_qkv = [inner_rows(normed, d).astype(BF16) for d in (dq, dk, dv)]
+    attn_share = share(jnp.concatenate([d_out] + d_qkv, axis=1))
+    grad_tokens, gain_part_one = finish(x, grad_mixed, dq, dk, dv, gain_one, first_all)
+    grad_tokens = exchange(grad_tokens.reshape(2, shard_len, width)).astype(F32)
+
+    def halves(values, widths):
+        mine, theirs, start = [], [], 0
+        for w in widths:
+            mine.append(values[:, start : start + w])
+            theirs.append(values[:, start + w : start + 2 * w])
+            start += 2 * w
+        got = swap(jnp.concatenate(theirs, axis=1))
+        total = jnp.concatenate(mine, axis=1).astype(F32) + got.astype(F32)
+        return jnp.split(total, [sum(widths[: i + 1]) for i in range(len(widths) - 1)], axis=1)
+
+    g_gate, g_up, g_down = halves(ffn_share, [hidden_held] * 3)
+    g_out, g_query, g_key, g_value = halves(attn_share, [cols] * 4)
+    gain_sums = lax.psum(jnp.concatenate([gain_part_one, gain_part_two], axis=0), ("dp", "tensor"))
+    return (
+        out, grad_tokens, gain_sums[0], g_query, g_key, g_value, g_out.T, gain_sums[1], g_gate, g_up, g_down.T,
+    )
+
+
 def solution(mesh):
     in_specs = (
         P("dp", "tensor", None),
@@ -415,4 +993,6 @@
         P("dp", "tensor"),
         P("tensor", "dp"),
     )
+    whole = mesh.shape["tensor"] == 2 and mesh.shape["dp"] == CACHE_LEN // CBLOCK
+    body = sequence_body if whole else tensor_body
     return jax.shard_map(body, mesh=mesh, in_specs=in_specs, out_specs=out_specs, check_vma=False)

time: 2630 us -> 1210 us (0.46)
  waiting for transfers between devices: 1200 us -> 210 us
  matrix products: 783 us -> 22 us
  Pallas kernels: 0 us -> 526 us
  other arithmetic: 280 us -> 32.2 us
  blocking collectives: 75.7 us -> 318 us
  local copies, waits for them, and re-layouts: 256 us -> 48.1 us
  starting transfers between devices: 2.68 us -> 36.4 us
    dot_general x110 -> x0, matrix products: 692 us -> none  [the longest x14 114 us: outer_cols(): lax.dot_general(left, right, (((1,), (1,)), ((), ())), preferred_element_...]
    all_gather x17 -> x2, waiting for transfers between devices: 646 us -> 0.02 us  [the longest x1 0.02 us: sequence_body(): first_all = lax.all_gather(first_rows, 'dp', axis=0, tiled=True)]
    pallas_call x0 -> x8, Pallas kernels: none -> 526 us  [the longest x1 135 us: ffn(): pl.pallas_call(ffn_kernel, grid=(tiles,), in_specs=[whole, whole, part(0)...]
    reduce_scatter x15 -> x1, waiting for transfers between devices: 551 us -> 103 us  [sequence_body(): ffn_share = share(jnp.concatenate([d_gate, d_up, d_down], axis=1))]
    all_to_all x0 -> x3, blocking collectives: none -> 211 us  [the longest x1 143 us: sequence_body(): lax.all_to_all(spread.reshape(chunks, micro * 2 * CBLOCK, cols), 'dp', sp...]
    reduce_sum x21 -> x0, other arithmetic: 103 us -> none  [the longest x16 75.5 us: attention_forward(): total = jnp.sum(e_local, axis=-1) + jnp.sum(e_remote, axis=-1)]
    slice x34 -> x8, local copies, waits for them, and re-layouts: 92.2 us -> 5.01 us  [the longest x2 2.62 us: halves(): mine.append(values[:, start:start + w])]
    all_to_all x0 -> x5, waiting for transfers between devices: none -> 82.5 us  [the longest x1 64.8 us: sequence_body(): lax.all_to_all(sent, ('dp', 'tensor'), split_axis=0, concat_axis=0, tiled...]
  transfers between devices with their start and end apart: 32 -> 13, of which waited for: 23 -> 6; matrix products, arithmetic and copies ran while one was open for 44% -> 4% of each run, Pallas kernels for 0% -> 22%
where the time goes in v1:
time: 1210 us
  Pallas kernels  526 us (43%)
  blocking collectives  318 us (26%)
  waiting for transfers between devices  210 us (17%)
  local copies, waits for them, and re-layouts  48.1 us (4%)
  starting transfers between devices  36.4 us (3%)
  other arithmetic  32.2 us (3%)
  matrix products  22 us (2%)
  between operations  14.5 us (1%)
    all_to_all x1, blocking collectives, sequence_body(): lax.all_to_all(spread.reshape(chunks, micro * 2 * CBLOCK, cols), 'dp', sp...  143 us
    pallas_call x1, Pallas kernels, ffn(): pl.pallas_call(ffn_kernel, grid=(tiles,), in_specs=[whole, whole, part(0)...  135 us
    pallas_call x1, Pallas kernels, pick_rows(): pl.pallas_call(pick_kernel, grid_spec=pltpu.PrefetchScalarGridSpec(num_sc...  129 us
    pallas_call x1, Pallas kernels, attend_back(): pl.pallas_call(functools.partial(attend_back_kernel, pair=pair), grid_spe...  112 us
    psum x1, blocking collectives, sequence_body(): lax.psum(jnp.concatenate([gain_part_one, gain_part_two], axis=0), ('dp',...  107 us
    reduce_scatter x1, waiting for transfers between devices, sequence_body(): ffn_share = share(jnp.concatenate([d_gate, d_up, d_down], axis=1))  103 us
    pallas_call x1, Pallas kernels, attend(): pl.pallas_call(functools.partial(attend_kernel, pair=pair), grid_spec=plt...  77.7 us
    all_to_all x1, waiting for transfers between devices, sequence_body(): lax.all_to_all(sent, ('dp', 'tensor'), split_axis=0, concat_axis=0, tiled...  64.8 us
  transfers between devices with their start and end apart: 13, of which 6 were waited for; matrix products, arithmetic and copies ran while one was open for 4% of the time, Pallas kernels for 22%

profile of v1, /device:TPU:0, one launch (start us, length us, event | category | flops | bytes accessed | tf_op | source)
XLA Modules:
  0.0 1206.8 jit_solution(4340803020801169657)
XLA Ops:
  8.2 3.0 collective-permute-start
  13.5 2.6 collective-permute-done
  16.2 1.8 concatenate.40
  18.0 1.1 pad_maximum_fusion.2
  19.1 1.8 collective-permute-start.1
  21.8 12.3 %collective-permute-done.1 = bf16[64,4736]{1,0:T(8,128)(2,1)S(1)} collective-permute-done((bf16[64,4736]{1,0:T(8,128)(2,1)S(1)}, bf16[64,4736]{1,0:T(8,128)(2,1)S(1)}, u32[]{:S(2)}, u32[]{:S(2)}) %collective-permute-start.1) | collective-permute-done | bytes 606240 | tf_op jit(solution)/shard_map/ppermute | solution.py:858
  36.2 27.5 %all_to_all.40.ok_ref = bf16[2,1024,512]{2,1,0:T(8,128)(2,1)S(1)} all-to-all(bf16[2,1024,512]{2,1,0:T(8,128)(2,1)} %param.29), channel_id=1, replica_groups=mesh['dp'=16,'tensor'=2] {'tensor'}, dimensions={0} | all-to-all | bytes 4194304 | tf_op jit(solution)/shard_map/all_to_all | solution.py:891
  63.7 4.9 all-to-all-start.2
  68.6 2.7 maximum_bitcast_fusion
  71.3 2.5 copy.62
  73.8 17.7 %all-to-all-done.2.ov_ref = bf16[2,1024,512]{2,1,0:T(8,128)(2,1)} async-done(((bf16[2,1024,512]{2,1,0:T(8,128)(2,1)}), bf16[2,1024,512]{2,1,0:T(8,128)(2,1)}, u32[]{:S(2)}, u32[]{:S(2)}) %all-to-all-start.2) | async-done | bytes 2097184 | tf_op jit(solution)/shard_map/all_to_all | solution.py:892
  91.6 142.9 %all_to_all.41 = bf16[16,256,512]{2,1,0:T(8,128)(2,1)} all-to-all(bf16[16,256,512]{2,1,0:T(8,128)(2,1)} %bitcast.40), channel_id=1, replica_groups=mesh['dp'=16,'tensor'=2] {'dp'}, dimensions={0} | all-to-all | bytes 8388608 | tf_op jit(solution)/shard_map/all_to_all | solution.py:898
  234.5 5.6 all-to-all-start
  240.1 1.2 slice_reduce_fusion
  242.0 129.1 %pick_rows.1 = bf16[32,128,512]{2,1,0:T(8,128)(2,1)} custom-call(s32[32]{0:T(128)} %reshape.84.table, bf16[32,128,512]{2,1,0:T(8,128)(2,1)} %bitcast.39), custom_call_target="tpu_custom_call" | custom-call | bytes 8388608 | tf_op jit(solution)/shard_map/pick_rows/pallas_call | solution.py:842
  371.2 5.5 all-to-all-start.4
  380.0 23.6 %project.1 = (bf16[2048,1024]{1,0:T(8,128)(2,1)S(1)}, bf16[2048,3072]{1,0:T(8,128)(2,1)}) custom-call(bf16[2048,1024]{1,0:T(8,128)(2,1)} %bitcast.x_ref, f32[1,1024]{1,0:T(1,128)S(1)} %copy.61.gain_ref, bf16[1024,3200]{1,0:T(8,128)(2,1)} %all-gather.3.cloned.1.call-done.w_ref), custom_call_target="tpu_custom_call" | custom-call | flops 12884901888 | bytes 27262976 | tf_op jit(solution)/shard_map/project/pallas_call | solution.py:653
  403.6 2.1 copy-done.7
  405.6 64.8 %all-to-all-done.4 = bf16[32,128,512]{2,1,0:T(8,128)(2,1)} async-done(((bf16[32,128,512]{2,1,0:T(8,128)(2,1)}), bf16[32,128,512]{2,1,0:T(8,128)(2,1)}, u32[]{:S(2)}, u32[]{:S(2)}) %all-to-all-start.4) | async-done | bytes 4194336 | tf_op jit(solution)/shard_map/all_to_all | solution.py:919
  470.4 5.6 all-to-all-start.5
  476.6 77.7 %attend.1 = (bf16[2048,1024]{1,0:T(8,128)(2,1)S(1)}, f32[2048,1024]{1,0:T(8,128)}) custom-call(s32[130]{0:T(256)S(1)} %pad_add_fusion.meta, bf16[2048,3072]{1,0:T(8,128)(2,1)} %get-tuple-element.44.q_ref.k_ref.v_ref, bf16[2048,3072]{1,0:T(8,128)(2,1)} %get-tuple-element.44.q_ref.k_ref.v_ref, bf16[2048,3072]{1,0:T(8,128)(2,1)} %get-tuple-element.44.q_ref.k_ref.v_ref, ...), custom_call_target="tpu_custom_call" | custom-call | flops 31876710400 | bytes 31457280 | tf_op jit(solution)/shard_map/attend/pallas_call | solution.py:593
  554.3 2.0 copy-done.2
  556.3 2.2 copy-done.3
  558.5 7.9 mix.1
  566.4 3.2 copy-done
  569.7 2.0 copy-done.6
  571.6 134.6 %ffn.1 = (bf16[2048,1024]{1,0:T(8,128)(2,1)}, f32[2048,1024]{1,0:T(8,128)}, bf16[1024,2816]{1,0:T(8,128)(2,1)}, bf16[1024,2816]{1,0:T(8,128)(2,1)}, bf16[1024,2816]{1,0:T(8,128)(2,1)}) custom-call(bf16[2048,1024]{1,0:T(8,128)(2,1)} %copy-done.6, bf16[2048,1024]{1,0:T(8,128)(2,1)} %bitcast.14.g_ref, ...), custom_call_target="tpu_custom_call" | custom-call | flops 106300440576 | bytes 62914560 | tf_op jit(solution)/shard_map/ffn/pallas_call | solution.py:736
  706.2 17.6 %unmix.1 = (bf16[2048,1024]{1,0:T(8,128)(2,1)S(1)}, f32[2048,1024]{1,0:T(8,128)}, bf16[2048,1024]{1,0:T(8,128)(2,1)S(1)}, bf16[2048,1024]{1,0:T(8,128)(2,1)S(1)}, f32[1,1024]{1,0:T(1,128)S(1)}) custom-call(f32[2048,1024]{1,0:T(8,128)} %copy-done, f32[2048,1024]{1,0:T(8,128)} %get-tuple-element.48.gn_ref, bf16[2048,1024]{1,0:T(8,128)(2,1)} %get-tuple-element.49.ffn_ref, ...), custom_call_target="tpu_custom_call" | custom-call | flops 4294967296 | bytes 48234496 | tf_op jit(solution)/shard_map/unmix/pallas_call | solution.py:777
  723.8 5.0 convolution_convert_fusion.3
  728.9 112.2 %attend_back.1 = (bf16[2048,1024]{1,0:T(8,128)(2,1)}, bf16[2048,1024]{1,0:T(8,128)(2,1)}, bf16[2048,1024]{1,0:T(8,128)(2,1)}) custom-call(s32[130]{0:T(256)S(1)} %pad_add_fusion.meta, bf16[2048,3072]{1,0:T(8,128)(2,1)} %get-tuple-element.44.q_ref.k_ref.v_ref, bf16[2048,3072]{1,0:T(8,128)(2,1)} %get-tuple-element.44.q_ref.k_ref.v_ref, ...), custom_call_target="tpu_custom_call" | custom-call | flops 47815065600 | bytes 41943040 | tf_op jit(solution)/shard_map/attend_back/pallas_call | solution.py:617
  841.1 7.1 convolution_convert_fusion.2
  848.2 5.0 convolution_convert_fusion.1
  853.3 4.8 convolution_convert_fusion
  858.1 3.9 pad_maximum_fusion.1
  862.0 11.3 copy.70
  873.4 13.8 %pad_maximum_fusion = bf16[1024,8448]{1,0:T(8,128)(2,1)} fusion(bf16[1024,2816]{1,0:T(8,128)(2,1)} %get-tuple-element.64, bf16[1024,2816]{1,0:T(8,128)(2,1)} %get-tuple-element.63, bf16[1024,2816]{1,0:T(8,128)(2,1)} %get-tuple-element.62), kind=kLoop, calls=%fused_computation | loop fusion | flops 51904512 | bytes 34603008 | tf_op jit(solution)/shard_map/concatenate | solution.py:933
  887.2 23.1 %finish.1 = (bf16[2048,1024]{1,0:T(8,128)(2,1)S(1)}, f32[1,1024]{1,0:T(1,128)S(1)}) custom-call(bf16[2048,1024]{1,0:T(8,128)(2,1)} %bitcast.x_ref, f32[2048,1024]{1,0:T(8,128)} %get-tuple-element.51.gm_ref, bf16[2048,1024]{1,0:T(8,128)(2,1)} %get-tuple-element.54.dq_ref, bf16[2048,1024]{1,0:T(8,128)(2,1)} %get-tuple-element.55.dk_ref, ...), custom_call_target="tpu_custom_call" | custom-call | flops 12884901888 | bytes 41943040 | tf_op jit(solution)/shard_map/finish/pallas_call | solution.py:818
  910.3 40.9 %all_to_all.42 = bf16[2,1024,1024]{2,1,0:T(8,128)(2,1)} all-to-all(bf16[2,1024,1024]{2,1,0:T(8,128)(2,1)S(1)} %bitcast.38), channel_id=1, replica_groups=mesh['dp'=16,'tensor'=2] {'tensor'}, dimensions={0} | all-to-all | bytes 8388608 | tf_op jit(solution)/shard_map/all_to_all | solution.py:943
  951.1 5.6 all-to-all-start.6
  956.8 107.0 %psum.7 = f32[2,1024]{1,0:T(2,128)S(1)} all-reduce(f32[2,1024]{1,0:T(2,128)S(1)} %pad_maximum_fusion.6), channel_id=1, replica_groups=mesh['dp'=16,'tensor'=2] {'dp','tensor'}, use_global_device_ids=true, to_apply=%region_0.0 | all-reduce | flops 2048 | bytes 16384 | tf_op jit(solution)/shard_map/psum | solution.py:957
  1064.4 6.8 convert_element_type.39
  1071.2 1.2 fusion.1
  1073.1 2.2 collective-permute-start.2
  1075.8 102.8 %reduce-scatter.5.cloned.1.call-done = bf16[64,8448]{1,0:T(8,128)(2,1)} async-done(((bf16[1024,8448]{1,0:T(8,128)(2,1)}), bf16[64,8448]{1,0:T(8,128)(2,1)}) %reduce-scatter.5.cloned.1.call-update) | async-done | bytes 1081360 | tf_op jit(solution)/shard_map/reduce_scatter | solution.py:933
  1178.6 1.4 fusion
  1180.1 1.5 collective-permute-start.3
  1184.9 9.3 collective-permute-done.3
  1195.3 4.6 copy.88
  (94 shorter events, 17.1 us)
Async XLA Ops:
  7.2 27.9 %copy-start.11 = (bf16[1408,64]{0,1:T(8,128)(2,1)S(1)}, bf16[1408,64]{0,1:T(8,128)(2,1)}, u32[]{:S(2)}) copy-start(bf16[1408,64]{0,1:T(8,128)(2,1)} %param.28) | copy-start | bytes 540676
  7.2 27.9 %copy-start.10 = (bf16[64,1408]{1,0:T(8,128)(2,1)S(1)}, bf16[64,1408]{1,0:T(8,128)(2,1)}, u32[]{:S(2)}) copy-start(bf16[64,1408]{1,0:T(8,128)(2,1)} %param.27) | copy-start | bytes 540676
  7.2 232.9 %all-gather.3.cloned.1.call-start = ((), (), s32[]{:S(2)}) async-start(), calls=%async_computation.10 | async-start | bytes 6963200 | tf_op jit(solution)/shard_map/all_gather | solution.py:888
  8.2 7.9 collective-permute-start
  17.9 538.3 %all-gather.5.cloned.1.call-start = ((), (), s32[]{:S(2)}) async-start(), calls=%async_computation.11 | async-start | bytes 20611072 | tf_op jit(solution)/shard_map/all_gather | solution.py:912
  19.1 14.9 %collective-permute-start.1 = (bf16[64,4736]{1,0:T(8,128)(2,1)S(1)}, bf16[64,4736]{1,0:T(8,128)(2,1)S(1)}, u32[]{:S(2)}, u32[]{:S(2)}) collective-permute-start(bf16[64,4736]{1,0:T(8,128)(2,1)S(1)} %pad_maximum_fusion.2), channel_id=1, source_target_pairs={{0,1},{1,0},{2,3},{3,2},{4,5},{5,4},{6,7},{7,6},{8,9},{9,8},{10,11... | collective-permute-start | bytes 1818632 | tf_op jit(solution)/shard_map/ppermute | solution.py:858
  35.2 1.0 copy-start.9
  63.7 27.8 %all-to-all-start.2 = ((bf16[2,1024,512]{2,1,0:T(8,128)(2,1)}), bf16[2,1024,512]{2,1,0:T(8,128)(2,1)}, u32[]{:S(2)}, u32[]{:S(2)}) async-start(bf16[2,1024,512]{2,1,0:T(8,128)(2,1)} %param.30), calls=%async_computation.2 | async-start | bytes 4194304 | tf_op jit(solution)/shard_map/all_to_all | solution.py:892
  234.5 136.7 %all-to-all-start = ((bf16[2,1024,1024]{2,1,0:T(8,128)(2,1)}), bf16[2,1024,1024]{2,1,0:T(8,128)(2,1)}, u32[]{:S(2)}, u32[]{:S(2)}) async-start(bf16[2,1024,1024]{2,1,0:T(8,128)(2,1)} %param.19), calls=%async_computation | async-start | bytes 8388608 | tf_op jit(solution)/shard_map/all_to_all | solution.py:889
  371.1 5.5 copy-start.12
  371.1 5.5 copy-start.13
  371.1 5.9 copy-start.14
  371.2 99.2 %all-to-all-start.4 = ((bf16[32,128,512]{2,1,0:T(8,128)(2,1)}), bf16[32,128,512]{2,1,0:T(8,128)(2,1)}, u32[]{:S(2)}, u32[]{:S(2)}) async-start(bf16[32,128,512]{2,1,0:T(8,128)(2,1)} %pick_rows.1), calls=%async_computation.4 | async-start | bytes 8388608 | tf_op jit(solution)/shard_map/all_to_all | solution.py:919
  403.6 2.1 copy-start.7
  470.4 101.3 %all-to-all-start.5 = ((bf16[2,1024,1024]{2,1,0:T(8,128)(2,1)}), bf16[2,1024,1024]{2,1,0:T(8,128)(2,1)}, u32[]{:S(2)}, u32[]{:S(2)}) async-start(bf16[2,1024,1024]{2,1,0:T(8,128)(2,1)} %param.35), calls=%async_computation.5 | async-start | bytes 8388608 | tf_op jit(solution)/shard_map/all_to_all | solution.py:890
  476.0 595.2 %reduce-scatter.7.cloned.1.call-start = ((), (), s32[]{:S(2)}) async-start(), calls=%async_computation.13 | async-start | bytes 8912896
  554.3 2.0 copy-start.2
  556.3 2.2 copy-start.3
  566.4 3.3 copy-start
  569.7 2.0 copy-start.6
  706.2 17.6 %copy-start.4 = (bf16[2048,1024]{1,0:T(8,128)(2,1)S(1)}, bf16[2048,1024]{1,0:T(8,128)(2,1)}, u32[]{:S(2)}) copy-start(bf16[2048,1024]{1,0:T(8,128)(2,1)} %copy-done.2) | copy-start | bytes 12582916
  723.8 5.0 copy-start.1
  723.8 5.0 copy-start.5
  728.9 112.2 %copy-start.8 = (bf16[2048,1024]{1,0:T(8,128)(2,1)S(1)}, bf16[2048,1024]{1,0:T(8,128)(2,1)}, u32[]{:S(2)}) copy-start(bf16[2048,1024]{1,0:T(8,128)(2,1)} %copy-done.7) | copy-start | bytes 12582916
  841.0 7.2 copy-start.15
  848.2 5.0 copy-start.16
  873.3 305.3 %reduce-scatter.5.cloned.1.call-start = ((), (), s32[]{:S(2)}) async-start(), calls=%async_computation.12 | async-start | bytes 18382848 | tf_op jit(solution)/shard_map/reduce_scatter | solution.py:933
  951.1 120.1 %all-to-all-start.6 = ((bf16[2,1024,1024]{2,1,0:T(8,128)(2,1)}), bf16[2,1024,1024]{2,1,0:T(8,128)(2,1)}, u32[]{:S(2)}, u32[]{:S(2)}) async-start(bf16[2,1024,1024]{2,1,0:T(8,128)(2,1)} %bitcast.37), calls=%async_computation.6 | async-start | bytes 8388608 | tf_op jit(solution)/shard_map/all_to_all | solution.py:937
  1073.1 108.5 %collective-permute-start.2 = (bf16[64,2048]{0,1:T(8,128)(2,1)S(1)}, bf16[64,2048]{0,1:T(8,128)(2,1)S(1)}, u32[]{:S(2)}, u32[]{:S(2)}) collective-permute-start(bf16[64,2048]{0,1:T(8,128)(2,1)S(1)} %pad_maximum_fusion.4), channel_id=1, source_target_pairs={{0,1},{1,0},{2,3},{3,2},{4,5},{5,4},{6,7},{7,6},{8,9},{9,8},{10,11... | collective-permute-start | bytes 786440 | tf_op jit(solution)/shard_map/ppermute | solution.py:858
  1180.1 14.1 %collective-permute-start.3 = (bf16[64,4224]{1,0:T(8,128)(2,1)S(1)}, bf16[64,4224]{1,0:T(8,128)(2,1)S(1)}, u32[]{:S(2)}, u32[]{:S(2)}) collective-permute-start(bf16[64,4224]{1,0:T(8,128)(2,1)S(1)} %pad_maximum_fusion.3), channel_id=1, source_target_pairs={{0,1},{1,0},{2,3},{3,2},{4,5},{5,4},{6,7},{7,6},{8,9},{9,8},{10,11... | collective-permute-start | bytes 1622024 | tf_op jit(solution)/shard_map/ppermute | solution.py:858
Sparse Core Ops, SparseCore 0:
  18.1 64.8 all-gather.2
  84.6 182.7 all-gather.4
  873.5 116.4 reduce-scatter.6
  994.0 184.6 reduce-scatter.4

commit v2 on v1

--- a/solution.py
+++ b/solution.py
@@ -845,13 +845,197 @@
             num_scalar_prefetch=1,
             grid=(),
             in_specs=[pl.BlockSpec(memory_space=pl.ANY)],
-            out_specs=pl.BlockSpec(memory_space=pl.ANY),
+            out_specs=pl.BlockSpec(memory_space=pltpu.VMEM),
             scratch_shapes=[pltpu.SemaphoreType.DMA((count,))],
         ),
         out_shape=jax.ShapeDtypeStruct(held.shape, held.dtype),
+        compiler_params=pltpu.CompilerParams(vmem_limit_bytes=16 * MIB),
         cost_estimate=pl.CostEstimate(flops=0, bytes_accessed=2 * held.size * 2, transcendentals=0),
         name="pick_rows",
     )(table, held)
+
+
+RING = 8
+RIGHT = RING // 2
+LEFT = RING - 1 - RIGHT
+
+
+def spread_kernel(
+    tok_ref, ck_ref, cv_ref, small_ref, extra_ref, big_ref,
+    x_ref, ok_ref, ov_ref, held_ref, first_ref, second_ref,
+    tok_buf, k_buf, v_buf, local_sem, x_send, x_recv, all_send, all_recv, ring_send, ring_recv, pair_send, pair_recv,
+):
+    me = lax.axis_index("dp")
+    spot = lax.axis_index("tensor")
+    peer = 1 - spot
+    devices = held_ref.shape[0]
+    rows, cols = small_ref.shape[0], small_ref.shape[1] // 3
+    core = me % 2
+    z, y = me // 4, (me // 2) % 2
+    place = z + y * (7 - 2 * z)
+
+    def at_place(p):
+        yy = p // 4
+        return (p + yy * (7 - 2 * p)) * 4 + yy * 2
+
+    def target(dp, tensor):
+        return (dp, tensor)
+
+    barrier = pltpu.get_barrier_semaphore()
+    for d in range(1, devices):
+        pl.semaphore_signal(barrier, inc=1, device_id=target((me + d) % devices, spot), device_id_type=pl.DeviceIdType.MESH)
+    pl.semaphore_signal(barrier, inc=1, device_id=target(me, peer), device_id_type=pl.DeviceIdType.MESH)
+    pl.semaphore_wait(barrier, devices)
+
+    def remote(src, dst, send, recv, device):
+        return pltpu.make_async_remote_copy(
+            src_ref=src, dst_ref=dst, send_sem=send, recv_sem=recv,
+            device_id=device, device_id_type=pl.DeviceIdType.MESH,
+        )
+
+    mine = pl.multiple_of(me * rows, rows)
+    across = target(me, peer)
+    weight_copies = []
+    for i in range(3):
+        weight_copies.append(
+            remote(
+                small_ref.at[:, pl.ds(i * cols, cols)],
+                first_ref.at[pl.ds(mine, rows), pl.ds((2 * i + 1) * cols, cols)],
+                x_send.at[i], x_recv.at[i], across,
+            )
+        )
+    for copy in weight_copies:
+        copy.start()
+    for i in range(3):
+        first_ref[pl.ds(mine, rows), pl.ds(2 * i * cols, cols)] = small_ref[:, pl.ds(i * cols, cols)]
+    first_ref[pl.ds(mine, rows), pl.ds(6 * cols, HD)] = extra_ref[...]
+
+    loads = [
+        pltpu.make_async_copy(tok_ref.at[spot], tok_buf, local_sem.at[0]),
+        pltpu.make_async_copy(ck_ref.at[spot], k_buf, local_sem.at[1]),
+        pltpu.make_async_copy(cv_ref.at[spot], v_buf, local_sem.at[2]),
+    ]
+    stores = [
+        pltpu.make_async_copy(tok_buf, x_ref.at[spot], local_sem.at[3]),
+        pltpu.make_async_copy(k_buf, ok_ref.at[spot], local_sem.at[4]),
+        pltpu.make_async_copy(v_buf, ov_ref.at[spot], local_sem.at[5]),
+    ]
+    for copy in loads:
+        copy.start()
+
+    x_copies = [remote(tok_ref.at[peer], x_ref.at[spot], x_send.at[3], x_recv.at[3], across)]
+    wide = big_ref.shape[1]
+    hidden = (wide - cols) // 3
+    starts = [(0, cols)] + [(cols + i * hidden, hidden) for i in range(3)]
+    own_cols = []
+    for i, (start, size) in enumerate(starts):
+        base = 2 * start
+        own_cols.append(pltpu.make_async_copy(
+            big_ref.at[:, pl.ds(start, size)], second_ref.at[:, pl.ds(base, size)], local_sem.at[6 + i]))
+        x_copies.append(remote(
+            big_ref.at[:, pl.ds(start, size)], second_ref.at[:, pl.ds(base + size, size)],
+            x_send.at[4 + i], x_recv.at[4 + i], across))
+    x_copies.append(remote(ck_ref.at[peer], ok_ref.at[spot], x_send.at[8], x_recv.at[8], across))
+    x_copies.append(remote(cv_ref.at[peer], ov_ref.at[spot], x_send.at[9], x_recv.at[9], across))
+    for copy in x_copies + own_cols:
+        copy.start()
+
+    def to_device(d, dst_dp):
+        chunk = pl.ds(pl.multiple_of(dst_dp * CBLOCK, CBLOCK), CBLOCK)
+        dst = target(dst_dp, spot)
+        return [
+            remote(ck_ref.at[:, chunk, :], held_ref.at[me, :, 0], all_send.at[0, d], all_recv.at[0, d], dst),
+            remote(cv_ref.at[:, chunk, :], held_ref.at[me, :, 1], all_send.at[1, d], all_recv.at[1, d], dst),
+        ]
+
+    for copy in weight_copies:
+        copy.wait_recv()
+
+    def block(p, c):
+        return first_ref.at[pl.ds(pl.multiple_of((at_place(p) + c) * rows, rows), rows), :]
+
+    ahead = (place + 1) % RING
+    behind = (place + RING - 1) % RING
+
+    def hop(s, direction):
+        p = (place + RING - (s - 1)) % RING if direction == 0 else (place + s - 1) % RING
+        to = ahead if direction == 0 else behind
+        k = (s - 1) * 2 + direction
+        return remote(block(p, core), block(p, core), ring_send.at[k], ring_recv.at[k], target(at_place(to) + core, spot))
+
+    def to_pair(i, p):
+        return remote(block(p, core), block(p, core), pair_send.at[i], pair_recv.at[i], target(at_place(place) + 1 - core, spot))
+
+    hops = [hop(1, 0), hop(1, 1)]
+    for copy in hops:
+        copy.start()
+    pairs = [to_pair(0, place)]
+    pairs[0].start()
+    copies = []
+    for d in range(1, devices):
+        for copy in to_device(d, (me + d) % devices):
+            copy.start()
+            copies.append(copy)
+    chunk = pl.ds(pl.multiple_of(me * CBLOCK, CBLOCK), CBLOCK)
+    kept = [
+        pltpu.make_async_copy(ck_ref.at[:, chunk, :], held_ref.at[me, :, 0], local_sem.at[10]),
+        pltpu.make_async_copy(cv_ref.at[:, chunk, :], held_ref.at[me, :, 1], local_sem.at[11]),
+    ]
+    for copy in kept:
+        copy.start()
+    for load, store in zip(loads, stores):
+        load.wait()
+        store.start()
+    for s in range(1, RIGHT + 1):
+        for direction in range(2):
+            if direction == 1 and s > LEFT:
+                continue
+            hops[(s - 1) * 2 + direction].wait_recv()
+            p = (place + RING - s) % RING if direction == 0 else (place + s) % RING
+            if s < (RIGHT if direction == 0 else LEFT):
+                nxt = hop(s + 1, direction)
+                nxt.start()
+                hops.append(nxt)
+            pair = to_pair(len(pairs), p)
+            pair.start()
+            pairs.append(pair)
+    for copy in weight_copies + hops:
+        copy.wait_send()
+    for copy in pairs + x_copies + copies:
+        copy.wait()
+    for copy in stores + own_cols + kept:
+        copy.wait()
+
+
+def spread(tokens, cache_keys, cache_values, small, extra, big, devices):
+    micro, shard_len, width = tokens.shape
+    rows, cols = small.shape[0], small.shape[1] // 3
+    anywhere = pl.BlockSpec(memory_space=pl.ANY)
+    vmem = pl.BlockSpec(memory_space=pltpu.VMEM)
+    dma = pltpu.SemaphoreType.DMA
+    return pl.pallas_call(
+        spread_kernel,
+        in_specs=[anywhere, anywhere, anywhere, vmem, vmem, vmem],
+        out_specs=[anywhere, anywhere, anywhere, anywhere, vmem, anywhere],
+        out_shape=[
+            jax.ShapeDtypeStruct((2, shard_len, width), BF16),
+            jax.ShapeDtypeStruct((2, CACHE_LEN, cols), BF16),
+            jax.ShapeDtypeStruct((2, CACHE_LEN, cols), BF16),
+            jax.ShapeDtypeStruct((devices, micro, 2, CBLOCK, cols), BF16),
+            jax.ShapeDtypeStruct((rows * devices, 6 * cols + HD), BF16),
+            jax.ShapeDtypeStruct((rows, 2 * big.shape[1]), BF16),
+        ],
+        scratch_shapes=[
+            pltpu.VMEM((shard_len, width), BF16),
+            pltpu.VMEM((CACHE_LEN, cols), BF16),
+            pltpu.VMEM((CACHE_LEN, cols), BF16),
+            dma((12,)), dma((10,)), dma((10,)), dma((2, devices)), dma((2, devices)),
+            dma((RING - 1,)), dma((RING - 1,)), dma((RING,)), dma((RING,)),
+        ],
+        compiler_params=pltpu.CompilerParams(collective_id=0, has_side_effects=True, vmem_limit_bytes=32 * MIB),
+        cost_estimate=pl.CostEstimate(flops=0, bytes_accessed=300 * MIB, transcendentals=0),
+        name="spread",
+    )(tokens, cache_keys, cache_values, small, extra, big)
 
 
 def swap(values):
@@ -873,42 +1057,16 @@
     chunks = CACHE_LEN // CBLOCK
 
     small = jnp.concatenate([w_query, w_key, w_value], axis=1)
-    small_other = swap(small)
     partner_column = jnp.zeros((rows_held, 1), BF16).at[:micro, 0].set(partner.astype(BF16))
     extra = jnp.concatenate(
         [gain_attn[:, None], gain_ffn[:, None], partner_column, jnp.zeros((rows_held, HD - 3), BF16)], axis=1
     )
-    first_rows = jnp.concatenate(
-        [
-            w_query, small_other[:, :cols], w_key, small_other[:, cols : 2 * cols],
-            w_value, small_other[:, 2 * cols :], extra,
-        ],
-        axis=1,
-    )
-    first_all = lax.all_gather(first_rows, "dp", axis=0, tiled=True)
-    x = exchange(tokens).reshape(L, width)
+    big = jnp.concatenate([w_out.T, w_gate, w_up, w_down.T], axis=1)
+    x, own_k, own_v, held, first_all, second_rows = spread(
+        tokens, cache_keys, cache_values, small, extra, big, devices
+    )
+    x = x.reshape(L, width)
     cotangent = exchange(grad_out).reshape(L, width)
-    own_k = exchange(cache_keys)
-    own_v = exchange(cache_values)
-
-    spread = jnp.stack(
-        [cache_keys.reshape(micro, chunks, CBLOCK, cols), cache_values.reshape(micro, chunks, CBLOCK, cols)], axis=2
-    ).swapaxes(0, 1)
-    per = chunks // devices
-    held = lax.all_to_all(
-        spread.reshape(chunks, micro * 2 * CBLOCK, cols), "dp", split_axis=0, concat_axis=0, tiled=True
-    )
-
-    big = jnp.concatenate([w_out.T, w_gate, w_up, w_down.T], axis=1)
-    big_other = swap(big)
-    a, b, c = cols, cols + hidden_held, cols + 2 * hidden_held
-    second_rows = jnp.concatenate(
-        [
-            big[:, :a], big_other[:, :a], big[:, a:b], big_other[:, a:b],
-            big[:, b:c], big_other[:, b:c], big[:, c:], big_other[:, c:],
-        ],
-        axis=1,
-    )
     second_all = lax.all_gather(second_rows, "dp", axis=0, tiled=True)
 
     tail = first_all[:, 3 * width :]
@@ -938,7 +1096,10 @@
     d_out = inner_rows(branch, context).astype(BF16)
     dq, dk, dv = attend_back(meta, qkv, own_k, own_v, fetched, grad_context, context, lse)
     d_qkv = [inner_rows(normed, d).astype(BF16) for d in (dq, dk, dv)]
-    attn_share = share(jnp.concatenate([d_out] + d_qkv, axis=1))
+    attn_grads, ffn_share, out = lax.optimization_barrier(
+        (jnp.concatenate([d_out] + d_qkv, axis=1), ffn_share, out)
+    )
+    attn_share = share(attn_grads)
     grad_tokens, gain_part_one = finish(x, grad_mixed, dq, dk, dv, gain_one, first_all)
     grad_tokens = exchange(grad_tokens.reshape(2, shard_len, width)).astype(F32)
 

time: 1210 us -> 938 us (0.78)
  blocking collectives: 318 us -> 90.1 us
  waiting for transfers between devices: 210 us -> 110 us
  Pallas kernels: 526 us -> 558 us
  local copies, waits for them, and re-layouts: 48.1 us -> 78.7 us
    all_to_all x3 -> x0, blocking collectives: 211 us -> none  [the longest x1 143 us: sequence_body(): lax.all_to_all(spread.reshape(chunks, micro * 2 * CBLOCK, cols), 'dp', sp...]
    pallas_call x0 -> x1, Pallas kernels: none -> 142 us  [spread(): pl.pallas_call(spread_kernel, in_specs=[anywhere, anywhere, anywhere, vme...]
    pallas_call x1, Pallas kernels: 129 us -> 6.38 us  [pick_rows(): pl.pallas_call(pick_kernel, grid_spec=pltpu.PrefetchScalarGridSpec(num_sc...]
    reduce_scatter x1, waiting for transfers between devices: 103 us -> 2.41 us  [sequence_body(): ffn_share = share(jnp.concatenate([d_gate, d_up, d_down], axis=1))]
    all_to_all x1, waiting for transfers between devices: 64.8 us -> 98 us  [sequence_body(): lax.all_to_all(sent, ('dp', 'tensor'), split_axis=0, concat_axis=0, tiled...]
    unnamed x55 -> x78, local copies, waits for them, and re-layouts: 34.4 us -> 62.3 us
    all_to_all x2 -> x1, waiting for transfers between devices: 17.7 us -> 0.01 us  [sequence_body(): grad_tokens = exchange(grad_tokens.reshape(2, shard_len, width)).astype(F32)]
    psum x1, blocking collectives: 107 us -> 90.1 us  [sequence_body(): lax.psum(jnp.concatenate([gain_part_one, gain_part_two], axis=0), ('dp',...]
  transfers between devices with their start and end apart: 13 -> 9, of which waited for: 6 -> 3; matrix products, arithmetic and copies ran while one was open for 4% -> 6% of each run, Pallas kernels for 22% -> 30%
where the time goes in v2:
time: 938 us; the launch traced here: 932 us
  Pallas kernels  558 us (59%)
  waiting for transfers between devices  110 us (12%)
  blocking collectives  90.1 us (10%)
  local copies, waits for them, and re-layouts  78.7 us (8%)
  other arithmetic  29 us (3%)
  starting transfers between devices  26.9 us (3%)
  matrix products  25.6 us (3%)
  between operations  14.4 us (2%)
    pallas_call x1, Pallas kernels, spread(): pl.pallas_call(spread_kernel, in_specs=[anywhere, anywhere, anywhere, vme...  142 us
    pallas_call x1, Pallas kernels, ffn(): pl.pallas_call(ffn_kernel, grid=(tiles,), in_specs=[whole, whole, part(0)...  135 us
    pallas_call x1, Pallas kernels, attend_back(): pl.pallas_call(functools.partial(attend_back_kernel, pair=pair), grid_spe...  119 us
    all_to_all x1, waiting for transfers between devices, sequence_body(): lax.all_to_all(sent, ('dp', 'tensor'), split_axis=0, concat_axis=0, tiled...  98 us
    psum x1, blocking collectives, sequence_body(): lax.psum(jnp.concatenate([gain_part_one, gain_part_two], axis=0), ('dp',...  90.1 us
    pallas_call x1, Pallas kernels, attend(): pl.pallas_call(functools.partial(attend_kernel, pair=pair), grid_spec=plt...  82.2 us
    unnamed x78, local copies, waits for them, and re-layouts  62.3 us
    dot_general x4, matrix products, inner_rows(): lax.dot_general(left, right, (((0,), (0,)), ((), ())), preferred_element_...  25.6 us
  transfers between devices with their start and end apart: 9, of which 3 were waited for; matrix products, arithmetic and copies ran while one was open for 6% of the time, Pallas kernels for 30%

profile of v2, /device:TPU:0, one launch (start us, length us, event | category | flops | bytes accessed | tf_op | source)
XLA Modules:
  0.0 932.4 jit_solution(8293452062550206433)
XLA Ops:
  11.8 2.2 copy-done.2
  13.9 1.6 copy-done.12
  15.5 1.6 copy-done.13
  17.1 141.9 %spread.1 = (bf16[2,1024,1024]{2,1,0:T(8,128)(2,1)S(1)}, bf16[2,1024,512]{2,1,0:T(8,128)(2,1)S(1)}, bf16[2,1024,512]{2,1,0:T(8,128)(2,1)S(1)}, bf16[16,2,2,64,51...) custom-call(bf16[2,1024,1024]{2,1,0:T(8,128)(2,1)S(1)} %copy-done.2, ...), custom_call_target="tpu_custom_call" | custom-call | bytes 314572800 | tf_op jit(solution)/shard_map/spread/pallas_call | solution.py:1016
  159.0 2.0 copy-done.5
  161.0 2.0 copy-done.7
  165.8 2.2 copy-done.6
  168.0 6.4 pick_rows.1
  174.4 2.0 copy-done
  176.4 5.1 all-to-all-start
  181.5 9.5 %copy.53 = bf16[1024,3200]{0,1:T(8,128)(2,1)} copy(bf16[1024,3200]{1,0:T(8,128)(2,1)} %get-tuple-element.54.w_ref) | data formatting | bytes 13107200 | tf_op jit(solution)/shard_map/spread/pallas_call | solution.py:1016
  194.1 2.2 copy-done.8
  196.3 23.3 %project.1 = (bf16[2048,1024]{1,0:T(8,128)(2,1)S(1)}, bf16[2048,3072]{1,0:T(8,128)(2,1)}) custom-call(bf16[2048,1024]{1,0:T(8,128)(2,1)S(1)} %bitcast.34, f32[1,1024]{1,0:T(1,128)S(1)} %get-tuple-element.140.gain_ref, bf16[1024,3200]{1,0:T(8,128)(2,1)} %get-tuple-element.54.w_ref), custom_call_target="tpu_custom_call" | custom-call | flops 12884901888 | bytes 27262976 | tf_op jit(solution)/shard_map/project/pallas_call | solution.py:653
  219.6 2.1 copy-done.24
  221.7 98.0 %all-to-all-done = bf16[32,128,512]{2,1,0:T(8,128)(2,1)} async-done(((bf16[32,128,512]{2,1,0:T(8,128)(2,1)}), bf16[32,128,512]{2,1,0:T(8,128)(2,1)}, u32[]{:S(2)}, u32[]{:S(2)}) %all-to-all-start) | async-done | bytes 4194336 | tf_op jit(solution)/shard_map/all_to_all | solution.py:1077
  319.7 5.6 all-to-all-start.1
  325.5 1.6 copy-done.22
  327.1 82.2 %attend.1 = (bf16[2048,1024]{1,0:T(8,128)(2,1)S(1)}, f32[2048,1024]{1,0:T(8,128)}) custom-call(s32[130]{0:T(256)S(1)} %pad_add_fusion.meta, bf16[2048,3072]{1,0:T(8,128)(2,1)} %get-tuple-element.55.q_ref.k_ref.v_ref, bf16[2048,3072]{1,0:T(8,128)(2,1)} %get-tuple-element.55.q_ref.k_ref.v_ref, bf16[2048,3072]{1,0:T(8,128)(2,1)} %get-tuple-element.55.q_ref.k_ref.v_ref, ...), custom_call_target="tpu_custom_call" | custom-call | flops 31876710400 | bytes 31457280 | tf_op jit(solution)/shard_map/attend/pallas_call | solution.py:593
  409.3 2.0 copy-done.10
  411.3 2.2 copy-done.9
  413.5 2.2 copy-done.11
  415.6 7.6 mix.1
  423.2 3.2 copy-done.1
  426.4 2.0 copy-done.20
  428.4 134.6 %ffn.1 = (bf16[2048,1024]{1,0:T(8,128)(2,1)}, f32[2048,1024]{1,0:T(8,128)}, bf16[1024,2816]{1,0:T(8,128)(2,1)}, bf16[1024,2816]{1,0:T(8,128)(2,1)}, bf16[1024,2816]{1,0:T(8,128)(2,1)}) custom-call(bf16[2048,1024]{1,0:T(8,128)(2,1)} %copy-done.20, bf16[2048,1024]{1,0:T(8,128)(2,1)} %bitcast.10.g_ref, ...), custom_call_target="tpu_custom_call" | custom-call | flops 106300440576 | bytes 62914560 | tf_op jit(solution)/shard_map/ffn/pallas_call | solution.py:736
  563.0 13.8 %pad_maximum_fusion = bf16[1024,8448]{1,0:T(8,128)(2,1)} fusion(bf16[1024,2816]{1,0:T(8,128)(2,1)} %get-tuple-element.74, bf16[1024,2816]{1,0:T(8,128)(2,1)} %get-tuple-element.73, bf16[1024,2816]{1,0:T(8,128)(2,1)} %get-tuple-element.72), kind=kLoop, calls=%fused_computation | loop fusion | flops 51904512 | bytes 34603008 | tf_op jit(solution)/shard_map/concatenate | solution.py:1091
  576.9 20.1 %unmix.1 = (bf16[2048,1024]{1,0:T(8,128)(2,1)S(1)}, f32[2048,1024]{1,0:T(8,128)}, bf16[2048,1024]{1,0:T(8,128)(2,1)S(1)}, bf16[2048,1024]{1,0:T(8,128)(2,1)S(1)}, f32[1,1024]{1,0:T(1,128)S(1)}) custom-call(f32[2048,1024]{1,0:T(8,128)} %copy-done.1, f32[2048,1024]{1,0:T(8,128)} %get-tuple-element.63.gn_ref, bf16[2048,1024]{1,0:T(8,128)(2,1)} %get-tuple-element.64.ffn_ref, ...), custom_call_target="tpu_custom_call" | custom-call | flops 4294967296 | bytes 48234496 | tf_op jit(solution)/shard_map/unmix/pallas_call | solution.py:777
  597.0 2.3 copy-done.3
  599.3 2.4 copy-done.18
  601.6 2.1 copy-done.19
  603.7 5.6 all-to-all-start.2
  609.6 8.2 convolution_convert_fusion.3
  617.8 119.2 %attend_back.1 = (bf16[2048,1024]{1,0:T(8,128)(2,1)}, bf16[2048,1024]{1,0:T(8,128)(2,1)}, bf16[2048,1024]{1,0:T(8,128)(2,1)}) custom-call(s32[130]{0:T(256)S(1)} %copy-done.17, bf16[2048,3072]{1,0:T(8,128)(2,1)} %get-tuple-element.55.q_ref.k_ref.v_ref, bf16[2048,3072]{1,0:T(8,128)(2,1)} %get-tuple-element.55.q_ref.k_ref.v_ref, ...), custom_call_target="tpu_custom_call" | custom-call | flops 47815065600 | bytes 41943040 | tf_op jit(solution)/shard_map/attend_back/pallas_call | solution.py:617
  737.0 7.2 convolution_convert_fusion.2
  744.2 4.9 convolution_convert_fusion.1
  749.2 5.3 convolution_convert_fusion
  754.5 3.9 pad_maximum_fusion.1
  758.4 2.4 reduce-scatter.5.cloned.1.call-done
  760.8 11.3 %copy.58 = bf16[1024,4096]{1,0:T(8,128)(2,1)} copy(bf16[1024,4096]{0,1:T(8,128)(2,1)} %pad_maximum_fusion.1) | data formatting | bytes 16777216
  772.8 22.9 %finish.1 = (bf16[2048,1024]{1,0:T(8,128)(2,1)S(1)}, f32[1,1024]{1,0:T(1,128)S(1)}) custom-call(bf16[2048,1024]{1,0:T(8,128)(2,1)} %bitcast.33, f32[2048,1024]{1,0:T(8,128)} %get-tuple-element.77.gm_ref, bf16[2048,1024]{1,0:T(8,128)(2,1)} %get-tuple-element.69.dq_ref, bf16[2048,1024]{1,0:T(8,128)(2,1)} %get-tuple-element.70.dk_ref, ...), custom_call_target="tpu_custom_call" | custom-call | flops 12884901888 | bytes 41943040 | tf_op jit(solution)/shard_map/finish/pallas_call | solution.py:818
  795.8 2.0 copy-done.4
  797.8 5.7 all-to-all-start.3
  803.6 2.1 collective-permute-start.1
  805.7 90.1 %psum.7 = f32[2,1024]{1,0:T(2,128)S(1)} all-reduce(f32[2,1024]{1,0:T(2,128)S(1)} %pad_maximum_fusion.6), channel_id=1, replica_groups=mesh['dp'=16,'tensor'=2] {'dp','tensor'}, use_global_device_ids=true, to_apply=%region_1.0 | all-reduce | flops 2048 | bytes 16384 | tf_op jit(solution)/shard_map/psum | solution.py:1118
  896.4 6.6 convert_element_type.43
  904.9 2.3 collective-permute-start
  908.7 9.1 collective-permute-done
  921.1 4.6 copy.69
  (101 shorter events, 18.9 us)
Async XLA Ops:
  7.2 404.1 %all-gather.2.cloned.1.call-start = ((), (), s32[]{:S(2)}) async-start(), calls=%async_computation.6 | async-start | bytes 20611072 | tf_op jit(solution)/shard_map/all_gather | solution.py:1070
  11.8 2.2 copy-start.2
  13.9 1.6 copy-start.12
  15.5 1.6 copy-start.13
  159.0 2.0 copy-start.5
  161.0 2.0 copy-start.7
  163.1 1.3 copy-start.21
  165.8 2.2 copy-start.6
  174.4 2.0 copy-start
  176.4 143.3 %all-to-all-start = ((bf16[32,128,512]{2,1,0:T(8,128)(2,1)}), bf16[32,128,512]{2,1,0:T(8,128)(2,1)}, u32[]{:S(2)}, u32[]{:S(2)}) async-start(bf16[32,128,512]{2,1,0:T(8,128)(2,1)} %copy-done), calls=%async_computation | async-start | bytes 8388608 | tf_op jit(solution)/shard_map/all_to_all | solution.py:1077
  181.5 9.6 %copy-start.27 = (s32[2,16,4]{1,2,0:T(4,128)S(1)}, s32[2,16,4]{1,2,0:T(4,128)}, u32[]{:S(2)}) copy-start(s32[2,16,4]{1,2,0:T(4,128)} %param.34) | copy-start | bytes 1540
  181.5 9.6 %copy-start.28 = (s32[2,16,4]{1,2,0:T(4,128)S(1)}, s32[2,16,4]{1,2,0:T(4,128)}, u32[]{:S(2)}) copy-start(s32[2,16,4]{1,2,0:T(4,128)} %param.33) | copy-start | bytes 1540
  181.5 9.9 %copy-start.29 = (s32[2]{0:T(128)S(1)}, s32[2]{0:T(128)}, u32[]{:S(2)}) copy-start(s32[2]{0:T(128)} %param.31) | copy-start | bytes 28
  192.7 132.8 %copy-start.16 = (s32[130]{0:T(256)}, s32[130]{0:T(256)S(1)}, u32[]{:S(2)}) copy-start(s32[130]{0:T(256)S(1)} %pad_add_fusion.meta) | copy-start | bytes 1564
  193.5 0.6 copy-start.14
  194.1 2.2 copy-start.8
  219.6 2.1 copy-start.24
  319.7 108.7 %all-to-all-start.1 = ((bf16[2,1024,1024]{2,1,0:T(8,128)(2,1)}), bf16[2,1024,1024]{2,1,0:T(8,128)(2,1)}, u32[]{:S(2)}, u32[]{:S(2)}) async-start(bf16[2,1024,1024]{2,1,0:T(8,128)(2,1)} %param.35), calls=%async_computation.1 | async-start | bytes 8388608 | tf_op jit(solution)/shard_map/all_to_all | solution.py:1069
  325.3 435.5 %reduce-scatter.5.cloned.1.call-start = ((), (), s32[]{:S(2)}) async-start(), calls=%async_computation.7 | async-start | bytes 18382848 | tf_op jit(solution)/shard_map/reduce_scatter | solution.py:1091
  325.5 1.6 copy-start.22
  409.3 2.0 copy-start.10
  411.3 2.2 copy-start.9
  413.5 2.2 copy-start.11
  423.2 3.2 copy-start.1
  426.4 2.0 copy-start.20
  597.0 2.3 copy-start.3
  599.3 2.4 copy-start.18
  601.6 2.1 copy-start.19
  603.7 154.7 %all-to-all-start.2 = ((bf16[2,1024,1024]{2,1,0:T(8,128)(2,1)}), bf16[2,1024,1024]{2,1,0:T(8,128)(2,1)}, u32[]{:S(2)}, u32[]{:S(2)}) async-start(bf16[2,1024,1024]{2,1,0:T(8,128)(2,1)} %bitcast.30), calls=%async_computation.3 | async-start | bytes 8388608 | tf_op jit(solution)/shard_map/all_to_all | solution.py:1095
  609.3 293.8 %reduce-scatter.7.cloned.1.call-start = ((), (), s32[]{:S(2)}) async-start(), calls=%async_computation.8 | async-start | bytes 8912896
  609.6 8.2 copy-start.17
  609.6 8.2 copy-start.23
  617.8 119.2 %copy-start.25 = (bf16[2048,1024]{1,0:T(8,128)(2,1)S(1)}, bf16[2048,1024]{1,0:T(8,128)(2,1)}, u32[]{:S(2)}) copy-start(bf16[2048,1024]{1,0:T(8,128)(2,1)} %copy-done.24) | copy-start | bytes 12582916
  737.0 7.2 copy-start.30
  744.2 5.0 copy-start.31
  772.1 0.7 copy-start.15
  795.7 2.0 copy-start.4
  797.8 5.7 copy-start.26
  797.8 98.6 %all-to-all-start.3 = ((bf16[2,1024,1024]{2,1,0:T(8,128)(2,1)}), bf16[2,1024,1024]{2,1,0:T(8,128)(2,1)}, u32[]{:S(2)}, u32[]{:S(2)}) async-start(bf16[2,1024,1024]{2,1,0:T(8,128)(2,1)} %bitcast.31), calls=%async_computation.4 | async-start | bytes 8388608 | tf_op jit(solution)/shard_map/all_to_all | solution.py:1104
  803.6 99.4 %collective-permute-start.1 = (bf16[64,4224]{1,0:T(8,128)(2,1)S(1)}, bf16[64,4224]{1,0:T(8,128)(2,1)S(1)}, u32[]{:S(2)}, u32[]{:S(2)}) collective-permute-start(bf16[64,4224]{1,0:T(8,128)(2,1)S(1)} %pad_maximum_fusion.3), channel_id=1, source_target_pairs={{0,1},{1,0},{2,3},{3,2},{4,5},{5,4},{6,7},{7,6},{8,9},{9,8},{10,11... | collective-permute-start | bytes 1622024 | tf_op jit(solution)/shard_map/ppermute | solution.py:1042
  904.9 12.9 %collective-permute-start = (bf16[64,2048]{0,1:T(8,128)(2,1)S(1)}, bf16[64,2048]{0,1:T(8,128)(2,1)S(1)}, u32[]{:S(2)}, u32[]{:S(2)}) collective-permute-start(bf16[64,2048]{0,1:T(8,128)(2,1)S(1)} %pad_maximum_fusion.4), channel_id=1, source_target_pairs={{0,1},{1,0},{2,3},{3,2},{4,5},{5,4},{6,7},{7,6},{8,9},{9,8},{10,11... | collective-permute-start | bytes 786440 | tf_op jit(solution)/shard_map/ppermute | solution.py:1042
Sparse Core Ops, SparseCore 0:
  164.5 184.5 all-gather.1
  577.0 183.7 reduce-scatter.4
  772.3 103.7 reduce-scatter.6

commit v3 on v2

--- a/solution.py
+++ b/solution.py
@@ -425,16 +425,25 @@
     return keys <= reach
 
 
-def pick_blocks(meta, block, own, other, buf):
+def pick_own(meta, block, own, buf):
     for i in range(KR):
         c = meta[2 + block * KR + i]
         buf[pl.ds(i * CBLOCK, CBLOCK), :] = own[0, pl.ds(pl.multiple_of(c * CBLOCK, CBLOCK), CBLOCK), :]
+
+
+def pick_other(meta, block, other, buf, start=0):
+    for i in range(KR):
         d = meta[2 + (L // QBLOCK) * KR + block * KR + i]
-        buf[pl.ds((KR + i) * CBLOCK, CBLOCK), :] = other[d, 0, 0]
+        buf[pl.ds(start + i * CBLOCK, CBLOCK), :] = other[d, 0, 0]
+
+
+def pick_blocks(meta, block, own, other, buf):
+    pick_own(meta, block, own, buf)
+    pick_other(meta, block, other, buf, KR * CBLOCK)
 
 
 def attend_kernel(
-    meta, q_ref, k_ref, v_ref, ok_ref, ov_ref, pk_ref, pv_ref, ctx_ref, lse_ref, kbuf, vbuf, sbuf, smem, *, pair
+    meta, q_ref, k_ref, v_ref, ok_ref, ov_ref, ctx_ref, lse_ref, kbuf, vbuf, sbuf, smem, *, pair
 ):
     step = pl.program_id(1)
     limit = meta[0]
@@ -443,8 +452,8 @@
     tiles = jnp.maximum(step + 1, free)
     blocks = TQ // QBLOCK
     for b in range(blocks):
-        pick_blocks(meta, step * blocks + b, ok_ref, pk_ref, kbuf.at[b])
-        pick_blocks(meta, step * blocks + b, ov_ref, pv_ref, vbuf.at[b])
+        pick_own(meta, step * blocks + b, ok_ref, kbuf.at[b])
+        pick_own(meta, step * blocks + b, ov_ref, vbuf.at[b])
     state = []
     for h in range(pair):
         cs = pl.ds(h * HD, HD)
@@ -493,8 +502,31 @@
     for h in range(pair):
         cs = pl.ds(h * HD, HD)
         total = jnp.sum(state[h][0], axis=1, keepdims=True)
-        ctx_ref[:, cs] = (state[h][1] / total).astype(BF16)
+        ctx_ref[:, cs] = state[h][1] / total
         lse_ref[:, cs] = jnp.broadcast_to(tops[h] * SCALE + jnp.log(total), (TQ, HD))
+
+
+def attend_other_kernel(meta, q_ref, pk_ref, pv_ref, part_ref, plse_ref, ctx_ref, lse_ref, kbuf, vbuf, *, pair):
+    step = pl.program_id(1)
+    blocks = TQ // QBLOCK
+    for b in range(blocks):
+        pick_other(meta, step * blocks + b, pk_ref, kbuf.at[b])
+        pick_other(meta, step * blocks + b, pv_ref, vbuf.at[b])
+    for h in range(pair):
+        cs = pl.ds(h * HD, HD)
+        rows = [pl.ds(b * QBLOCK, QBLOCK) for b in range(blocks)]
+        s = jnp.concatenate([mm(q_ref[rows[b], cs], kbuf[b, :, cs], NT) for b in range(blocks)], 0)
+        before = plse_ref[:, cs]
+        top = jnp.maximum(before, jnp.max(fold_max(s), axis=1, keepdims=True) * SCALE)
+        keep = jnp.exp(before - top)
+        p = jnp.exp2(s * EXP_SCALE - top[:, :1] * LOG2E)
+        low = p.astype(BF16)
+        more = jnp.concatenate(
+            [mm(low[b * QBLOCK : (b + 1) * QBLOCK], vbuf[b, :, cs]) for b in range(blocks)], 0
+        )
+        total = keep + jnp.sum(fold_sum(p), axis=1, keepdims=True)
+        ctx_ref[:, cs] = ((part_ref[:, cs] * keep + more) / total).astype(BF16)
+        lse_ref[:, cs] = top + jnp.log(total)
 
 
 def attend_back_kernel(
@@ -584,27 +616,51 @@
     ]
 
 
-def attend(meta, qkv, own_k, own_v, fetched, pair=2):
+def attend(meta, qkv, own_k, own_v, pair=2):
     width = qkv.shape[1] // 3
     heads = width // HD
     wide = pair * HD
     row = pl.BlockSpec((TQ, wide), lambda h, i, meta: (i, h))
-    area = L * 1900 * width
+    area = L * 1600 * width
     return pl.pallas_call(
         functools.partial(attend_kernel, pair=pair),
         grid_spec=pltpu.PrefetchScalarGridSpec(
             num_scalar_prefetch=1,
             grid=(heads // pair, L // TQ),
-            in_specs=attention_specs(heads, pair),
+            in_specs=attention_specs(heads, pair)[:5],
             out_specs=[row, row],
-            scratch_shapes=[pltpu.VMEM((TQ // QBLOCK, 2 * KR * CBLOCK, wide), BF16)] * 2
-            + [pltpu.VMEM((pair, L // TK, TQ, TK), F32), pltpu.VMEM((pair, TQ, 2 * KR * CBLOCK), F32)],
+            scratch_shapes=[pltpu.VMEM((TQ // QBLOCK, KR * CBLOCK, wide), BF16)] * 2
+            + [pltpu.VMEM((pair, L // TK, TQ, TK), F32), pltpu.VMEM((pair, TQ, KR * CBLOCK), F32)],
+        ),
+        out_shape=[jax.ShapeDtypeStruct((L, width), F32)] * 2,
+        compiler_params=pltpu.CompilerParams(vmem_limit_bytes=40 * MIB),
+        cost_estimate=pl.CostEstimate(flops=12 * area, bytes_accessed=30 * MIB, transcendentals=area // HD),
+        name="attend",
+    )(meta, qkv, qkv, qkv, own_k, own_v)
+
+
+def attend_other(meta, qkv, fetched, partial, lse, pair=4):
+    width = qkv.shape[1] // 3
+    heads = width // HD
+    wide = pair * HD
+    row = pl.BlockSpec((TQ, wide), lambda h, i, meta: (i, h))
+    specs = attention_specs(heads, pair)
+    return pl.pallas_call(
+        functools.partial(attend_other_kernel, pair=pair),
+        grid_spec=pltpu.PrefetchScalarGridSpec(
+            num_scalar_prefetch=1,
+            grid=(heads // pair, L // TQ),
+            in_specs=[specs[0], specs[5], specs[6], row, row],
+            out_specs=[row, row],
+            scratch_shapes=[pltpu.VMEM((TQ // QBLOCK, KR * CBLOCK, wide), BF16)] * 2,
         ),
         out_shape=[jax.ShapeDtypeStruct((L, width), BF16), jax.ShapeDtypeStruct((L, width), F32)],
         compiler_params=pltpu.CompilerParams(vmem_limit_bytes=40 * MIB),
-        cost_estimate=pl.CostEstimate(flops=8 * area, bytes_accessed=30 * MIB, transcendentals=area // HD),
-        name="attend",
-    )(meta, qkv, qkv, qkv, own_k, own_v, fetched, fetched)
+        cost_estimate=pl.CostEstimate(
+            flops=4 * L * 256 * width, bytes_accessed=30 * MIB, transcendentals=L * 256 * heads
+        ),
+        name="attend_other",
+    )(meta, qkv, fetched, fetched, partial, lse)
 
 
 def attend_back(meta, qkv, own_k, own_v, fetched, grad_context, context, lse, pair=2):
@@ -684,7 +740,7 @@
     )(x, context, gain, weights)
 
 
-def ffn_kernel(n_ref, g_ref, wg_ref, wu_ref, wd_ref, out_ref, gn_ref, dg_ref, du_ref, dd_ref, acc, ag, au, ad):
+def ffn_kernel(n_ref, g_ref, wg_ref, wu_ref, wd_ref, out_ref, gn_ref, grads_ref, acc, ag, au, ad):
     tile = pl.program_id(0)
     last = pl.num_programs(0) - 1
 
@@ -717,9 +773,9 @@
         return carry
 
     lax.fori_loop(0, L // ROWS, chunk, 0)
-    dg_ref[...] = ag[...].astype(BF16)
-    du_ref[...] = au[...].astype(BF16)
-    dd_ref[...] = ad[...].astype(BF16)
+    grads_ref[:, :HT] = ag[...].astype(BF16)
+    grads_ref[:, HT : 2 * HT] = au[...].astype(BF16)
+    grads_ref[:, 2 * HT :] = ad[...].astype(BF16)
 
     @pl.when(tile == last)
     def _():
@@ -732,14 +788,14 @@
     lead = width // HT
     part = lambda k: pl.BlockSpec((width, HT), lambda j: (0, lead + k * tiles + j))
     whole = pl.BlockSpec((L, width), lambda j: (0, 0), pipeline_mode=once)
-    grad = pl.BlockSpec((width, HT), lambda j: (0, j))
+    grad = pl.BlockSpec((width, 3 * HT), lambda j: (0, j))
     return pl.pallas_call(
         ffn_kernel,
         grid=(tiles,),
         in_specs=[whole, whole, part(0), part(1), part(2)],
-        out_specs=[whole, whole, grad, grad, grad],
+        out_specs=[whole, whole, grad],
         out_shape=[jax.ShapeDtypeStruct((L, width), BF16), jax.ShapeDtypeStruct((L, width), F32)]
-        + [jax.ShapeDtypeStruct((width, hidden), BF16)] * 3,
+        + [jax.ShapeDtypeStruct((width, 3 * hidden), BF16)],
         scratch_shapes=[pltpu.VMEM((L, width), F32)] + [pltpu.VMEM((width, HT), F32)] * 3,
         compiler_params=pltpu.CompilerParams(vmem_limit_bytes=56 * MIB),
         cost_estimate=pl.CostEstimate(
@@ -792,39 +848,275 @@
     )(mixed, grad_normed, ffn_out, cotangent, gain, weights)
 
 
-def finish_kernel(x_ref, gm_ref, dq_ref, dk_ref, dv_ref, gain_ref, w_ref, gt_ref, gg_ref):
-    width = x_ref.shape[1]
-    grad = mm(dq_ref[...], w_ref[:, :width], NT)
-    grad += mm(dk_ref[...], w_ref[:, width : 2 * width], NT)
-    grad += mm(dv_ref[...], w_ref[:, 2 * width : 3 * width], NT)
-    rows = x_ref[...].astype(F32)
-    scale = lax.rsqrt(jnp.mean(rows * rows, axis=1, keepdims=True) + EPS)
-    unit = rows * scale
-    inner = grad * gain_ref[...]
-    back = scale * (inner - unit * jnp.mean(inner * unit, axis=1, keepdims=True))
-    gt_ref[...] = (gm_ref[...] + back).astype(BF16)
-
-    @pl.when(pl.program_id(0) == 0)
-    def _():
-        gg_ref[...] = jnp.zeros_like(gg_ref)
-
-    gg_ref[...] += jnp.sum(grad * unit, axis=0, keepdims=True)
-
-
-def finish(x, grad_mixed, dq, dk, dv, gain, weights):
+RING = 8
+RIGHT = RING // 2
+LEFT = RING - 1 - RIGHT
+
+
+def ring_place(p):
+    y = p // 4
+    return (p + y * (7 - 2 * p)) * 2 + y
+
+
+def meet(devices, me, spot):
+    barrier = pltpu.get_barrier_semaphore()
+    for d in range(1, devices):
+        pl.semaphore_signal(
+            barrier, inc=1, device_id=((me + d) % devices, spot), device_id_type=pl.DeviceIdType.MESH
+        )
+    pl.semaphore_signal(barrier, inc=1, device_id=(me, 1 - spot), device_id_type=pl.DeviceIdType.MESH)
+    pl.semaphore_wait(barrier, devices)
+
+
+def remote(src, dst, send, recv, device):
+    return pltpu.make_async_remote_copy(
+        src_ref=src, dst_ref=dst, send_sem=send, recv_sem=recv, device_id=device, device_id_type=pl.DeviceIdType.MESH
+    )
+
+
+FT = 256
+
+
+def finish_kernel(
+    x_ref, gm_ref, n_ref, ctx_ref, br_ref, dq_ref, dk_ref, dv_ref, w_ref, gain_ref, gain_two_ref,
+    gt_ref, sums_ref, share_ref,
+    n_buf, ctx_buf, br_buf, dq_buf, dk_buf, dv_buf, w_buf, x_buf, gm_buf, gt_buf,
+    part, got, land, across, gains, gain_land,
+    load_sem, x_sem, gm_sem, gt_sem, pair_send, pair_recv, ring_send, ring_recv, x_send, x_recv, g_send, g_recv,
+    *, devices,
+):
+    me = lax.axis_index("dp")
+    spot = lax.axis_index("tensor")
+    core = me % 2
+    z, y = me // 4, (me // 2) % 2
+    place = z + y * (7 - 2 * z)
+    width = n_buf.shape[1]
+    half = width // 2
+    rows = part.shape[2]
+    loads = [
+        pltpu.make_async_copy(src, dst, load_sem.at[i])
+        for i, (src, dst) in enumerate(
+            [
+                (ctx_ref, ctx_buf), (br_ref, br_buf), (n_ref, n_buf), (dv_ref, dv_buf),
+                (dk_ref, dk_buf), (dq_ref, dq_buf), (w_ref.at[:, pl.ds(0, 3 * width)], w_buf),
+            ]
+        )
+    ]
+    for copy in loads:
+        copy.start()
+    meet(devices, me, spot)
+
+    def tile_in(t, slot):
+        rs = pl.ds(pl.multiple_of(t * FT, FT), FT)
+        return [
+            pltpu.make_async_copy(x_ref.at[rs, :], x_buf.at[slot], x_sem.at[slot]),
+            pltpu.make_async_copy(gm_ref.at[rs, :], gm_buf.at[slot], gm_sem.at[slot]),
+        ]
+
+    def tile_out(t, slot):
+        rs = pl.ds(pl.multiple_of(t * FT, FT), FT)
+        return pltpu.make_async_copy(gt_buf.at[slot], gt_ref.at[rs, :], gt_sem.at[slot])
+
+    for copy in tile_in(0, 0):
+        copy.start()
+
+    pair = (me + 1 - 2 * core, spot)
+
+    def to_pair(m):
+        cs = pl.ds(m * width, width)
+        return remote(part.at[:, 1 - core, :, cs], got.at[:, :, cs], pair_send.at[m], pair_recv.at[m], pair)
+
+    def product(m, left, right):
+        def chunk(c, carry):
+            cs = pl.ds(pl.multiple_of(c * half, half), half)
+            value = mm(left[...], right[:, cs], TN).astype(BF16)
+            part[:, :, :, pl.ds(pl.multiple_of(m * width + c * half, half), half)] = value.reshape(
+                part.shape[0], 2, rows, half
+            )
+            return carry
+
+        lax.fori_loop(0, 2, chunk, 0)
+        to_pair(m).start()
+
+    def join(m):
+        to_pair(m).wait_recv()
+        cs = pl.ds(m * width, width)
+
+        def one(b, carry):
+            got[b, :, cs] = (got[b, :, cs].astype(F32) + part[b, core, :, cs].astype(F32)).astype(BF16)
+            return carry
+
+        lax.fori_loop(0, part.shape[0], one, 0)
+
+    span = 2 * width
+    neighbours = [(place + 1) % RING, (place + RING - 1) % RING]
+
+    def held_block(direction, s):
+        p = (place + 2 * RING - 1 - s) % RING if direction == 0 else (place + 1 + s) % RING
+        return got.at[ring_place(p), :, pl.ds(direction * span, span)]
+
+    def hop(direction, s):
+        to = ring_place(neighbours[direction]) * 2 + core
+        return remote(
+            held_block(direction, s), land.at[direction, s],
+            ring_send.at[direction, s], ring_recv.at[direction, s], (to, spot),
+        )
+
+    def advance(direction, s, more=True):
+        hop(direction, s).wait_recv()
+        block = held_block(direction, s + 1)
+        block[...] = (block[...].astype(F32) + land[direction, s].astype(F32)).astype(BF16)
+        if more:
+            hop(direction, s + 1).start()
+
+    def finish_rows(t, slot):
+        for copy in tile_in(t, slot):
+            copy.wait()
+        rs = pl.ds(pl.multiple_of(t * FT, FT), FT)
+        grad = mm(dq_buf[rs, :], w_buf[:, :width], NT)
+        grad += mm(dk_buf[rs, :], w_buf[:, width : 2 * width], NT)
+        grad += mm(dv_buf[rs, :], w_buf[:, 2 * width :], NT)
+        values = x_buf[slot].astype(F32)
+        scale = lax.rsqrt(jnp.mean(values * values, axis=1, keepdims=True) + EPS)
+        unit = values * scale
+        inner = grad * gain_ref[...]
+        back = scale * (inner - unit * jnp.mean(inner * unit, axis=1, keepdims=True))
+        gt_buf[slot] = (gm_buf[slot] + back).astype(BF16)
+        gains[:1, :] += jnp.sum(grad * unit, axis=0, keepdims=True)
+
+    for i in (0, 1):
+        loads[i].wait()
+    product(0, br_buf, ctx_buf)
+    for i in (2, 3):
+        loads[i].wait()
+    product(1, n_buf, dv_buf)
+    join(0)
+    join(1)
+    hop(0, 0).start()
+    loads[4].wait()
+    product(2, n_buf, dk_buf)
+    advance(0, 0)
+    loads[5].wait()
+    product(3, n_buf, dq_buf)
+    advance(0, 1)
+    join(2)
+    join(3)
+    hop(1, 0).start()
+    loads[6].wait()
+    gains[:1, :] = jnp.zeros((1, width), F32)
+    gains[1:, :] = gain_two_ref[...]
+
+    def sweep(i, carry):
+        for slot in (0, 1):
+            t = 2 * i + slot
+            if slot == 0:
+                for copy in tile_in(t + 1, 1):
+                    copy.start()
+            else:
+
+                @pl.when(i < 3)
+                def _():
+                    for copy in tile_in(t + 1, 0):
+                        copy.start()
+
+            @pl.when(i > 0)
+            def _():
+                tile_out(t - 2, slot).wait()
+
+            finish_rows(t, slot)
+            tile_out(t, slot).start()
+        advance(0, i + 2)
+        advance(1, i)
+        return carry
+
+    lax.fori_loop(0, L // FT // 2, sweep, 0)
+
+    partners = [
+        (me + 1 - 2 * core, spot),
+        (me + 2 - 4 * y, spot),
+        (me + 4 - 8 * (z % 2), spot),
+        (me + 8 - 16 * (z // 2), spot),
+        (me, 1 - spot),
+    ]
+
+    def add_gains(r):
+        return remote(gains, gain_land.at[r], g_send.at[r], g_recv.at[r], partners[r])
+
+    def gain_round(r):
+        add_gains(r).wait()
+        gains[...] = gains[...] + gain_land[r]
+        if r < 4:
+            add_gains(r + 1).start()
+
+    own = ring_place(place)
+    peer = (me, 1 - spot)
+
+    def over(m):
+        return remote(
+            got.at[own, :, pl.ds(m * width + half, half)], across.at[:, pl.ds(m * half, half)],
+            x_send.at[m], x_recv.at[m], peer,
+        )
+
+    add_gains(0).start()
+    advance(0, 6, False)
+    over(0).start()
+    over(1).start()
+    gain_round(0)
+    advance(1, 4)
+    gain_round(1)
+    gain_round(2)
+    advance(1, 5)
+    gain_round(3)
+    gain_round(4)
+    advance(1, 6, False)
+    over(2).start()
+    over(3).start()
+    sums_ref[...] = gains[...]
+    for m in range(4):
+        over(m).wait_recv()
+        cs = pl.ds(m * half, half)
+        share_ref[:, cs] = got[own, :, pl.ds(m * width, half)].astype(F32) + across[:, cs].astype(F32)
+    for m in range(4):
+        over(m).wait_send()
+        to_pair(m).wait_send()
+    for s in range(RING - 1):
+        hop(0, s).wait_send()
+        hop(1, s).wait_send()
+    tile_out(L // FT - 2, 0).wait()
+    tile_out(L // FT - 1, 1).wait()
+
+
+def finish(x, grad_mixed, normed, context, branch, dq, dk, dv, weights, gain, gain_two_part, devices):
     width = x.shape[1]
-    row = pl.BlockSpec((ROWS, width), lambda i: (i, 0))
-    one = pl.BlockSpec((1, width), lambda i: (0, 0))
+    rows = width // devices
+    anywhere = pl.BlockSpec(memory_space=pltpu.HBM)
+    vmem = pl.BlockSpec(memory_space=pltpu.VMEM)
+    dma = pltpu.SemaphoreType.DMA
+    whole = pltpu.VMEM((L, width), BF16)
     return pl.pallas_call(
-        finish_kernel,
-        grid=(L // ROWS,),
-        in_specs=[row, row, row, row, row, one, pl.BlockSpec((width, 3 * width), lambda i: (0, 0))],
-        out_specs=[row, one],
-        out_shape=[jax.ShapeDtypeStruct((L, width), BF16), jax.ShapeDtypeStruct((1, width), F32)],
-        compiler_params=pltpu.CompilerParams(vmem_limit_bytes=48 * MIB),
-        cost_estimate=pl.CostEstimate(flops=6 * L * width * width, bytes_accessed=40 * MIB, transcendentals=0),
+        functools.partial(finish_kernel, devices=devices),
+        in_specs=[anywhere] * 9 + [vmem] * 2,
+        out_specs=[anywhere, vmem, vmem],
+        out_shape=[
+            jax.ShapeDtypeStruct((L, width), BF16),
+            jax.ShapeDtypeStruct((2, width), F32),
+            jax.ShapeDtypeStruct((rows, 2 * width), F32),
+        ],
+        scratch_shapes=[
+            whole, whole, whole, whole, whole, whole, pltpu.VMEM((width, 3 * width), BF16),
+            pltpu.VMEM((2, FT, width), BF16), pltpu.VMEM((2, FT, width), F32), pltpu.VMEM((2, FT, width), BF16),
+            pltpu.VMEM((RING, 2, rows, 4 * width), BF16),
+            pltpu.VMEM((RING, rows, 4 * width), BF16),
+            pltpu.VMEM((2, RING - 1, rows, 2 * width), BF16),
+            pltpu.VMEM((rows, 2 * width), BF16),
+            pltpu.VMEM((2, width), F32), pltpu.VMEM((5, 2, width), F32),
+            dma((7,)), dma((2,)), dma((2,)), dma((2,)), dma((4,)), dma((4,)),
+            dma((2, RING - 1)), dma((2, RING - 1)), dma((4,)), dma((4,)), dma((5,)), dma((5,)),
+        ],
+        compiler_params=pltpu.CompilerParams(collective_id=1, has_side_effects=True, vmem_limit_bytes=60 * MIB),
+        cost_estimate=pl.CostEstimate(flops=14 * L * width * width, bytes_accessed=80 * MIB, transcendentals=0),
         name="finish",
-    )(x, grad_mixed, dq, dk, dv, gain, weights)
+    )(x, grad_mixed, normed, context, branch, dq, dk, dv, weights, gain, gain_two_part)
 
 
 def pick_kernel(table, held_ref, sent_ref, sems):
@@ -853,11 +1145,6 @@
         cost_estimate=pl.CostEstimate(flops=0, bytes_accessed=2 * held.size * 2, transcendentals=0),
         name="pick_rows",
     )(table, held)
-
-
-RING = 8
-RIGHT = RING // 2
-LEFT = RING - 1 - RIGHT
 
 
 def spread_kernel(
@@ -1010,7 +1297,7 @@
 def spread(tokens, cache_keys, cache_values, small, extra, big, devices):
     micro, shard_len, width = tokens.shape
     rows, cols = small.shape[0], small.shape[1] // 3
-    anywhere = pl.BlockSpec(memory_space=pl.ANY)
+    anywhere = pl.BlockSpec(memory_space=pltpu.HBM)
     vmem = pl.BlockSpec(memory_space=pltpu.VMEM)
     dma = pltpu.SemaphoreType.DMA
     return pl.pallas_call(
@@ -1069,8 +1356,8 @@
     cotangent = exchange(grad_out).reshape(L, width)
     second_all = lax.all_gather(second_rows, "dp", axis=0, tiled=True)
 
-    tail = first_all[:, 3 * width :]
-    gains = tail[:, :2].astype(F32).T
+    tail = lax.optimization_barrier(first_all[:, 3 * width :])
+    gains = mm((jnp.arange(2)[:, None] == jnp.arange(HD)[None, :]).astype(BF16), tail, NT)
     gain_one, gain_two = gains[:1], gains[1:]
     table = tail[:, 2].reshape(devices, rows_held)[:, :micro].reshape(seqs).astype(jnp.int32)
     sent = pick_rows(table, held.reshape(seqs, 2 * CBLOCK, cols))
@@ -1084,38 +1371,27 @@
         ]
     )
     normed, qkv = project(x, gain_one, first_all)
-    context, lse = attend(meta, qkv, own_k, own_v, fetched)
+    partial, partial_lse = attend(meta, qkv, own_k, own_v)
+    context, lse = attend_other(meta, qkv, fetched, partial, partial_lse)
     mixed, normed_two = mix(x, context, gain_two, second_all)
-    ffn_out, grad_normed_two, d_gate, d_up, d_down = ffn(normed_two, cotangent, second_all, width, hidden)
+    ffn_out, grad_normed_two, ffn_grads = ffn(normed_two, cotangent, second_all, width, hidden)
     share = functools.partial(lax.psum_scatter, axis_name="dp", scatter_dimension=0, tiled=True)
-    ffn_share = share(jnp.concatenate([d_gate, d_up, d_down], axis=1))
+    ffn_share = share(ffn_grads)
     out, grad_mixed, branch, grad_context, gain_part_two = unmix(
         mixed, grad_normed_two, ffn_out, cotangent, gain_two, second_all
     )
     out = exchange(out.reshape(2, shard_len, width))
-    d_out = inner_rows(branch, context).astype(BF16)
     dq, dk, dv = attend_back(meta, qkv, own_k, own_v, fetched, grad_context, context, lse)
-    d_qkv = [inner_rows(normed, d).astype(BF16) for d in (dq, dk, dv)]
-    attn_grads, ffn_share, out = lax.optimization_barrier(
-        (jnp.concatenate([d_out] + d_qkv, axis=1), ffn_share, out)
-    )
-    attn_share = share(attn_grads)
-    grad_tokens, gain_part_one = finish(x, grad_mixed, dq, dk, dv, gain_one, first_all)
+    dq, out, ffn_share = lax.optimization_barrier((dq, out, ffn_share))
+    grad_tokens, gain_sums, attn_share = finish(
+        x, grad_mixed, normed, context, branch, dq, dk, dv, first_all, gain_one, gain_part_two, devices
+    )
     grad_tokens = exchange(grad_tokens.reshape(2, shard_len, width)).astype(F32)
-
-    def halves(values, widths):
-        mine, theirs, start = [], [], 0
-        for w in widths:
-            mine.append(values[:, start : start + w])
-            theirs.append(values[:, start + w : start + 2 * w])
-            start += 2 * w
-        got = swap(jnp.concatenate(theirs, axis=1))
-        total = jnp.concatenate(mine, axis=1).astype(F32) + got.astype(F32)
-        return jnp.split(total, [sum(widths[: i + 1]) for i in range(len(widths) - 1)], axis=1)
-
-    g_gate, g_up, g_down = halves(ffn_share, [hidden_held] * 3)
-    g_out, g_query, g_key, g_value = halves(attn_share, [cols] * 4)
-    gain_sums = lax.psum(jnp.concatenate([gain_part_one, gain_part_two], axis=0), ("dp", "tensor"))
+    g_out, g_value, g_key, g_query = jnp.split(attn_share, 4, axis=1)
+    pieces = ffn_share.reshape(rows_held, hidden // HT, 3, HT).swapaxes(1, 2).reshape(rows_held, 3, hidden)
+    got = swap(pieces[:, :, hidden_held:])
+    total = pieces[:, :, :hidden_held].astype(F32) + got.astype(F32)
+    g_gate, g_up, g_down = total[:, 0], total[:, 1], total[:, 2]
     return (
         out, grad_tokens, gain_sums[0], g_query, g_key, g_value, g_out.T, gain_sums[1], g_gate, g_up, g_down.T,
     )

time: 938 us -> 934 us (level)
  blocking collectives: 90.1 us -> 0 us
  waiting for transfers between devices: 110 us -> 195 us
  Pallas kernels: 558 us -> 623 us
  matrix products: 25.6 us -> 0.16 us
  local copies, waits for them, and re-layouts: 78.7 us -> 58.2 us
  other arithmetic: 29 us -> 10.3 us
    psum x1 -> x0, blocking collectives: 90.1 us -> none  [sequence_body(): lax.psum(jnp.concatenate([gain_part_one, gain_part_two], axis=0), ('dp',...]
    pallas_call x1 -> x2, Pallas kernels: 22.9 us -> 108 us  [the longest x1 87.4 us: finish(): pl.pallas_call(functools.partial(finish_kernel, devices=devices), in_spec...]
    ppermute x2 -> x1, waiting for transfers between devices: 9.07 us -> 47.3 us  [swap(): return lax.ppermute(values, 'tensor', [(0, 1), (1, 0)])]
    reduce_scatter x1, waiting for transfers between devices: 2.41 us -> 39.8 us  [sequence_body(): ffn_share = share(ffn_grads)]
    dot_general x4 -> x1, matrix products: 25.6 us -> 0.16 us  [mm(): return lax.dot_general(left, right, dims, preferred_element_type=F32)]
    concatenate x5 -> x0, other arithmetic: 17.9 us -> none  [the longest x1 13.8 us: sequence_body(): ffn_share = share(jnp.concatenate([d_gate, d_up, d_down], axis=1))]
    unnamed x78 -> x59, local copies, waits for them, and re-layouts: 62.3 us -> 50.2 us
    pallas_call x1, Pallas kernels: 82.2 us -> 71.3 us  [attend(): pl.pallas_call(functools.partial(attend_kernel, pair=pair), grid_spec=plt...]
  transfers between devices with their start and end apart: 9 -> 7, of which waited for: 3 -> 3; matrix products, arithmetic and copies ran while one was open for 6% -> 1% of each run, Pallas kernels for 30% -> 28%
where the time goes in v3:
time: 934 us; the launch traced here: 930 us
  Pallas kernels  623 us (67%)
  waiting for transfers between devices  195 us (21%)
  local copies, waits for them, and re-layouts  58.2 us (6%)
  starting transfers between devices  27.5 us (3%)
  between operations  14.8 us (2%)
  other arithmetic  10.3 us (1%)
    pallas_call x1, Pallas kernels, spread(): pl.pallas_call(spread_kernel, in_specs=[anywhere, anywhere, anywhere, vme...  142 us
    pallas_call x1, Pallas kernels, ffn(): pl.pallas_call(ffn_kernel, grid=(tiles,), in_specs=[whole, whole, part(0)...  135 us
    pallas_call x1, Pallas kernels, attend_back(): pl.pallas_call(functools.partial(attend_back_kernel, pair=pair), grid_spe...  112 us
    all_to_all x1, waiting for transfers between devices, sequence_body(): lax.all_to_all(sent, ('dp', 'tensor'), split_axis=0, concat_axis=0, tiled...  108 us
    pallas_call x1, Pallas kernels, finish(): pl.pallas_call(functools.partial(finish_kernel, devices=devices), in_spec...  87.4 us
    pallas_call x1, Pallas kernels, attend(): pl.pallas_call(functools.partial(attend_kernel, pair=pair), grid_spec=plt...  71.3 us
    unnamed x59, local copies, waits for them, and re-layouts  50.2 us
    ppermute x1, waiting for transfers between devices, swap(): return lax.ppermute(values, 'tensor', [(0, 1), (1, 0)])  47.3 us
  transfers between devices with their start and end apart: 7, of which 3 were waited for; matrix products, arithmetic and copies ran while one was open for 1% of the time, Pallas kernels for 28%

profile of v3, /device:TPU:0, one launch (start us, length us, event | category | flops | bytes accessed | tf_op | source)
XLA Modules:
  0.0 929.7 jit_solution(10747786652453118576)
XLA Ops:
  8.8 0.8 copy.38
  9.6 0.9 pad_maximum_fusion.1.small_ref
  10.6 1.1 pad_maximum_fusion.big_ref
  11.8 2.2 copy-done.3
  13.9 1.6 copy-done.12
  15.5 1.6 copy-done.13
  17.1 141.9 %spread.1 = (bf16[2,1024,1024]{2,1,0:T(8,128)(2,1)S(1)}, bf16[2,1024,512]{2,1,0:T(8,128)(2,1)S(1)}, bf16[2,1024,512]{2,1,0:T(8,128)(2,1)S(1)}, bf16[16,2,2,64,51...) custom-call(bf16[2,1024,1024]{2,1,0:T(8,128)(2,1)S(1)} %copy-done.3, ...), custom_call_target="tpu_custom_call" | custom-call | bytes 314572800 | tf_op jit(solution)/shard_map/spread/pallas_call | solution.py:1303
  159.0 2.0 copy-done.5
  161.0 2.0 copy-done.7
  163.1 1.3 copy-done.18
  164.4 1.0 slice.52
  165.8 2.2 copy-done.6
  168.0 6.4 pick_rows.1
  174.4 2.0 copy-done
  176.4 5.1 all-to-all-start
  184.0 2.3 copy-done.8
  186.3 23.3 %project.1 = (bf16[2048,1024]{1,0:T(8,128)(2,1)S(1)}, bf16[2048,3072]{1,0:T(8,128)(2,1)}) custom-call(bf16[2048,1024]{1,0:T(8,128)(2,1)S(1)} %bitcast.32, f32[1,1024]{1,0:T(1,128)S(1)} %get-tuple-element.95.gain_ref, bf16[1024,3200]{1,0:T(8,128)(2,1)} %get-tuple-element.55.w_ref), custom_call_target="tpu_custom_call" | custom-call | flops 12884901888 | bytes 27262976 | tf_op jit(solution)/shard_map/project/pallas_call | solution.py:709
  209.6 2.0 copy-done.22
  211.6 108.2 %all-to-all-done = bf16[32,128,512]{2,1,0:T(8,128)(2,1)} async-done(((bf16[32,128,512]{2,1,0:T(8,128)(2,1)}), bf16[32,128,512]{2,1,0:T(8,128)(2,1)}, u32[]{:S(2)}, u32[]{:S(2)}) %all-to-all-start) | async-done | bytes 4194336 | tf_op jit(solution)/shard_map/all_to_all | solution.py:1364
  319.7 5.7 all-to-all-start.1
  325.7 1.6 copy-done.19
  327.3 71.3 %attend.1 = (f32[2048,1024]{1,0:T(8,128)S(1)}, f32[2048,1024]{1,0:T(8,128)}) custom-call(s32[130]{0:T(256)S(1)} %pad_add_fusion.meta, bf16[2048,3072]{1,0:T(8,128)(2,1)} %get-tuple-element.56.q_ref.k_ref.v_ref, bf16[2048,3072]{1,0:T(8,128)(2,1)} %get-tuple-element.56.q_ref.k_ref.v_ref, bf16[2048,3072]{1,0:T(8,128)(2,1)} %get-tuple-element.56.q_ref.k_ref.v_ref, ...), custom_call_target="tpu_custom_call" | custom-call | flops 40265318400 | bytes 31457280 | tf_op jit(solution)/shard_map/attend/pallas_call | solution.py:625
  398.6 3.3 copy-done.2
  401.9 20.1 %attend_other.1 = (bf16[2048,1024]{1,0:T(8,128)(2,1)S(1)}, f32[2048,1024]{1,0:T(8,128)}) custom-call(s32[130]{0:T(256)S(1)} %pad_add_fusion.meta, bf16[2048,3072]{1,0:T(8,128)(2,1)} %get-tuple-element.56.q_ref.k_ref.v_ref, bf16[16,2,2,64,512]{4,3,2,1,0:T(8,128)(2,1)} %bitcast.8.pk_ref.pv_ref, bf16[16,2,2,64,512]{4,3,2,1,0:T(8,128)(2,1)} %bitcast.8.pk_ref.pv_ref, ...), custom_call_target="tpu_custom_call" | custom-call | flops 2147483648 | bytes 31457280 | tf_op jit(solution)/shard_map/attend_other/pallas_call | solution.py:648
  422.1 2.0 copy-done.10
  424.1 2.2 copy-done.9
  426.3 2.2 copy-done.11
  428.5 7.6 mix.1
  436.1 3.4 copy-done.1
  439.5 1.9 copy-done.17
  441.4 134.7 %ffn.1 = (bf16[2048,1024]{1,0:T(8,128)(2,1)}, f32[2048,1024]{1,0:T(8,128)}, bf16[1024,8448]{1,0:T(8,128)(2,1)}) custom-call(bf16[2048,1024]{1,0:T(8,128)(2,1)} %copy-done.17, bf16[2048,1024]{1,0:T(8,128)(2,1)} %bitcast.9.g_ref, bf16[1024,9472]{1,0:T(8,128)(2,1)} %all-gather.2.cloned.1.call-done.w_ref.wg_ref.wu_ref.wd_ref, ...), custom_call_target="tpu_custom_call" | custom-call | flops 106300440576 | bytes 62914560 | tf_op jit(solution)/shard_map/ffn/pallas_call | solution.py:792
  576.1 19.0 %unmix.1 = (bf16[2048,1024]{1,0:T(8,128)(2,1)S(1)}, f32[2048,1024]{1,0:T(8,128)}, bf16[2048,1024]{1,0:T(8,128)(2,1)S(1)}, bf16[2048,1024]{1,0:T(8,128)(2,1)S(1)}, f32[1,1024]{1,0:T(1,128)S(1)}) custom-call(f32[2048,1024]{1,0:T(8,128)} %copy-done.1, f32[2048,1024]{1,0:T(8,128)} %get-tuple-element.66.gn_ref, bf16[2048,1024]{1,0:T(8,128)(2,1)} %get-tuple-element.67.ffn_ref, ...), custom_call_target="tpu_custom_call" | custom-call | flops 4294967296 | bytes 48234496 | tf_op jit(solution)/shard_map/unmix/pallas_call | solution.py:833
  595.1 2.3 copy-done.4
  597.5 2.3 copy-done.15
  599.8 2.3 copy-done.16
  602.6 8.7 all-to-all-start.2
  611.3 1.6 copy-done.20
  612.9 111.8 %attend_back.1 = (bf16[2048,1024]{1,0:T(8,128)(2,1)}, bf16[2048,1024]{1,0:T(8,128)(2,1)}, bf16[2048,1024]{1,0:T(8,128)(2,1)}) custom-call(s32[130]{0:T(256)S(1)} %pad_add_fusion.meta, bf16[2048,3072]{1,0:T(8,128)(2,1)} %get-tuple-element.56.q_ref.k_ref.v_ref, bf16[2048,3072]{1,0:T(8,128)(2,1)} %get-tuple-element.56.q_ref.k_ref.v_ref, ...), custom_call_target="tpu_custom_call" | custom-call | flops 47815065600 | bytes 41943040 | tf_op jit(solution)/shard_map/attend_back/pallas_call | solution.py:673
  724.6 39.8 %reduce-scatter.2.cloned.1.call-done = bf16[64,8448]{1,0:T(8,128)(2,1)} async-done(((bf16[1024,8448]{1,0:T(8,128)(2,1)}), bf16[64,8448]{1,0:T(8,128)(2,1)}) %reduce-scatter.2.cloned.1.call-update) | async-done | bytes 1081360 | tf_op jit(solution)/shard_map/reduce_scatter | solution.py:1379
  764.5 87.4 %finish.1 = (bf16[2048,1024]{1,0:T(8,128)(2,1)}, f32[2,1024]{1,0:T(2,128)}, f32[64,2048]{1,0:T(8,128)}) custom-call(bf16[2048,1024]{1,0:T(8,128)(2,1)} %bitcast.31, f32[2048,1024]{1,0:T(8,128)} %get-tuple-element.74.gm_ref, bf16[2048,1024]{1,0:T(8,128)(2,1)} %copy-done.22, bf16[2048,1024]{1,0:T(8,128)(2,1)} %copy-done.10, bf16[2048,1024]{1,0:T(8,128)(2,1)} %copy-done.15, ...), custom_call_target="tpu_custom_call" | custom-call | flops 30064771072 | bytes 83886080 | tf_op jit(solution)/shard_map/finish/pallas_call | solution.py:1096
  851.9 5.7 all-to-all-start.3
  858.5 0.8 reshape.87
  859.3 2.0 collective-permute-start
  861.9 0.8 slice_bitcast_fusion.3
  862.7 47.3 %collective-permute-done = bf16[64,3,1408]{2,0,1:T(8,128)(2,1)S(1)} collective-permute-done((bf16[64,3,1408]{2,0,1:T(8,128)(2,1)S(1)}, bf16[64,3,1408]{2,0,1:T(8,128)(2,1)S(1)}, u32[]{:S(2)}, u32[]{:S(2)}) %collective-permute-start) | collective-permute-done | bytes 540704 | tf_op jit(solution)/shard_map/ppermute | solution.py:1329
  910.2 1.0 slice_bitcast_fusion
  911.2 6.6 convert_element_type.21
  917.8 4.6 copy.41
  (69 shorter events, 7.0 us)
Async XLA Ops:
  7.2 416.9 %all-gather.2.cloned.1.call-start = ((), (), s32[]{:S(2)}) async-start(), calls=%async_computation.5 | async-start | bytes 20611072 | tf_op jit(solution)/shard_map/all_gather | solution.py:1357
  11.7 2.2 copy-start.3
  13.9 1.6 copy-start.12
  15.5 1.6 copy-start.13
  159.0 2.0 copy-start.5
  161.0 2.0 copy-start.7
  163.0 1.3 copy-start.18
  165.8 2.2 copy-start.6
  174.4 2.0 copy-start
  176.4 5.1 copy-start.28
  176.4 5.7 copy-start.26
  176.4 5.7 copy-start.27
  176.4 143.3 %all-to-all-start = ((bf16[32,128,512]{2,1,0:T(8,128)(2,1)}), bf16[32,128,512]{2,1,0:T(8,128)(2,1)}, u32[]{:S(2)}, u32[]{:S(2)}) async-start(bf16[32,128,512]{2,1,0:T(8,128)(2,1)} %copy-done), calls=%async_computation | async-start | bytes 8388608 | tf_op jit(solution)/shard_map/all_to_all | solution.py:1364
  183.4 0.6 copy-start.14
  184.0 2.3 copy-start.8
  209.6 2.0 copy-start.22
  319.7 121.7 %all-to-all-start.1 = ((bf16[2,1024,1024]{2,1,0:T(8,128)(2,1)}), bf16[2,1024,1024]{2,1,0:T(8,128)(2,1)}, u32[]{:S(2)}, u32[]{:S(2)}) async-start(bf16[2,1024,1024]{2,1,0:T(8,128)(2,1)} %param.35), calls=%async_computation.1 | async-start | bytes 8388608 | tf_op jit(solution)/shard_map/all_to_all | solution.py:1356
  325.5 439.0 %reduce-scatter.2.cloned.1.call-start = ((), (), s32[]{:S(2)}) async-start(), calls=%async_computation.6 | async-start | bytes 18382848 | tf_op jit(solution)/shard_map/reduce_scatter | solution.py:1379
  325.7 1.6 copy-start.19
  398.6 3.3 copy-start.2
  422.1 2.0 copy-start.10
  424.1 2.2 copy-start.9
  426.3 2.2 copy-start.11
  436.1 3.4 copy-start.1
  439.5 1.9 copy-start.17
  595.1 2.3 copy-start.4
  597.5 2.3 copy-start.15
  599.8 2.3 copy-start.16
  602.0 0.6 copy-start.21
  602.6 122.0 %all-to-all-start.2 = ((bf16[2,1024,1024]{2,1,0:T(8,128)(2,1)}), bf16[2,1024,1024]{2,1,0:T(8,128)(2,1)}, u32[]{:S(2)}, u32[]{:S(2)}) async-start(bf16[2,1024,1024]{2,1,0:T(8,128)(2,1)} %bitcast.29), calls=%async_computation.2 | async-start | bytes 8388608 | tf_op jit(solution)/shard_map/all_to_all | solution.py:1383
  611.3 1.6 copy-start.20
  851.9 5.8 copy-start.23
  851.9 59.2 %all-to-all-start.3 = ((bf16[2,1024,1024]{2,1,0:T(8,128)(2,1)}), bf16[2,1024,1024]{2,1,0:T(8,128)(2,1)}, u32[]{:S(2)}, u32[]{:S(2)}) async-start(bf16[2,1024,1024]{2,1,0:T(8,128)(2,1)} %bitcast.35), calls=%async_computation.4 | async-start | bytes 8388608 | tf_op jit(solution)/shard_map/all_to_all | solution.py:1389
  857.7 3.6 copy-start.25
  857.7 4.2 copy-start.24
  859.3 50.8 %collective-permute-start = (bf16[64,3,1408]{2,0,1:T(8,128)(2,1)S(1)}, bf16[64,3,1408]{2,0,1:T(8,128)(2,1)S(1)}, u32[]{:S(2)}, u32[]{:S(2)}) collective-permute-start(bf16[64,3,1408]{2,0,1:T(8,128)(2,1)S(1)} %slice.69), channel_id=1, source_target_pairs={{0,1},{1,0},{2,3},{3,2},{4,5},{5,4},{6,7},{7,6},{8,9},{9,8},{10,11... | collective-permute-start | bytes 1622024 | tf_op jit(solution)/shard_map/ppermute | solution.py:1329
Sparse Core Ops, SparseCore 0:
  164.5 184.5 all-gather.1
  576.2 188.1 reduce-scatter.1

commit v4 on v3

--- a/solution.py
+++ b/solution.py
@@ -740,69 +740,175 @@
     )(x, context, gain, weights)
 
 
-def ffn_kernel(n_ref, g_ref, wg_ref, wu_ref, wd_ref, out_ref, gn_ref, grads_ref, acc, ag, au, ad):
+RING = 8
+RIGHT = RING // 2
+LEFT = RING - 1 - RIGHT
+
+
+def ring_place(p):
+    y = p // 4
+    return (p + y * (7 - 2 * p)) * 2 + y
+
+
+def meet(devices, me, spot):
+    barrier = pltpu.get_barrier_semaphore()
+    for d in range(1, devices):
+        pl.semaphore_signal(
+            barrier, inc=1, device_id=((me + d) % devices, spot), device_id_type=pl.DeviceIdType.MESH
+        )
+    pl.semaphore_signal(barrier, inc=1, device_id=(me, 1 - spot), device_id_type=pl.DeviceIdType.MESH)
+    pl.semaphore_wait(barrier, devices)
+
+
+def remote(src, dst, send, recv, device):
+    return pltpu.make_async_remote_copy(
+        src_ref=src, dst_ref=dst, send_sem=send, recv_sem=recv, device_id=device, device_id_type=pl.DeviceIdType.MESH
+    )
+
+
+def ffn_kernel(
+    n_ref, g_ref, wg0, wg1, wu0, wu1, wd0, wd1, out_ref, gn_ref, share_ref,
+    acc, ag, au, ad, part, got, passed, land, pair_send, pair_recv, x_send, x_recv, *, devices,
+):
     tile = pl.program_id(0)
-    last = pl.num_programs(0) - 1
+    tiles = pl.num_programs(0)
+    me = lax.axis_index("dp")
+    spot = lax.axis_index("tensor")
+    core = me % 2
+    pair = (me + 1 - 2 * core, spot)
+    peer = (me, 1 - spot)
+    side = HT // 2
 
     @pl.when(tile == 0)
     def _():
+        barrier = pltpu.get_barrier_semaphore()
+        for device in (pair, peer):
+            pl.semaphore_signal(barrier, inc=1, device_id=device, device_id_type=pl.DeviceIdType.MESH)
+        pl.semaphore_wait(barrier, 2)
         acc[...] = jnp.zeros_like(acc)
         gn_ref[...] = jnp.zeros_like(gn_ref)
+
+    def to_pair(k):
+        return remote(part.at[k % 2, :, 1 - core], got.at[k], pair_send.at[k], pair_recv.at[k], pair)
+
+    def to_peer(k):
+        return remote(passed.at[k % 2], land.at[k], x_send.at[k], x_recv.at[k], peer)
+
+    def join(k):
+        to_pair(k).wait()
+
+        @pl.when(k >= 2)
+        def _():
+            to_peer(k - 2).wait_send()
+
+        def one(b, carry):
+            total = got[k, b].astype(F32) + part[k % 2, b, core].astype(F32)
+            low = total.astype(BF16)
+            for m in range(3):
+                passed[k % 2, b, :, m * side : (m + 1) * side] = low[:, m * HT + side : (m + 1) * HT]
+                got[k, b, :, m * side : (m + 1) * side] = low[:, m * HT : m * HT + side]
+            return carry
+
+        lax.fori_loop(0, part.shape[1], one, 0)
+        to_peer(k).start()
+
+    def settle(k):
+        to_peer(k).wait_recv()
+
+        def one(b, carry):
+            total = got[k, b, :, : 3 * side].astype(F32) + land[k, b].astype(F32)
+            rs = pl.ds(pl.multiple_of(b * part.shape[3], part.shape[3]), part.shape[3])
+            share_ref[rs, pl.ds(pl.multiple_of(k * 3 * side, 3 * side), 3 * side)] = total.astype(BF16)
+            return carry
+
+        lax.fori_loop(0, part.shape[1], one, 0)
 
     ag[...] = jnp.zeros_like(ag)
     au[...] = jnp.zeros_like(au)
     ad[...] = jnp.zeros_like(ad)
+    wg = jnp.concatenate([wg0[...], wg1[...]], axis=1)
+    wu = jnp.concatenate([wu0[...], wu1[...]], axis=1)
+    wd = jnp.concatenate([wd0[...], wd1[...]], axis=1)
 
     def chunk(r, carry):
         rs = pl.ds(pl.multiple_of(r * ROWS, ROWS), ROWS)
         rows = n_ref[rs, :]
         cotangent = g_ref[rs, :]
-        gate = mm(rows, wg_ref[...])
-        up = mm(rows, wu_ref[...])
-        grad_hidden = mm(cotangent, wd_ref[...])
+        gate = mm(rows, wg)
+        up = mm(rows, wu)
+        grad_hidden = mm(cotangent, wd)
         sigma = 1.0 / (1.0 + jnp.exp(-gate))
         silu = gate * sigma
         hidden = (silu * up).astype(BF16)
         grad_gate = (grad_hidden * up * (sigma * (1.0 + gate * (1.0 - sigma)))).astype(BF16)
         grad_up = (grad_hidden * silu).astype(BF16)
-        acc[rs, :] += mm(hidden, wd_ref[...], NT)
-        gn_ref[rs, :] += mm(grad_gate, wg_ref[...], NT) + mm(grad_up, wu_ref[...], NT)
+        acc[rs, :] += mm(hidden, wd, NT)
+        gn_ref[rs, :] += mm(grad_gate, wg, NT) + mm(grad_up, wu, NT)
         ag[...] += mm(rows, grad_gate, TN)
         au[...] += mm(rows, grad_up, TN)
         ad[...] += mm(cotangent, hidden, TN)
         return carry
 
     lax.fori_loop(0, L // ROWS, chunk, 0)
-    grads_ref[:, :HT] = ag[...].astype(BF16)
-    grads_ref[:, HT : 2 * HT] = au[...].astype(BF16)
-    grads_ref[:, 2 * HT :] = ad[...].astype(BF16)
-
-    @pl.when(tile == last)
+    for m, held in enumerate((ag, au, ad)):
+        part[tile % 2, :, :, :, m * HT : (m + 1) * HT] = held[...].astype(BF16).reshape(part.shape[1:4] + (HT,))
+    to_pair(tile).start()
+
+    @pl.when(tile > 0)
     def _():
+        join(tile - 1)
+
+    @pl.when(tile > 1)
+    def _():
+        settle(tile - 2)
+
+    @pl.when(tile == tiles - 1)
+    def _():
+        join(tile)
+        settle(tile - 1)
         out_ref[...] = acc[...].astype(BF16)
-
-
-def ffn(normed, cotangent, weights, width, hidden):
+        settle(tile)
+        to_peer(tile - 1).wait_send()
+        to_peer(tile).wait_send()
+
+
+def ffn(normed, cotangent, weights, width, hidden, devices):
     once = pl.Buffered(1)
     tiles = hidden // HT
-    lead = width // HT
-    part = lambda k: pl.BlockSpec((width, HT), lambda j: (0, lead + k * tiles + j))
+    side = HT // 2
+    rows = width // devices
+    chips = devices // 2
+    lead = width // side
+    part = lambda k: pl.BlockSpec((width, side), lambda j: (0, lead + k * tiles + j))
     whole = pl.BlockSpec((L, width), lambda j: (0, 0), pipeline_mode=once)
-    grad = pl.BlockSpec((width, 3 * HT), lambda j: (0, j))
+    dma = pltpu.SemaphoreType.DMA
     return pl.pallas_call(
-        ffn_kernel,
+        functools.partial(ffn_kernel, devices=devices),
         grid=(tiles,),
-        in_specs=[whole, whole, part(0), part(1), part(2)],
-        out_specs=[whole, whole, grad],
-        out_shape=[jax.ShapeDtypeStruct((L, width), BF16), jax.ShapeDtypeStruct((L, width), F32)]
-        + [jax.ShapeDtypeStruct((width, 3 * hidden), BF16)],
-        scratch_shapes=[pltpu.VMEM((L, width), F32)] + [pltpu.VMEM((width, HT), F32)] * 3,
-        compiler_params=pltpu.CompilerParams(vmem_limit_bytes=56 * MIB),
+        in_specs=[whole, whole] + [part(k) for k in range(6)],
+        out_specs=[
+            whole, whole, pl.BlockSpec((width // 2, 3 * hidden // 2), lambda j: (0, 0), pipeline_mode=once)
+        ],
+        out_shape=[
+            jax.ShapeDtypeStruct((L, width), BF16),
+            jax.ShapeDtypeStruct((L, width), F32),
+            jax.ShapeDtypeStruct((width // 2, 3 * hidden // 2), BF16),
+        ],
+        scratch_shapes=[pltpu.VMEM((L, width), F32)]
+        + [pltpu.VMEM((width, HT), F32)] * 3
+        + [
+            pltpu.VMEM((2, chips, 2, rows, 3 * HT), BF16),
+            pltpu.VMEM((tiles, chips, rows, 3 * HT), BF16),
+            pltpu.VMEM((2, chips, rows, 3 * side), BF16),
+            pltpu.VMEM((tiles, chips, rows, 3 * side), BF16),
+            dma((tiles,)), dma((tiles,)), dma((tiles,)), dma((tiles,)),
+        ],
+        compiler_params=pltpu.CompilerParams(collective_id=2, has_side_effects=True, vmem_limit_bytes=61 * MIB),
         cost_estimate=pl.CostEstimate(
             flops=18 * L * width * hidden, bytes_accessed=60 * MIB, transcendentals=L * hidden
         ),
         name="ffn",
-    )(normed, cotangent, weights, weights, weights)
+    )(normed, cotangent, *([weights] * 6))
 
 
 def unmix_kernel(mixed_ref, gn_ref, ffn_ref, g_ref, gain_ref, w_ref, out_ref, gm_ref, br_ref, gc_ref, gg_ref):
@@ -848,32 +954,6 @@
     )(mixed, grad_normed, ffn_out, cotangent, gain, weights)
 
 
-RING = 8
-RIGHT = RING // 2
-LEFT = RING - 1 - RIGHT
-
-
-def ring_place(p):
-    y = p // 4
-    return (p + y * (7 - 2 * p)) * 2 + y
-
-
-def meet(devices, me, spot):
-    barrier = pltpu.get_barrier_semaphore()
-    for d in range(1, devices):
-        pl.semaphore_signal(
-            barrier, inc=1, device_id=((me + d) % devices, spot), device_id_type=pl.DeviceIdType.MESH
-        )
-    pl.semaphore_signal(barrier, inc=1, device_id=(me, 1 - spot), device_id_type=pl.DeviceIdType.MESH)
-    pl.semaphore_wait(barrier, devices)
-
-
-def remote(src, dst, send, recv, device):
-    return pltpu.make_async_remote_copy(
-        src_ref=src, dst_ref=dst, send_sem=send, recv_sem=recv, device_id=device, device_id_type=pl.DeviceIdType.MESH
-    )
-
-
 FT = 256
 
 
@@ -882,7 +962,7 @@
     gt_ref, sums_ref, share_ref,
     n_buf, ctx_buf, br_buf, dq_buf, dk_buf, dv_buf, w_buf, x_buf, gm_buf, gt_buf,
     part, got, land, across, gains, gain_land,
-    load_sem, x_sem, gm_sem, gt_sem, pair_send, pair_recv, ring_send, ring_recv, x_send, x_recv, g_send, g_recv,
+    load_sem, x_sem, gm_sem, gt_sem, gt_recv, pair_send, pair_recv, ring_send, ring_recv, x_send, x_recv, g_send, g_recv,
     *, devices,
 ):
     me = lax.axis_index("dp")
@@ -913,11 +993,22 @@
             pltpu.make_async_copy(gm_ref.at[rs, :], gm_buf.at[slot], gm_sem.at[slot]),
         ]
 
-    def tile_out(t, slot):
-        rs = pl.ds(pl.multiple_of(t * FT, FT), FT)
-        return pltpu.make_async_copy(gt_buf.at[slot], gt_ref.at[rs, :], gt_sem.at[slot])
-
-    for copy in tile_in(0, 0):
+    held = L // FT // 2
+
+    def give(k, slot):
+        rs = pl.ds(pl.multiple_of(k * FT, FT), FT)
+        return remote(
+            gt_buf.at[slot], gt_ref.at[spot, rs, :], gt_sem.at[slot], gt_recv.at[k], (me, 1 - spot)
+        )
+
+    def keep(k, slot):
+        rs = pl.ds(pl.multiple_of(k * FT, FT), FT)
+        return pltpu.make_async_copy(gt_buf.at[slot], gt_ref.at[spot, rs, :], gt_sem.at[slot])
+
+    def tile_of(k):
+        return (k + held * (1 - spot)) % (2 * held)
+
+    for copy in tile_in(tile_of(0), 0):
         copy.start()
 
     pair = (me + 1 - 2 * core, spot)
@@ -969,7 +1060,7 @@
         if more:
             hop(direction, s + 1).start()
 
-    def finish_rows(t, slot):
+    def finish_rows(t, slot, k):
         for copy in tile_in(t, slot):
             copy.wait()
         rs = pl.ds(pl.multiple_of(t * FT, FT), FT)
@@ -981,7 +1072,7 @@
         unit = values * scale
         inner = grad * gain_ref[...]
         back = scale * (inner - unit * jnp.mean(inner * unit, axis=1, keepdims=True))
-        gt_buf[slot] = (gm_buf[slot] + back).astype(BF16)
+        gt_buf[k] = (gm_buf[slot] + back).astype(BF16)
         gains[:1, :] += jnp.sum(grad * unit, axis=0, keepdims=True)
 
     for i in (0, 1):
@@ -1008,28 +1099,32 @@
 
     def sweep(i, carry):
         for slot in (0, 1):
-            t = 2 * i + slot
+            k = 2 * i + slot
             if slot == 0:
-                for copy in tile_in(t + 1, 1):
+                for copy in tile_in(tile_of(k + 1), 1):
                     copy.start()
             else:
 
                 @pl.when(i < 3)
                 def _():
-                    for copy in tile_in(t + 1, 0):
+                    for copy in tile_in(tile_of(k + 1), 0):
                         copy.start()
 
-            @pl.when(i > 0)
+            finish_rows(tile_of(k), slot, k)
+
+            @pl.when(i < 2)
             def _():
-                tile_out(t - 2, slot).wait()
-
-            finish_rows(t, slot)
-            tile_out(t, slot).start()
+                give(k, k).start()
+
+            @pl.when(i >= 2)
+            def _():
+                keep(k - held, k).start()
+
         advance(0, i + 2)
         advance(1, i)
         return carry
 
-    lax.fori_loop(0, L // FT // 2, sweep, 0)
+    lax.fori_loop(0, held, sweep, 0)
 
     partners = [
         (me + 1 - 2 * core, spot),
@@ -1082,8 +1177,9 @@
     for s in range(RING - 1):
         hop(0, s).wait_send()
         hop(1, s).wait_send()
-    tile_out(L // FT - 2, 0).wait()
-    tile_out(L // FT - 1, 1).wait()
+    for k in range(held):
+        give(k, k).wait()
+        keep(k, k + held).wait()
 
 
 def finish(x, grad_mixed, normed, context, branch, dq, dk, dv, weights, gain, gain_two_part, devices):
@@ -1098,19 +1194,19 @@
         in_specs=[anywhere] * 9 + [vmem] * 2,
         out_specs=[anywhere, vmem, vmem],
         out_shape=[
-            jax.ShapeDtypeStruct((L, width), BF16),
+            jax.ShapeDtypeStruct((2, L // 2, width), BF16),
             jax.ShapeDtypeStruct((2, width), F32),
             jax.ShapeDtypeStruct((rows, 2 * width), F32),
         ],
         scratch_shapes=[
             whole, whole, whole, whole, whole, whole, pltpu.VMEM((width, 3 * width), BF16),
-            pltpu.VMEM((2, FT, width), BF16), pltpu.VMEM((2, FT, width), F32), pltpu.VMEM((2, FT, width), BF16),
+            pltpu.VMEM((2, FT, width), BF16), pltpu.VMEM((2, FT, width), F32), pltpu.VMEM((L // FT, FT, width), BF16),
             pltpu.VMEM((RING, 2, rows, 4 * width), BF16),
             pltpu.VMEM((RING, rows, 4 * width), BF16),
             pltpu.VMEM((2, RING - 1, rows, 2 * width), BF16),
             pltpu.VMEM((rows, 2 * width), BF16),
             pltpu.VMEM((2, width), F32), pltpu.VMEM((5, 2, width), F32),
-            dma((7,)), dma((2,)), dma((2,)), dma((2,)), dma((4,)), dma((4,)),
+            dma((7,)), dma((2,)), dma((2,)), dma((2 * (L // FT // 2),)), dma((L // FT // 2,)), dma((4,)), dma((4,)),
             dma((2, RING - 1)), dma((2, RING - 1)), dma((4,)), dma((4,)), dma((5,)), dma((5,)),
         ],
         compiler_params=pltpu.CompilerParams(collective_id=1, has_side_effects=True, vmem_limit_bytes=60 * MIB),
@@ -1353,7 +1449,9 @@
         tokens, cache_keys, cache_values, small, extra, big, devices
     )
     x = x.reshape(L, width)
-    cotangent = exchange(grad_out).reshape(L, width)
+    theirs = swap(lax.dynamic_index_in_dim(grad_out, 1 - spot, 0, keepdims=False))
+    mine = lax.dynamic_index_in_dim(grad_out, spot, 0, keepdims=False)
+    cotangent = jnp.where(spot == 0, jnp.concatenate([mine, theirs], 0), jnp.concatenate([theirs, mine], 0))
     second_all = lax.all_gather(second_rows, "dp", axis=0, tiled=True)
 
     tail = lax.optimization_barrier(first_all[:, 3 * width :])
@@ -1374,24 +1472,25 @@
     partial, partial_lse = attend(meta, qkv, own_k, own_v)
     context, lse = attend_other(meta, qkv, fetched, partial, partial_lse)
     mixed, normed_two = mix(x, context, gain_two, second_all)
-    ffn_out, grad_normed_two, ffn_grads = ffn(normed_two, cotangent, second_all, width, hidden)
-    share = functools.partial(lax.psum_scatter, axis_name="dp", scatter_dimension=0, tiled=True)
-    ffn_share = share(ffn_grads)
+    ffn_out, grad_normed_two, ffn_grads = ffn(normed_two, cotangent, second_all, width, hidden, devices)
+    ffn_share = lax.psum_scatter(
+        ffn_grads, "dp", scatter_dimension=0, tiled=True,
+        axis_index_groups=[list(range(c, devices, 2)) for c in range(2)],
+    )
     out, grad_mixed, branch, grad_context, gain_part_two = unmix(
         mixed, grad_normed_two, ffn_out, cotangent, gain_two, second_all
     )
     out = exchange(out.reshape(2, shard_len, width))
     dq, dk, dv = attend_back(meta, qkv, own_k, own_v, fetched, grad_context, context, lse)
-    dq, out, ffn_share = lax.optimization_barrier((dq, out, ffn_share))
+    dq, out = lax.optimization_barrier((dq, out))
     grad_tokens, gain_sums, attn_share = finish(
         x, grad_mixed, normed, context, branch, dq, dk, dv, first_all, gain_one, gain_part_two, devices
     )
-    grad_tokens = exchange(grad_tokens.reshape(2, shard_len, width)).astype(F32)
+    grad_tokens = grad_tokens.astype(F32)
     g_out, g_value, g_key, g_query = jnp.split(attn_share, 4, axis=1)
-    pieces = ffn_share.reshape(rows_held, hidden // HT, 3, HT).swapaxes(1, 2).reshape(rows_held, 3, hidden)
-    got = swap(pieces[:, :, hidden_held:])
-    total = pieces[:, :, :hidden_held].astype(F32) + got.astype(F32)
-    g_gate, g_up, g_down = total[:, 0], total[:, 1], total[:, 2]
+    pieces = ffn_share.reshape(rows_held, hidden // HT, 3, HT // 2).swapaxes(1, 2)
+    pieces = pieces.reshape(rows_held, 3, hidden_held).astype(F32)
+    g_gate, g_up, g_down = pieces[:, 0], pieces[:, 1], pieces[:, 2]
     return (
         out, grad_tokens, gain_sums[0], g_query, g_key, g_value, g_out.T, gain_sums[1], g_gate, g_up, g_down.T,
     )

time: 934 us -> 812 us (0.87); the launches traced: 930 us -> 797 us
  waiting for transfers between devices: 195 us -> 29.6 us
  Pallas kernels: 623 us -> 665 us
  starting transfers between devices: 27.5 us -> 12.5 us
    all_to_all x1, waiting for transfers between devices: 108 us -> 22.7 us  [sequence_body(): lax.all_to_all(sent, ('dp', 'tensor'), split_axis=0, concat_axis=0, tiled...]
    ppermute x1, waiting for transfers between devices: 47.3 us -> 0.01 us  [swap(): return lax.ppermute(values, 'tensor', [(0, 1), (1, 0)])]
    reduce_scatter x1, waiting for transfers between devices: 39.8 us -> 0.01 us  [sequence_body(): lax.psum_scatter(ffn_grads, 'dp', scatter_dimension=0, tiled=True, axis_i...]
    pallas_call x1, Pallas kernels: 135 us -> 162 us  [ffn(): pl.pallas_call(functools.partial(ffn_kernel, devices=devices), grid=(tile...]
    pallas_call x1, Pallas kernels: 87.4 us -> 103 us  [finish(): pl.pallas_call(functools.partial(finish_kernel, devices=devices), in_spec...]
    all_to_all x2 -> x0, starting transfers between devices: 11.5 us -> none  [the longest x1 5.74 us: sequence_body(): grad_tokens = exchange(grad_tokens.reshape(2, shard_len, width)).astype(F32)]
  transfers between devices with their start and end apart: 7 -> 5, of which waited for: 3 -> 2; matrix products, arithmetic and copies ran while one was open for 1% -> 3% of each run, Pallas kernels for 28% -> 44%
where the time goes in v4:
time: 812 us; the launch traced here: 797 us
  Pallas kernels  665 us (82%)
  local copies, waits for them, and re-layouts  60.3 us (7%)
  waiting for transfers between devices  29.6 us (4%)
  other arithmetic  15.1 us (2%)
  between operations  14.5 us (2%)
  starting transfers between devices  12.5 us (2%)
    pallas_call x1, Pallas kernels, ffn(): pl.pallas_call(functools.partial(ffn_kernel, devices=devices), grid=(tile...  162 us
    pallas_call x1, Pallas kernels, spread(): pl.pallas_call(spread_kernel, in_specs=[anywhere, anywhere, anywhere, vme...  142 us
    pallas_call x1, Pallas kernels, attend_back(): pl.pallas_call(functools.partial(attend_back_kernel, pair=pair), grid_spe...  112 us
    pallas_call x1, Pallas kernels, finish(): pl.pallas_call(functools.partial(finish_kernel, devices=devices), in_spec...  103 us
    pallas_call x1, Pallas kernels, attend(): pl.pallas_call(functools.partial(attend_kernel, pair=pair), grid_spec=plt...  71.3 us
    unnamed x59, local copies, waits for them, and re-layouts  47.2 us
    pallas_call x1, Pallas kernels, project(): pl.pallas_call(project_kernel, grid=(L // ROWS,), in_specs=[row(width), p...  23.4 us
    all_to_all x1, waiting for transfers between devices, sequence_body(): lax.all_to_all(sent, ('dp', 'tensor'), split_axis=0, concat_axis=0, tiled...  22.7 us
  transfers between devices with their start and end apart: 5, of which 2 were waited for; matrix products, arithmetic and copies ran while one was open for 3% of the time, Pallas kernels for 44%

profile of v4, /device:TPU:0, one launch (start us, length us, event | category | flops | bytes accessed | tf_op | source)
XLA Modules:
  0.0 797.1 jit_solution(67537481462678185)
XLA Ops:
  8.0 0.8 copy.37
  8.8 0.8 copy.38
  9.6 0.9 pad_maximum_fusion.1.small_ref
  10.6 1.1 pad_maximum_fusion.big_ref
  11.8 2.2 copy-done.3
  13.9 1.6 copy-done.12
  15.5 1.6 copy-done.13
  17.1 141.9 %spread.1 = (bf16[2,1024,1024]{2,1,0:T(8,128)(2,1)S(1)}, bf16[2,1024,512]{2,1,0:T(8,128)(2,1)S(1)}, bf16[2,1024,512]{2,1,0:T(8,128)(2,1)S(1)}, bf16[16,2,2,64,51...) custom-call(bf16[2,1024,1024]{2,1,0:T(8,128)(2,1)S(1)} %copy-done.3, ...), custom_call_target="tpu_custom_call" | custom-call | bytes 314572800 | tf_op jit(solution)/shard_map/spread/pallas_call | solution.py:1399
  159.0 2.0 copy-done.5
  161.0 2.0 copy-done.7
  163.0 1.3 copy-done.18
  164.4 1.0 slice.46
  165.8 2.2 copy-done.6
  168.0 6.4 pick_rows.1
  174.4 2.1 copy-done
  176.5 5.1 all-to-all-start
  181.7 4.7 dynamic-slice_bitcast_fusion.1
  186.4 1.7 collective-permute-start
  189.0 0.7 pad_add_fusion.meta
  190.0 2.2 copy-done.8
  192.2 23.4 %project.1 = (bf16[2048,1024]{1,0:T(8,128)(2,1)S(1)}, bf16[2048,3072]{1,0:T(8,128)(2,1)}) custom-call(bf16[2048,1024]{1,0:T(8,128)(2,1)S(1)} %bitcast.34, f32[1,1024]{1,0:T(1,128)S(1)} %get-tuple-element.95.gain_ref, bf16[1024,3200]{1,0:T(8,128)(2,1)} %get-tuple-element.54.w_ref), custom_call_target="tpu_custom_call" | custom-call | flops 12884901888 | bytes 27262976 | tf_op jit(solution)/shard_map/project/pallas_call | solution.py:709
  215.6 2.0 copy-done.22
  217.7 71.3 %attend.1 = (f32[2048,1024]{1,0:T(8,128)S(1)}, f32[2048,1024]{1,0:T(8,128)}) custom-call(s32[130]{0:T(256)S(1)} %pad_add_fusion.meta, bf16[2048,3072]{1,0:T(8,128)(2,1)} %get-tuple-element.55.q_ref.k_ref.v_ref, bf16[2048,3072]{1,0:T(8,128)(2,1)} %get-tuple-element.55.q_ref.k_ref.v_ref, bf16[2048,3072]{1,0:T(8,128)(2,1)} %get-tuple-element.55.q_ref.k_ref.v_ref, ...), custom_call_target="tpu_custom_call" | custom-call | flops 40265318400 | bytes 31457280 | tf_op jit(solution)/shard_map/attend/pallas_call | solution.py:625
  289.0 3.3 copy-done.2
  292.2 4.9 maximum_select_fusion.g_ref
  297.1 22.7 %all-to-all-done = bf16[32,128,512]{2,1,0:T(8,128)(2,1)} async-done(((bf16[32,128,512]{2,1,0:T(8,128)(2,1)}), bf16[32,128,512]{2,1,0:T(8,128)(2,1)}, u32[]{:S(2)}, u32[]{:S(2)}) %all-to-all-start) | async-done | bytes 4194336 | tf_op jit(solution)/shard_map/all_to_all | solution.py:1462
  319.8 20.3 %attend_other.1 = (bf16[2048,1024]{1,0:T(8,128)(2,1)S(1)}, f32[2048,1024]{1,0:T(8,128)}) custom-call(s32[130]{0:T(256)S(1)} %pad_add_fusion.meta, bf16[2048,3072]{1,0:T(8,128)(2,1)} %get-tuple-element.55.q_ref.k_ref.v_ref, bf16[16,2,2,64,512]{4,3,2,1,0:T(8,128)(2,1)} %bitcast.8.pk_ref.pv_ref, bf16[16,2,2,64,512]{4,3,2,1,0:T(8,128)(2,1)} %bitcast.8.pk_ref.pv_ref, ...), custom_call_target="tpu_custom_call" | custom-call | flops 2147483648 | bytes 31457280 | tf_op jit(solution)/shard_map/attend_other/pallas_call | solution.py:648
  340.1 2.1 copy-done.10
  342.2 6.9 all-gather.2.cloned.1.call-done.w_ref.wg0.wg1.wu0.wu1.wd0.wd1
  349.1 2.2 copy-done.9
  351.3 2.2 copy-done.11
  353.5 7.6 mix.1
  361.1 3.4 copy-done.1
  364.5 2.0 copy-done.17
  366.5 161.7 %ffn.1 = (bf16[2048,1024]{1,0:T(8,128)(2,1)}, f32[2048,1024]{1,0:T(8,128)}, bf16[512,4224]{1,0:T(8,128)(2,1)}) custom-call(bf16[2048,1024]{1,0:T(8,128)(2,1)} %copy-done.17, bf16[2048,1024]{1,0:T(8,128)(2,1)} %maximum_select_fusion.g_ref, bf16[1024,9472]{1,0:T(8,128)(2,1)} %all-gather.2.cloned.1.call-done.w_ref.wg0.wg1.wu0.wu1.wd0.wd1, ...), custom_call_target="tpu_custom_call" | custom-call | flops 106300440576 | bytes 62914560 | tf_op jit(solution)/shard_map/ffn/pallas_call | solution.py:885
  528.1 17.5 %unmix.1 = (bf16[2048,1024]{1,0:T(8,128)(2,1)S(1)}, f32[2048,1024]{1,0:T(8,128)}, bf16[2048,1024]{1,0:T(8,128)(2,1)S(1)}, bf16[2048,1024]{1,0:T(8,128)(2,1)S(1)}, f32[1,1024]{1,0:T(1,128)S(1)}) custom-call(f32[2048,1024]{1,0:T(8,128)} %copy-done.1, f32[2048,1024]{1,0:T(8,128)} %get-tuple-element.65.gn_ref, bf16[2048,1024]{1,0:T(8,128)(2,1)} %get-tuple-element.66.ffn_ref, ...), custom_call_target="tpu_custom_call" | custom-call | flops 4294967296 | bytes 48234496 | tf_op jit(solution)/shard_map/unmix/pallas_call | solution.py:939
  545.7 2.0 copy-done.4
  547.7 2.0 copy-done.15
  549.7 1.9 copy-done.16
  552.2 5.6 all-to-all-start.1
  557.8 1.6 copy-done.20
  559.4 111.9 %attend_back.1 = (bf16[2048,1024]{1,0:T(8,128)(2,1)}, bf16[2048,1024]{1,0:T(8,128)(2,1)}, bf16[2048,1024]{1,0:T(8,128)(2,1)}) custom-call(s32[130]{0:T(256)S(1)} %pad_add_fusion.meta, bf16[2048,3072]{1,0:T(8,128)(2,1)} %get-tuple-element.55.q_ref.k_ref.v_ref, bf16[2048,3072]{1,0:T(8,128)(2,1)} %get-tuple-element.55.q_ref.k_ref.v_ref, ...), custom_call_target="tpu_custom_call" | custom-call | flops 47815065600 | bytes 41943040 | tf_op jit(solution)/shard_map/attend_back/pallas_call | solution.py:673
  671.4 103.0 %finish.1 = (bf16[2,1024,1024]{2,1,0:T(8,128)(2,1)}, f32[2,1024]{1,0:T(2,128)}, f32[64,2048]{1,0:T(8,128)}) custom-call(bf16[2048,1024]{1,0:T(8,128)(2,1)} %bitcast.33, f32[2048,1024]{1,0:T(8,128)} %get-tuple-element.72.gm_ref, bf16[2048,1024]{1,0:T(8,128)(2,1)} %copy-done.22, bf16[2048,1024]{1,0:T(8,128)(2,1)} %copy-done.10, bf16[2048,1024]{1,0:T(8,128)(2,1)} %copy-done.15, ...), custom_call_target="tpu_custom_call" | custom-call | flops 30064771072 | bytes 83886080 | tf_op jit(solution)/shard_map/finish/pallas_call | solution.py:1192
  774.4 6.7 convert_element_type.27
  781.7 0.8 slice_bitcast_fusion.3
  782.5 1.5 reshape.80
  784.4 1.0 slice_bitcast_fusion
  785.4 4.6 copy.41
  (65 shorter events, 4.2 us)
Async XLA Ops:
  7.2 341.9 %all-gather.2.cloned.1.call-start = ((), (), s32[]{:S(2)}) async-start(), calls=%async_computation.3 | async-start | bytes 20611072 | tf_op jit(solution)/shard_map/all_gather | solution.py:1455
  11.7 2.2 copy-start.3
  13.9 1.6 copy-start.12
  15.5 1.6 copy-start.13
  159.0 2.0 copy-start.5
  161.0 2.0 copy-start.7
  163.0 1.3 copy-start.18
  165.8 2.2 copy-start.6
  174.4 2.1 copy-start
  176.5 143.3 %all-to-all-start = ((bf16[32,128,512]{2,1,0:T(8,128)(2,1)}), bf16[32,128,512]{2,1,0:T(8,128)(2,1)}, u32[]{:S(2)}, u32[]{:S(2)}) async-start(bf16[32,128,512]{2,1,0:T(8,128)(2,1)} %copy-done), calls=%async_computation | async-start | bytes 8388608 | tf_op jit(solution)/shard_map/all_to_all | solution.py:1462
  181.6 600.9 %reduce-scatter.2.cloned.1.call-start = ((), (), s32[]{:S(2)}) async-start(), calls=%async_computation.4 | async-start | bytes 4866048 | tf_op jit(solution)/shard_map/reduce_scatter | solution.py:1476
  181.7 6.4 copy-start.28
  181.7 7.0 copy-start.26
  181.7 7.0 copy-start.27
  186.4 105.8 %collective-permute-start = (bf16[1024,1024]{1,0:T(8,128)(2,1)}, bf16[1024,1024]{1,0:T(8,128)(2,1)}, u32[]{:S(2)}, u32[]{:S(2)}) collective-permute-start(bf16[1024,1024]{1,0:T(8,128)(2,1)} %get-tuple-element.84), channel_id=1, source_target_pairs={{0,1},{1,0},{2,3},{3,2},{4,5},{5,4},{6,7},{7,6},{8,9},{9,8},{10,11... | collective-permute-start | bytes 6291464 | tf_op jit(solution)/shard_map/ppermute | solution.py:1425
  190.0 25.7 %copy-start.14 = (f32[1,1024]{1,0:T(1,128)}, f32[1,1024]{1,0:T(1,128)S(1)}, u32[]{:S(2)}) copy-start(f32[1,1024]{1,0:T(1,128)S(1)} %get-tuple-element.95.gain_ref) | copy-start | bytes 12292
  190.0 2.2 copy-start.8
  192.2 25.5 %copy-start.19 = (bf16[2,1024,512]{2,1,0:T(8,128)(2,1)S(1)}, bf16[2,1024,512]{2,1,0:T(8,128)(2,1)}, u32[]{:S(2)}) copy-start(bf16[2,1024,512]{2,1,0:T(8,128)(2,1)} %copy-done.18) | copy-start | bytes 6291460
  215.6 2.0 copy-start.22
  217.7 74.6 %copy-start.23 = (bf16[1024,1024]{1,0:T(8,128)(2,1)S(1)}, bf16[1024,1024]{1,0:T(8,128)(2,1)}, u32[]{:S(2)}) copy-start(bf16[1024,1024]{1,0:T(8,128)(2,1)} %get-tuple-element.83) | copy-start | bytes 6291460
  289.0 3.3 copy-start.2
  340.1 2.1 copy-start.10
  349.1 2.2 copy-start.9
  351.3 2.2 copy-start.11
  361.1 3.4 copy-start.1
  364.5 2.0 copy-start.17
  545.7 2.0 copy-start.4
  547.7 2.0 copy-start.15
  549.7 1.9 copy-start.16
  551.6 0.6 copy-start.21
  552.2 119.2 %all-to-all-start.1 = ((bf16[2,1024,1024]{2,1,0:T(8,128)(2,1)}), bf16[2,1024,1024]{2,1,0:T(8,128)(2,1)}, u32[]{:S(2)}, u32[]{:S(2)}) async-start(bf16[2,1024,1024]{2,1,0:T(8,128)(2,1)} %bitcast.31), calls=%async_computation.1 | async-start | bytes 8388608 | tf_op jit(solution)/shard_map/all_to_all | solution.py:1483
  557.8 1.7 copy-start.20
  774.4 6.7 copy-start.25
  774.4 7.3 copy-start.24
Sparse Core Ops, SparseCore 0:
  164.5 184.5 all-gather.1
  528.3 95.9 reduce-scatter.1

commit v5 on v4

--- a/solution.py
+++ b/solution.py
@@ -633,7 +633,7 @@
             + [pltpu.VMEM((pair, L // TK, TQ, TK), F32), pltpu.VMEM((pair, TQ, KR * CBLOCK), F32)],
         ),
         out_shape=[jax.ShapeDtypeStruct((L, width), F32)] * 2,
-        compiler_params=pltpu.CompilerParams(vmem_limit_bytes=40 * MIB),
+        compiler_params=pltpu.CompilerParams(vmem_limit_bytes=60 * MIB),
         cost_estimate=pl.CostEstimate(flops=12 * area, bytes_accessed=30 * MIB, transcendentals=area // HD),
         name="attend",
     )(meta, qkv, qkv, qkv, own_k, own_v)
@@ -655,7 +655,7 @@
             scratch_shapes=[pltpu.VMEM((TQ // QBLOCK, KR * CBLOCK, wide), BF16)] * 2,
         ),
         out_shape=[jax.ShapeDtypeStruct((L, width), BF16), jax.ShapeDtypeStruct((L, width), F32)],
-        compiler_params=pltpu.CompilerParams(vmem_limit_bytes=40 * MIB),
+        compiler_params=pltpu.CompilerParams(vmem_limit_bytes=60 * MIB),
         cost_estimate=pl.CostEstimate(
             flops=4 * L * 256 * width, bytes_accessed=30 * MIB, transcendentals=L * 256 * heads
         ),
@@ -681,7 +681,7 @@
             + [pltpu.VMEM((L, wide), F32)] * 2,
         ),
         out_shape=[jax.ShapeDtypeStruct((L, width), BF16)] * 3,
-        compiler_params=pltpu.CompilerParams(vmem_limit_bytes=48 * MIB),
+        compiler_params=pltpu.CompilerParams(vmem_limit_bytes=60 * MIB),
         cost_estimate=pl.CostEstimate(flops=12 * area, bytes_accessed=40 * MIB, transcendentals=area // HD),
         name="attend_back",
     )(meta, qkv, qkv, qkv, own_k, own_v, fetched, fetched, grad_context, context, lse)
@@ -712,7 +712,7 @@
         in_specs=[row(width), pl.BlockSpec((1, width), lambda i: (0, 0)), whole(cols)],
         out_specs=[row(width), row(cols)],
         out_shape=[jax.ShapeDtypeStruct((L, width), BF16), jax.ShapeDtypeStruct((L, cols), BF16)],
-        compiler_params=pltpu.CompilerParams(vmem_limit_bytes=40 * MIB),
+        compiler_params=pltpu.CompilerParams(vmem_limit_bytes=60 * MIB),
         cost_estimate=pl.CostEstimate(flops=2 * L * width * cols, bytes_accessed=26 * MIB, transcendentals=0),
         name="project",
     )(x, gain, weights)
@@ -734,7 +734,7 @@
         in_specs=[row, row, pl.BlockSpec((1, width), lambda i: (0, 0)), pl.BlockSpec((width, width), lambda i: (0, 0))],
         out_specs=[row, row],
         out_shape=[jax.ShapeDtypeStruct((L, width), F32), jax.ShapeDtypeStruct((L, width), BF16)],
-        compiler_params=pltpu.CompilerParams(vmem_limit_bytes=32 * MIB),
+        compiler_params=pltpu.CompilerParams(vmem_limit_bytes=60 * MIB),
         cost_estimate=pl.CostEstimate(flops=2 * L * width * width, bytes_accessed=22 * MIB, transcendentals=0),
         name="mix",
     )(x, context, gain, weights)
@@ -766,9 +766,15 @@
     )
 
 
+UT = 256
+
+
 def ffn_kernel(
-    n_ref, g_ref, wg0, wg1, wu0, wu1, wd0, wd1, out_ref, gn_ref, share_ref,
-    acc, ag, au, ad, part, got, passed, land, pair_send, pair_recv, x_send, x_recv, *, devices,
+    n_ref, g_ref, wg0, wg1, wu0, wu1, wd0, wd1, gain_ref, mixed_ref, wo_ref,
+    share_ref, gg_ref, out_ref, gm_ref, br_ref, gc_ref,
+    acc, gn, hid, duo, part, got, passed, keep, land,
+    wo_buf, mixed_buf, out_buf, br_buf, gc_buf,
+    pair_send, pair_recv, x_send, x_recv, wo_sem, mixed_sem, done_sem, *, devices,
 ):
     tile = pl.program_id(0)
     tiles = pl.num_programs(0)
@@ -778,6 +784,8 @@
     pair = (me + 1 - 2 * core, spot)
     peer = (me, 1 - spot)
     side = HT // 2
+    width = n_ref.shape[1]
+    wo_copy = pltpu.make_async_copy(wo_ref.at[:, pl.ds(0, width)], wo_buf, wo_sem)
 
     @pl.when(tile == 0)
     def _():
@@ -786,93 +794,135 @@
             pl.semaphore_signal(barrier, inc=1, device_id=device, device_id_type=pl.DeviceIdType.MESH)
         pl.semaphore_wait(barrier, 2)
         acc[...] = jnp.zeros_like(acc)
-        gn_ref[...] = jnp.zeros_like(gn_ref)
+        gn[...] = jnp.zeros_like(gn)
 
     def to_pair(k):
-        return remote(part.at[k % 2, :, 1 - core], got.at[k], pair_send.at[k], pair_recv.at[k], pair)
+        return remote(part.at[k % 2, :, 1 - core], got.at[k % 2], pair_send.at[k % 2], pair_recv.at[k % 2], pair)
 
     def to_peer(k):
-        return remote(passed.at[k % 2], land.at[k], x_send.at[k], x_recv.at[k], peer)
+        return remote(passed.at[k % 2], land.at[k % 4], x_send.at[k % 2], x_recv.at[k % 4], peer)
 
     def join(k):
-        to_pair(k).wait()
-
-        @pl.when(k >= 2)
-        def _():
-            to_peer(k - 2).wait_send()
-
-        def one(b, carry):
-            total = got[k, b].astype(F32) + part[k % 2, b, core].astype(F32)
-            low = total.astype(BF16)
-            for m in range(3):
-                passed[k % 2, b, :, m * side : (m + 1) * side] = low[:, m * HT + side : (m + 1) * HT]
-                got[k, b, :, m * side : (m + 1) * side] = low[:, m * HT : m * HT + side]
-            return carry
-
-        lax.fori_loop(0, part.shape[1], one, 0)
-        to_peer(k).start()
+        slot = (k + 2) % 2
+        total = (got[slot].astype(F32) + part[slot, :, core].astype(F32)).astype(BF16)
+        for m in range(3):
+            passed[slot, :, :, m * side : (m + 1) * side] = total[:, :, m * HT + side : (m + 1) * HT]
+            keep[(k + 4) % 4, :, :, m * side : (m + 1) * side] = total[:, :, m * HT : m * HT + side]
 
     def settle(k):
-        to_peer(k).wait_recv()
-
-        def one(b, carry):
-            total = got[k, b, :, : 3 * side].astype(F32) + land[k, b].astype(F32)
-            rs = pl.ds(pl.multiple_of(b * part.shape[3], part.shape[3]), part.shape[3])
-            share_ref[rs, pl.ds(pl.multiple_of(k * 3 * side, 3 * side), 3 * side)] = total.astype(BF16)
-            return carry
-
-        lax.fori_loop(0, part.shape[1], one, 0)
-
-    ag[...] = jnp.zeros_like(ag)
-    au[...] = jnp.zeros_like(au)
-    ad[...] = jnp.zeros_like(ad)
-    wg = jnp.concatenate([wg0[...], wg1[...]], axis=1)
-    wu = jnp.concatenate([wu0[...], wu1[...]], axis=1)
+        slot = (jnp.maximum(k, -1) + 4) % 4
+        total = (keep[slot].astype(F32) + land[slot].astype(F32)).astype(BF16)
+        place = pl.multiple_of(jnp.maximum(k, 0) * 3 * side, 3 * side)
+        share_ref[:, pl.ds(place, 3 * side)] = total.reshape(share_ref.shape[0], 3 * side)
+
+    wgu = jnp.concatenate([wg0[...], wg1[...], wu0[...], wu1[...]], axis=1)
     wd = jnp.concatenate([wd0[...], wd1[...]], axis=1)
 
-    def chunk(r, carry):
-        rs = pl.ds(pl.multiple_of(r * ROWS, ROWS), ROWS)
-        rows = n_ref[rs, :]
-        cotangent = g_ref[rs, :]
-        gate = mm(rows, wg)
-        up = mm(rows, wu)
-        grad_hidden = mm(cotangent, wd)
+    def chunk(r):
+        rs = pl.ds(r * ROWS, ROWS)
+        both = mm(n_ref[rs, :], wgu)
+        grad_hidden = mm(g_ref[rs, :], wd)
+        gate, up = both[:, :HT], both[:, HT:]
         sigma = 1.0 / (1.0 + jnp.exp(-gate))
         silu = gate * sigma
         hidden = (silu * up).astype(BF16)
-        grad_gate = (grad_hidden * up * (sigma * (1.0 + gate * (1.0 - sigma)))).astype(BF16)
-        grad_up = (grad_hidden * silu).astype(BF16)
+        grad_gate = grad_hidden * up * (sigma * (1.0 + gate * (1.0 - sigma)))
+        grads = jnp.concatenate([grad_gate.astype(BF16), (grad_hidden * silu).astype(BF16)], axis=1)
         acc[rs, :] += mm(hidden, wd, NT)
-        gn_ref[rs, :] += mm(grad_gate, wg, NT) + mm(grad_up, wu, NT)
-        ag[...] += mm(rows, grad_gate, TN)
-        au[...] += mm(rows, grad_up, TN)
-        ad[...] += mm(cotangent, hidden, TN)
-        return carry
-
-    lax.fori_loop(0, L // ROWS, chunk, 0)
-    for m, held in enumerate((ag, au, ad)):
-        part[tile % 2, :, :, :, m * HT : (m + 1) * HT] = held[...].astype(BF16).reshape(part.shape[1:4] + (HT,))
-    to_pair(tile).start()
+        gn[rs, :] += mm(grads, wgu, NT)
+        hid[rs, :] = hidden
+        duo[rs, :] = grads
+
+    @pl.when(tile > 2)
+    def _():
+        to_peer(tile - 3).wait()
+
+    settle(tile - 3)
+    for r in range(L // ROWS):
+        chunk(r)
 
     @pl.when(tile > 0)
     def _():
-        join(tile - 1)
-
-    @pl.when(tile > 1)
+        to_pair(tile - 1).wait()
+
+    join(tile - 1)
+    slot = tile % 2
+    shape = part.shape[1:4]
+    part[slot, :, :, :, : 2 * HT] = mm(n_ref[...], duo[...], TN).astype(BF16).reshape(shape + (2 * HT,))
+    part[slot, :, :, :, 2 * HT :] = mm(g_ref[...], hid[...], TN).astype(BF16).reshape(shape + (HT,))
+    to_pair(tile).start()
+
+    @pl.when(tile > 0)
     def _():
-        settle(tile - 2)
+        to_peer(tile - 1).start()
+
+    def rows_of(t):
+        return pl.ds(pl.multiple_of(t * UT, UT), UT)
+
+    def fetch(t):
+        return pltpu.make_async_copy(mixed_ref.at[rows_of(t), :], mixed_buf.at[t % 2], mixed_sem.at[t % 2])
+
+    def write(t):
+        sources = [out_buf.at[t % 2], gn.at[rows_of(t), :], br_buf.at[t % 2], gc_buf.at[t % 2]]
+        return [
+            pltpu.make_async_copy(source, ref.at[rows_of(t), :], done_sem.at[i, t % 2])
+            for i, (source, ref) in enumerate(zip(sources, [out_ref, gm_ref, br_ref, gc_ref]))
+        ]
+
+    def unmix(t, carry):
+        @pl.when(t < L // UT - 1)
+        def _():
+            fetch(t + 1).start()
+
+        fetch(t).wait()
+
+        @pl.when(t > 1)
+        def _():
+            for copy in write(t - 2):
+                copy.wait()
+
+        rs = rows_of(t)
+        now = t % 2
+        mixed = mixed_buf[now]
+        grad = gn[rs, :]
+        scale = lax.rsqrt(jnp.mean(mixed * mixed, axis=1, keepdims=True) + EPS)
+        unit = mixed * scale
+        inner = grad * gain_ref[...]
+        back = scale * (inner - unit * jnp.mean(inner * unit, axis=1, keepdims=True))
+        grad_mixed = g_ref[rs, :].astype(F32) + back
+        out_buf[now] = (mixed + acc[rs, :]).astype(BF16)
+        gn[rs, :] = grad_mixed
+        branch = grad_mixed.astype(BF16)
+        br_buf[now] = branch
+        gc_buf[now] = mm(branch, wo_buf[...]).astype(BF16)
+        gg_ref[...] += jnp.sum(grad * unit, axis=0, keepdims=True)
+        for copy in write(t):
+            copy.start()
+        return carry
 
     @pl.when(tile == tiles - 1)
     def _():
+        wo_copy.start()
+        fetch(0).start()
+        gg_ref[...] = jnp.zeros_like(gg_ref)
+        to_peer(tile - 2).wait()
+        settle(tile - 2)
+        wo_copy.wait()
+        lax.fori_loop(0, 4, unmix, 0)
+        to_pair(tile).wait()
         join(tile)
+        to_peer(tile).start()
+        lax.fori_loop(4, L // UT, unmix, 0)
+        to_peer(tile - 1).wait()
         settle(tile - 1)
-        out_ref[...] = acc[...].astype(BF16)
+        to_peer(tile).wait()
         settle(tile)
-        to_peer(tile - 1).wait_send()
-        to_peer(tile).wait_send()
-
-
-def ffn(normed, cotangent, weights, width, hidden, devices):
+        for t in (L // UT - 2, L // UT - 1):
+            for copy in write(t):
+                copy.wait()
+
+
+def ffn(normed, cotangent, weights, gain, mixed, width, hidden, devices):
     once = pl.Buffered(1)
     tiles = hidden // HT
     side = HT // 2
@@ -881,77 +931,40 @@
     lead = width // side
     part = lambda k: pl.BlockSpec((width, side), lambda j: (0, lead + k * tiles + j))
     whole = pl.BlockSpec((L, width), lambda j: (0, 0), pipeline_mode=once)
+    fixed = lambda shape: pl.BlockSpec(shape, lambda j: (0, 0), pipeline_mode=once)
+    hbm = pl.BlockSpec(memory_space=pltpu.HBM)
     dma = pltpu.SemaphoreType.DMA
+    tile = lambda kind: pltpu.VMEM((2, UT, width), kind)
     return pl.pallas_call(
         functools.partial(ffn_kernel, devices=devices),
         grid=(tiles,),
-        in_specs=[whole, whole] + [part(k) for k in range(6)],
-        out_specs=[
-            whole, whole, pl.BlockSpec((width // 2, 3 * hidden // 2), lambda j: (0, 0), pipeline_mode=once)
-        ],
+        in_specs=[whole, whole] + [part(k) for k in range(6)] + [fixed((1, width)), hbm, hbm],
+        out_specs=[fixed((width // 2, 3 * hidden // 2)), fixed((1, width)), hbm, hbm, hbm, hbm],
         out_shape=[
+            jax.ShapeDtypeStruct((width // 2, 3 * hidden // 2), BF16),
+            jax.ShapeDtypeStruct((1, width), F32),
             jax.ShapeDtypeStruct((L, width), BF16),
             jax.ShapeDtypeStruct((L, width), F32),
-            jax.ShapeDtypeStruct((width // 2, 3 * hidden // 2), BF16),
+            jax.ShapeDtypeStruct((L, width), BF16),
+            jax.ShapeDtypeStruct((L, width), BF16),
         ],
-        scratch_shapes=[pltpu.VMEM((L, width), F32)]
-        + [pltpu.VMEM((width, HT), F32)] * 3
-        + [
+        scratch_shapes=[
+            pltpu.VMEM((L, width), F32), pltpu.VMEM((L, width), F32),
+            pltpu.VMEM((L, HT), BF16), pltpu.VMEM((L, 2 * HT), BF16),
             pltpu.VMEM((2, chips, 2, rows, 3 * HT), BF16),
-            pltpu.VMEM((tiles, chips, rows, 3 * HT), BF16),
+            pltpu.VMEM((2, chips, rows, 3 * HT), BF16),
             pltpu.VMEM((2, chips, rows, 3 * side), BF16),
-            pltpu.VMEM((tiles, chips, rows, 3 * side), BF16),
-            dma((tiles,)), dma((tiles,)), dma((tiles,)), dma((tiles,)),
+            pltpu.VMEM((4, chips, rows, 3 * side), BF16),
+            pltpu.VMEM((4, chips, rows, 3 * side), BF16),
+            pltpu.VMEM((width, width), BF16), tile(F32), tile(BF16), tile(BF16), tile(BF16),
+            dma((2,)), dma((2,)), dma((2,)), dma((4,)), dma, dma((2,)), dma((4, 2)),
         ],
         compiler_params=pltpu.CompilerParams(collective_id=2, has_side_effects=True, vmem_limit_bytes=61 * MIB),
         cost_estimate=pl.CostEstimate(
             flops=18 * L * width * hidden, bytes_accessed=60 * MIB, transcendentals=L * hidden
         ),
         name="ffn",
-    )(normed, cotangent, *([weights] * 6))
-
-
-def unmix_kernel(mixed_ref, gn_ref, ffn_ref, g_ref, gain_ref, w_ref, out_ref, gm_ref, br_ref, gc_ref, gg_ref):
-    mixed = mixed_ref[...]
-    grad = gn_ref[...]
-    scale = lax.rsqrt(jnp.mean(mixed * mixed, axis=1, keepdims=True) + EPS)
-    unit = mixed * scale
-    inner = grad * gain_ref[...]
-    grad_mixed = g_ref[...].astype(F32) + scale * (inner - unit * jnp.mean(inner * unit, axis=1, keepdims=True))
-    out_ref[...] = (mixed + ffn_ref[...].astype(F32)).astype(BF16)
-    gm_ref[...] = grad_mixed
-    branch = grad_mixed.astype(BF16)
-    br_ref[...] = branch
-    gc_ref[...] = mm(branch, w_ref[...]).astype(BF16)
-
-    @pl.when(pl.program_id(0) == 0)
-    def _():
-        gg_ref[...] = jnp.zeros_like(gg_ref)
-
-    gg_ref[...] += jnp.sum(grad * unit, axis=0, keepdims=True)
-
-
-def unmix(mixed, grad_normed, ffn_out, cotangent, gain, weights):
-    width = mixed.shape[1]
-    rows = ROWS // 2
-    row = pl.BlockSpec((rows, width), lambda i: (i, 0))
-    one = pl.BlockSpec((1, width), lambda i: (0, 0))
-    return pl.pallas_call(
-        unmix_kernel,
-        grid=(L // rows,),
-        in_specs=[row, row, row, row, one, pl.BlockSpec((width, width), lambda i: (0, 0))],
-        out_specs=[row, row, row, row, one],
-        out_shape=[
-            jax.ShapeDtypeStruct((L, width), BF16),
-            jax.ShapeDtypeStruct((L, width), F32),
-            jax.ShapeDtypeStruct((L, width), BF16),
-            jax.ShapeDtypeStruct((L, width), BF16),
-            jax.ShapeDtypeStruct((1, width), F32),
-        ],
-        compiler_params=pltpu.CompilerParams(vmem_limit_bytes=40 * MIB),
-        cost_estimate=pl.CostEstimate(flops=2 * L * width * width, bytes_accessed=46 * MIB, transcendentals=0),
-        name="unmix",
-    )(mixed, grad_normed, ffn_out, cotangent, gain, weights)
+    )(normed, cotangent, *([weights] * 6), gain, mixed, weights)
 
 
 FT = 256
@@ -1237,7 +1250,7 @@
             scratch_shapes=[pltpu.SemaphoreType.DMA((count,))],
         ),
         out_shape=jax.ShapeDtypeStruct(held.shape, held.dtype),
-        compiler_params=pltpu.CompilerParams(vmem_limit_bytes=16 * MIB),
+        compiler_params=pltpu.CompilerParams(vmem_limit_bytes=60 * MIB),
         cost_estimate=pl.CostEstimate(flops=0, bytes_accessed=2 * held.size * 2, transcendentals=0),
         name="pick_rows",
     )(table, held)
@@ -1415,7 +1428,7 @@
             dma((12,)), dma((10,)), dma((10,)), dma((2, devices)), dma((2, devices)),
             dma((RING - 1,)), dma((RING - 1,)), dma((RING,)), dma((RING,)),
         ],
-        compiler_params=pltpu.CompilerParams(collective_id=0, has_side_effects=True, vmem_limit_bytes=32 * MIB),
+        compiler_params=pltpu.CompilerParams(collective_id=0, has_side_effects=True, vmem_limit_bytes=60 * MIB),
         cost_estimate=pl.CostEstimate(flops=0, bytes_accessed=300 * MIB, transcendentals=0),
         name="spread",
     )(tokens, cache_keys, cache_values, small, extra, big)
@@ -1472,13 +1485,12 @@
     partial, partial_lse = attend(meta, qkv, own_k, own_v)
     context, lse = attend_other(meta, qkv, fetched, partial, partial_lse)
     mixed, normed_two = mix(x, context, gain_two, second_all)
-    ffn_out, grad_normed_two, ffn_grads = ffn(normed_two, cotangent, second_all, width, hidden, devices)
+    ffn_grads, gain_part_two, out, grad_mixed, branch, grad_context = ffn(
+        normed_two, cotangent, second_all, gain_two, mixed, width, hidden, devices
+    )
     ffn_share = lax.psum_scatter(
         ffn_grads, "dp", scatter_dimension=0, tiled=True,
         axis_index_groups=[list(range(c, devices, 2)) for c in range(2)],
-    )
-    out, grad_mixed, branch, grad_context, gain_part_two = unmix(
-        mixed, grad_normed_two, ffn_out, cotangent, gain_two, second_all
     )
     out = exchange(out.reshape(2, shard_len, width))
     dq, dk, dv = attend_back(meta, qkv, own_k, own_v, fetched, grad_context, context, lse)

time: 812 us -> 762 us (0.938); the launches traced: 797 us -> 757 us
  local copies, waits for them, and re-layouts: 60.3 us -> 18.3 us
  Pallas kernels: 665 us -> 652 us
  waiting for transfers between devices: 29.6 us -> 41.5 us
    unnamed x59 -> x11, local copies, waits for them, and re-layouts: 47.2 us -> 4.67 us
    pallas_call x1 -> x0, Pallas kernels: 17.5 us -> none  [unmix(): pl.pallas_call(unmix_kernel, grid=(L // rows,), in_specs=[row, row, row,...]
  transfers between devices with their start and end apart: 5 -> 5, of which waited for: 2 -> 2; matrix products, arithmetic and copies ran while one was open for 3% -> 3% of each run, Pallas kernels for 44% -> 45%
where the time goes in v5:
time: 762 us; the launch traced here: 757 us
  Pallas kernels  652 us (86%)
  waiting for transfers between devices  41.5 us (5%)
  local copies, waits for them, and re-layouts  18.3 us (2%)
  other arithmetic  17.8 us (2%)
  between operations  14.4 us (2%)
  starting transfers between devices  12.8 us (2%)
    pallas_call x1, Pallas kernels, ffn(): pl.pallas_call(functools.partial(ffn_kernel, devices=devices), grid=(tile...  160 us
    pallas_call x1, Pallas kernels, spread(): pl.pallas_call(spread_kernel, in_specs=[anywhere, anywhere, anywhere, vme...  143 us
    pallas_call x1, Pallas kernels, attend_back(): pl.pallas_call(functools.partial(attend_back_kernel, pair=pair), grid_spe...  112 us
    pallas_call x1, Pallas kernels, finish(): pl.pallas_call(functools.partial(finish_kernel, devices=devices), in_spec...  103 us
    pallas_call x1, Pallas kernels, attend(): pl.pallas_call(functools.partial(attend_kernel, pair=pair), grid_spec=plt...  71.1 us
    all_to_all x1, waiting for transfers between devices, sequence_body(): lax.all_to_all(sent, ('dp', 'tensor'), split_axis=0, concat_axis=0, tiled...  28.7 us
    pallas_call x1, Pallas kernels, project(): pl.pallas_call(project_kernel, grid=(L // ROWS,), in_specs=[row(width), p...  24.4 us
    pallas_call x1, Pallas kernels, attend_other(): pl.pallas_call(functools.partial(attend_other_kernel, pair=pair), grid_sp...  21.5 us
  transfers between devices with their start and end apart: 5, of which 2 were waited for; matrix products, arithmetic and copies ran while one was open for 3% of the time, Pallas kernels for 45%

profile of v5, /device:TPU:0, one launch (start us, length us, event | category | flops | bytes accessed | tf_op | source)
XLA Modules:
  0.0 756.5 jit_solution(13487133006244251605)
XLA Ops:
  7.2 0.0 all-gather.2.cloned.1.call-start
  7.2 0.7 convert_bitcast_fusion
  7.9 0.1 copy.36
  8.0 0.8 copy.37
  8.8 0.8 copy.38
  9.5 0.1 pad.16.clone
  9.6 1.6 pad_maximum_fusion.1.small_ref
  11.2 0.7 fusion.3.extra_ref
  11.9 2.0 pad_maximum_fusion.big_ref
  13.8 143.0 %spread.1 = (bf16[2,1024,1024]{2,1,0:T(8,128)(2,1)}, bf16[2,1024,512]{2,1,0:T(8,128)(2,1)}, bf16[2,1024,512]{2,1,0:T(8,128)(2,1)}, bf16[16,2,2,64,512]{4,3,2,1,0...) custom-call(bf16[2,1024,1024]{2,1,0:T(8,128)(2,1)} %tok_ref.1, bf16[2,1024,512]{2,1,0:T(8,128)(2,1)} %ck_ref.1, ...), custom_call_target="tpu_custom_call" | custom-call | bytes 314572800 | tf_op jit(solution)/shard_map/spread/pallas_call | solution.py:1412
  156.9 0.0 all-gather.2.cloned.1.call-update
  156.9 1.0 slice.46
  157.9 0.2 slice_reduce_fusion
  158.1 0.1 reshape_squeeze.11
  158.2 0.6 reshape.78.table
  158.8 5.1 pick_rows.1
  164.0 5.4 all-to-all-start
  169.3 0.0 reduce-scatter.2.cloned.1.call-start
  169.4 4.2 dynamic-slice_bitcast_fusion.1
  173.6 1.7 collective-permute-start
  175.4 0.6 dynamic_slice.16
  175.9 0.1 copy.35
  176.0 0.1 reshape_squeeze.10
  176.1 0.1 copy.34
  176.2 0.1 reshape_squeeze.9
  176.3 1.3 pad_add_fusion.meta
  177.6 0.2 fusion.4
  177.7 0.6 fusion.9
  178.4 24.4 %project.1 = (bf16[2048,1024]{1,0:T(8,128)(2,1)}, bf16[2048,3072]{1,0:T(8,128)(2,1)}) custom-call(bf16[2048,1024]{1,0:T(8,128)(2,1)} %bitcast.34, f32[1,1024]{1,0:T(1,128)} %get-tuple-element.91.gain_ref, bf16[1024,3200]{1,0:T(8,128)(2,1)} %get-tuple-element.52.w_ref), custom_call_target="tpu_custom_call" | custom-call | flops 12884901888 | bytes 27262976 | tf_op jit(solution)/shard_map/project/pallas_call | solution.py:709
  202.7 71.1 %attend.1 = (f32[2048,1024]{1,0:T(8,128)}, f32[2048,1024]{1,0:T(8,128)}) custom-call(s32[130]{0:T(256)} %pad_add_fusion.meta, bf16[2048,3072]{1,0:T(8,128)(2,1)} %get-tuple-element.53.q_ref.k_ref.v_ref, bf16[2048,3072]{1,0:T(8,128)(2,1)} %get-tuple-element.53.q_ref.k_ref.v_ref, bf16[2048,3072]{1,0:T(8,128)(2,1)} %get-tuple-element.53.q_ref.k_ref.v_ref, ...), custom_call_target="tpu_custom_call" | custom-call | flops 40265318400 | bytes 31457280 | tf_op jit(solution)/shard_map/attend/pallas_call | solution.py:625
  273.8 4.9 maximum_select_fusion.g_ref
  278.7 28.7 %all-to-all-done = bf16[32,128,512]{2,1,0:T(8,128)(2,1)} async-done(((bf16[32,128,512]{2,1,0:T(8,128)(2,1)}), bf16[32,128,512]{2,1,0:T(8,128)(2,1)}, u32[]{:S(2)}, u32[]{:S(2)}) %all-to-all-start) | async-done | bytes 4194336 | tf_op jit(solution)/shard_map/all_to_all | solution.py:1475
  307.4 21.5 %attend_other.1 = (bf16[2048,1024]{1,0:T(8,128)(2,1)}, f32[2048,1024]{1,0:T(8,128)}) custom-call(s32[130]{0:T(256)} %pad_add_fusion.meta, bf16[2048,3072]{1,0:T(8,128)(2,1)} %get-tuple-element.53.q_ref.k_ref.v_ref, bf16[16,2,2,64,512]{4,3,2,1,0:T(8,128)(2,1)} %bitcast.8.pk_ref.pv_ref, bf16[16,2,2,64,512]{4,3,2,1,0:T(8,128)(2,1)} %bitcast.8.pk_ref.pv_ref, ...), custom_call_target="tpu_custom_call" | custom-call | flops 2147483648 | bytes 31457280 | tf_op jit(solution)/shard_map/attend_other/pallas_call | solution.py:648
  328.9 12.7 %all-gather.2.cloned.1.call-done.w_ref.wg0.wg1.wu0.wu1.wd0.wd1.wo_ref = bf16[1024,9472]{1,0:T(8,128)(2,1)} async-done(((bf16[64,9472]{1,0:T(8,128)(2,1)}), bf16[1024,9472]{1,0:T(8,128)(2,1)}) %all-gather.2.cloned.1.call-update) | async-done | bytes 19398672 | tf_op jit(solution)/shard_map/all_gather | solution.py:1468
  341.6 11.5 %mix.1 = (f32[2048,1024]{1,0:T(8,128)}, bf16[2048,1024]{1,0:T(8,128)(2,1)}) custom-call(bf16[2048,1024]{1,0:T(8,128)(2,1)} %bitcast.35, bf16[2048,1024]{1,0:T(8,128)(2,1)} %get-tuple-element.59.ctx_ref, f32[1,1024]{1,0:T(1,128)} %get-tuple-element.90.gain_ref, bf16[1024,9472]{1,0:T(8,128)(2,1)} %all-gather.2.cloned.1.call-done.w_ref.wg0.wg1.wu0.wu1.wd0.wd1.wo_ref), custom_call_target="tpu_custom_call" | custom-call | flops 4294967296 | bytes 23068672 | tf_op jit(solution)/shard_map/mix/pallas_call | solution.py:731
  353.1 160.0 %ffn.1 = (bf16[512,4224]{1,0:T(8,128)(2,1)}, f32[1,1024]{1,0:T(1,128)}, bf16[2048,1024]{1,0:T(8,128)(2,1)}, f32[2048,1024]{1,0:T(8,128)}, bf16[2048,1024]{1,0:T(8,128)(2,1)}, /*index=5*/bf16[2048,1024]{1,0:T(8,128)(2,1)}) custom-call(bf16[2048,1024]{1,0:T(8,128)(2,1)} %get-tuple-element.61.n_ref, bf16[2048,1024]{1,0:T(8,128)(2,1)} %maximum_select_fusion.g_ref, ...), custom_call_target="tpu_custom_call" | custom-call | flops 106300440576 | bytes 62914560 | tf_op jit(solution)/shard_map/ffn/pallas_call | solution.py:938
  513.2 0.0 reduce-scatter.2.cloned.1.call-update
  513.2 5.6 all-to-all-start.1
  518.8 112.0 %attend_back.1 = (bf16[2048,1024]{1,0:T(8,128)(2,1)}, bf16[2048,1024]{1,0:T(8,128)(2,1)}, bf16[2048,1024]{1,0:T(8,128)(2,1)}) custom-call(s32[130]{0:T(256)} %pad_add_fusion.meta, bf16[2048,3072]{1,0:T(8,128)(2,1)} %get-tuple-element.53.q_ref.k_ref.v_ref, bf16[2048,3072]{1,0:T(8,128)(2,1)} %get-tuple-element.53.q_ref.k_ref.v_ref, ...), custom_call_target="tpu_custom_call" | custom-call | flops 47815065600 | bytes 41943040 | tf_op jit(solution)/shard_map/attend_back/pallas_call | solution.py:673
  630.9 102.9 %finish.1 = (bf16[2,1024,1024]{2,1,0:T(8,128)(2,1)}, f32[2,1024]{1,0:T(2,128)}, f32[64,2048]{1,0:T(8,128)}) custom-call(bf16[2048,1024]{1,0:T(8,128)(2,1)} %bitcast.36, f32[2048,1024]{1,0:T(8,128)} %get-tuple-element.68.gm_ref, bf16[2048,1024]{1,0:T(8,128)(2,1)} %get-tuple-element.69.n_ref, bf16[2048,1024]{1,0:T(8,128)(2,1)} %get-tuple-element.59.ctx_ref, ...), custom_call_target="tpu_custom_call" | custom-call | flops 30064771072 | bytes 83886080 | tf_op jit(solution)/shard_map/finish/pallas_call | solution.py:1205
  733.8 6.7 convert_element_type.27
  740.5 0.6 fusion.8
  741.1 0.8 slice_bitcast_fusion.3
  741.9 1.5 reshape.80
  743.5 0.2 copy.39
  743.6 0.2 reshape.79
  743.8 1.0 slice_bitcast_fusion
  744.8 4.6 copy.41
  (16 shorter events, 0.0 us)
Async XLA Ops:
  7.2 334.5 %all-gather.2.cloned.1.call-start = ((), (), s32[]{:S(2)}) async-start(), calls=%async_computation.3 | async-start | bytes 20611072 | tf_op jit(solution)/shard_map/all_gather | solution.py:1468
  164.0 143.5 %all-to-all-start = ((bf16[32,128,512]{2,1,0:T(8,128)(2,1)}), bf16[32,128,512]{2,1,0:T(8,128)(2,1)}, u32[]{:S(2)}, u32[]{:S(2)}) async-start(bf16[32,128,512]{2,1,0:T(8,128)(2,1)} %pick_rows.1), calls=%async_computation | async-start | bytes 8388608 | tf_op jit(solution)/shard_map/all_to_all | solution.py:1475
  169.3 572.6 %reduce-scatter.2.cloned.1.call-start = ((), (), s32[]{:S(2)}) async-start(), calls=%async_computation.4 | async-start | bytes 4866048 | tf_op jit(solution)/shard_map/reduce_scatter | solution.py:1491
  169.4 6.0 copy-start.4
  169.4 6.5 copy-start.2
  169.4 6.5 copy-start.3
  173.6 100.2 %collective-permute-start = (bf16[1024,1024]{1,0:T(8,128)(2,1)}, bf16[1024,1024]{1,0:T(8,128)(2,1)}, u32[]{:S(2)}, u32[]{:S(2)}) collective-permute-start(bf16[1024,1024]{1,0:T(8,128)(2,1)} %get-tuple-element.80), channel_id=1, source_target_pairs={{0,1},{1,0},{2,3},{3,2},{4,5},{5,4},{6,7},{7,6},{8,9},{9,8},{10,11... | collective-permute-start | bytes 6291464 | tf_op jit(solution)/shard_map/ppermute | solution.py:1438
  513.2 117.7 %all-to-all-start.1 = ((bf16[2,1024,1024]{2,1,0:T(8,128)(2,1)}), bf16[2,1024,1024]{2,1,0:T(8,128)(2,1)}, u32[]{:S(2)}, u32[]{:S(2)}) async-start(bf16[2,1024,1024]{2,1,0:T(8,128)(2,1)} %bitcast.32), calls=%async_computation.1 | async-start | bytes 8388608 | tf_op jit(solution)/shard_map/all_to_all | solution.py:1495
  733.8 6.7 copy-start.1
  733.8 7.3 copy-start
Sparse Core Ops, SparseCore 0:
  157.0 184.5 all-gather.1
  513.3 95.9 reduce-scatter.1

commit v6 on v5

--- a/solution.py
+++ b/solution.py
@@ -616,7 +616,7 @@
     ]
 
 
-def attend(meta, qkv, own_k, own_v, pair=2):
+def attend(meta, qkv, own_k, own_v, pair=4):
     width = qkv.shape[1] // 3
     heads = width // HD
     wide = pair * HD
@@ -663,7 +663,7 @@
     )(meta, qkv, fetched, fetched, partial, lse)
 
 
-def attend_back(meta, qkv, own_k, own_v, fetched, grad_context, context, lse, pair=2):
+def attend_back(meta, qkv, own_k, own_v, fetched, grad_context, context, lse, pair=4):
     width = context.shape[1]
     heads = width // HD
     wide = pair * HD
@@ -812,8 +812,10 @@
     def settle(k):
         slot = (jnp.maximum(k, -1) + 4) % 4
         total = (keep[slot].astype(F32) + land[slot].astype(F32)).astype(BF16)
-        place = pl.multiple_of(jnp.maximum(k, 0) * 3 * side, 3 * side)
-        share_ref[:, pl.ds(place, 3 * side)] = total.reshape(share_ref.shape[0], 3 * side)
+        total = total.reshape(share_ref.shape[0], 3 * side)
+        for m in range(3):
+            place = pl.multiple_of((m * tiles + jnp.maximum(k, 0)) * side, side)
+            share_ref[:, pl.ds(place, side)] = total[:, m * side : (m + 1) * side]
 
     wgu = jnp.concatenate([wg0[...], wg1[...], wu0[...], wu1[...]], axis=1)
     wd = jnp.concatenate([wd0[...], wd1[...]], axis=1)
@@ -1026,52 +1028,52 @@
 
     pair = (me + 1 - 2 * core, spot)
 
-    def to_pair(m):
-        cs = pl.ds(m * width, width)
-        return remote(part.at[:, 1 - core, :, cs], got.at[:, :, cs], pair_send.at[m], pair_recv.at[m], pair)
+    def column(m, h):
+        return (m // 2) * 2 * width + h * width + (m % 2) * half
+
+    def to_pair(m, h):
+        cs = pl.ds(column(m, h), half)
+        return remote(
+            part.at[:, 1 - core, :, cs], got.at[:, :, cs], pair_send.at[m, h], pair_recv.at[m, h], pair
+        )
 
     def product(m, left, right):
-        def chunk(c, carry):
-            cs = pl.ds(pl.multiple_of(c * half, half), half)
-            value = mm(left[...], right[:, cs], TN).astype(BF16)
-            part[:, :, :, pl.ds(pl.multiple_of(m * width + c * half, half), half)] = value.reshape(
-                part.shape[0], 2, rows, half
-            )
-            return carry
-
-        lax.fori_loop(0, 2, chunk, 0)
-        to_pair(m).start()
-
-    def join(m):
-        to_pair(m).wait_recv()
-        cs = pl.ds(m * width, width)
-
-        def one(b, carry):
-            got[b, :, cs] = (got[b, :, cs].astype(F32) + part[b, core, :, cs].astype(F32)).astype(BF16)
-            return carry
-
-        lax.fori_loop(0, part.shape[0], one, 0)
-
-    span = 2 * width
+        for h in range(2):
+            value = mm(left[...], right[:, h * half : (h + 1) * half], TN).astype(BF16)
+            part[:, :, :, column(m, h) : column(m, h) + half] = value.reshape(part.shape[0], 2, rows, half)
+            to_pair(m, h).start()
+
+    def join(m, h):
+        to_pair(m, h).wait_recv()
+        cs = pl.ds(column(m, h), half)
+        got[:, :, cs] = (got[:, :, cs].astype(F32) + part[:, core, :, cs].astype(F32)).astype(BF16)
+
     neighbours = [(place + 1) % RING, (place + RING - 1) % RING]
 
-    def held_block(direction, s):
+    def held_block(g, direction, s):
         p = (place + 2 * RING - 1 - s) % RING if direction == 0 else (place + 1 + s) % RING
-        return got.at[ring_place(p), :, pl.ds(direction * span, span)]
-
-    def hop(direction, s):
+        return got.at[ring_place(p), :, pl.ds((2 * g + direction) * width, width)]
+
+    def hop(g, direction, s):
         to = ring_place(neighbours[direction]) * 2 + core
         return remote(
-            held_block(direction, s), land.at[direction, s],
-            ring_send.at[direction, s], ring_recv.at[direction, s], (to, spot),
-        )
-
-    def advance(direction, s, more=True):
-        hop(direction, s).wait_recv()
-        block = held_block(direction, s + 1)
-        block[...] = (block[...].astype(F32) + land[direction, s].astype(F32)).astype(BF16)
-        if more:
-            hop(direction, s + 1).start()
+            held_block(g, direction, s), land.at[g, direction, s],
+            ring_send.at[g, direction, s], ring_recv.at[g, direction, s], (to, spot),
+        )
+
+    def advance(g, s, more=True):
+        for direction in range(2):
+            hop(g, direction, s).wait_recv()
+            block = held_block(g, direction, s + 1)
+            block[...] = (block[...].astype(F32) + land[g, direction, s].astype(F32)).astype(BF16)
+            if more:
+                hop(g, direction, s + 1).start()
+
+    def launch(g):
+        for h in range(2):
+            join(2 * g, h)
+            join(2 * g + 1, h)
+            hop(g, h, 0).start()
 
     def finish_rows(t, slot, k):
         for copy in tile_in(t, slot):
@@ -1088,56 +1090,54 @@
         gt_buf[k] = (gm_buf[slot] + back).astype(BF16)
         gains[:1, :] += jnp.sum(grad * unit, axis=0, keepdims=True)
 
+    def two_tiles(j, advances, give_away):
+        for slot in (0, 1):
+            k = 2 * j + slot
+            if slot == 0 or give_away:
+                for copy in tile_in(tile_of(k + 1), 1 - slot):
+                    copy.start()
+            else:
+
+                @pl.when(j < held - 1)
+                def _():
+                    for copy in tile_in(tile_of(k + 1), 0):
+                        copy.start()
+
+            finish_rows(tile_of(k), slot, k)
+            if give_away:
+                give(k, k).start()
+            else:
+                keep(k - held, k).start()
+        for g, s in advances:
+            advance(g, s)
+
+    gains[:1, :] = jnp.zeros((1, width), F32)
+    gains[1:, :] = gain_two_ref[...]
     for i in (0, 1):
         loads[i].wait()
     product(0, br_buf, ctx_buf)
     for i in (2, 3):
         loads[i].wait()
     product(1, n_buf, dv_buf)
-    join(0)
-    join(1)
-    hop(0, 0).start()
-    loads[4].wait()
+    launch(0)
+    for i in (4, 5, 6):
+        loads[i].wait()
+
+    def theirs(j, carry):
+        two_tiles(j, [(0, j)], True)
+        return carry
+
+    def ours(j, carry):
+        two_tiles(j, [(0, j + 2), (1, j - 2)], False)
+        return carry
+
+    lax.fori_loop(0, held // 2, theirs, 0)
     product(2, n_buf, dk_buf)
-    advance(0, 0)
-    loads[5].wait()
+    advance(0, 2)
     product(3, n_buf, dq_buf)
-    advance(0, 1)
-    join(2)
-    join(3)
-    hop(1, 0).start()
-    loads[6].wait()
-    gains[:1, :] = jnp.zeros((1, width), F32)
-    gains[1:, :] = gain_two_ref[...]
-
-    def sweep(i, carry):
-        for slot in (0, 1):
-            k = 2 * i + slot
-            if slot == 0:
-                for copy in tile_in(tile_of(k + 1), 1):
-                    copy.start()
-            else:
-
-                @pl.when(i < 3)
-                def _():
-                    for copy in tile_in(tile_of(k + 1), 0):
-                        copy.start()
-
-            finish_rows(tile_of(k), slot, k)
-
-            @pl.when(i < 2)
-            def _():
-                give(k, k).start()
-
-            @pl.when(i >= 2)
-            def _():
-                keep(k - held, k).start()
-
-        advance(0, i + 2)
-        advance(1, i)
-        return carry
-
-    lax.fori_loop(0, held, sweep, 0)
+    advance(0, 3)
+    launch(1)
+    lax.fori_loop(held // 2, held, ours, 0)
 
     partners = [
         (me + 1 - 2 * core, spot),
@@ -1159,37 +1159,39 @@
     own = ring_place(place)
     peer = (me, 1 - spot)
 
-    def over(m):
+    def over(g):
         return remote(
-            got.at[own, :, pl.ds(m * width + half, half)], across.at[:, pl.ds(m * half, half)],
-            x_send.at[m], x_recv.at[m], peer,
+            got.at[own, :, pl.ds((2 * g + 1) * width, width)], across.at[:, pl.ds(g * width, width)],
+            x_send.at[g], x_recv.at[g], peer,
         )
 
     add_gains(0).start()
     advance(0, 6, False)
     over(0).start()
-    over(1).start()
+    advance(1, 2)
     gain_round(0)
+    advance(1, 3)
+    gain_round(1)
     advance(1, 4)
-    gain_round(1)
     gain_round(2)
     advance(1, 5)
     gain_round(3)
+    advance(1, 6, False)
+    over(1).start()
     gain_round(4)
-    advance(1, 6, False)
-    over(2).start()
-    over(3).start()
     sums_ref[...] = gains[...]
+    for g in range(2):
+        over(g).wait_recv()
+        cs = pl.ds(g * width, width)
+        share_ref[:, cs] = got[own, :, pl.ds(2 * g * width, width)].astype(F32) + across[:, cs].astype(F32)
+    for g in range(2):
+        over(g).wait_send()
+        for direction in range(2):
+            for s in range(RING - 1):
+                hop(g, direction, s).wait_send()
     for m in range(4):
-        over(m).wait_recv()
-        cs = pl.ds(m * half, half)
-        share_ref[:, cs] = got[own, :, pl.ds(m * width, half)].astype(F32) + across[:, cs].astype(F32)
-    for m in range(4):
-        over(m).wait_send()
-        to_pair(m).wait_send()
-    for s in range(RING - 1):
-        hop(0, s).wait_send()
-        hop(1, s).wait_send()
+        for h in range(2):
+            to_pair(m, h).wait_send()
     for k in range(held):
         give(k, k).wait()
         keep(k, k + held).wait()
@@ -1216,11 +1218,11 @@
             pltpu.VMEM((2, FT, width), BF16), pltpu.VMEM((2, FT, width), F32), pltpu.VMEM((L // FT, FT, width), BF16),
             pltpu.VMEM((RING, 2, rows, 4 * width), BF16),
             pltpu.VMEM((RING, rows, 4 * width), BF16),
-            pltpu.VMEM((2, RING - 1, rows, 2 * width), BF16),
+            pltpu.VMEM((2, 2, RING - 1, rows, width), BF16),
             pltpu.VMEM((rows, 2 * width), BF16),
             pltpu.VMEM((2, width), F32), pltpu.VMEM((5, 2, width), F32),
-            dma((7,)), dma((2,)), dma((2,)), dma((2 * (L // FT // 2),)), dma((L // FT // 2,)), dma((4,)), dma((4,)),
-            dma((2, RING - 1)), dma((2, RING - 1)), dma((4,)), dma((4,)), dma((5,)), dma((5,)),
+            dma((7,)), dma((2,)), dma((2,)), dma((2 * (L // FT // 2),)), dma((L // FT // 2,)), dma((4, 2)), dma((4, 2)),
+            dma((2, 2, RING - 1)), dma((2, 2, RING - 1)), dma((2,)), dma((2,)), dma((5,)), dma((5,)),
         ],
         compiler_params=pltpu.CompilerParams(collective_id=1, has_side_effects=True, vmem_limit_bytes=60 * MIB),
         cost_estimate=pl.CostEstimate(flops=14 * L * width * width, bytes_accessed=80 * MIB, transcendentals=0),
@@ -1500,9 +1502,9 @@
     )
     grad_tokens = grad_tokens.astype(F32)
     g_out, g_value, g_key, g_query = jnp.split(attn_share, 4, axis=1)
-    pieces = ffn_share.reshape(rows_held, hidden // HT, 3, HT // 2).swapaxes(1, 2)
-    pieces = pieces.reshape(rows_held, 3, hidden_held).astype(F32)
-    g_gate, g_up, g_down = pieces[:, 0], pieces[:, 1], pieces[:, 2]
+    g_gate, g_up, g_down = [
+        ffn_share[:, i * hidden_held : (i + 1) * hidden_held].astype(F32) for i in range(3)
+    ]
     return (
         out, grad_tokens, gain_sums[0], g_query, g_key, g_value, g_out.T, gain_sums[1], g_gate, g_up, g_down.T,
     )

time: 762 us -> 746 us (0.979)
  Pallas kernels: 652 us -> 629 us
    pallas_call x1, Pallas kernels: 103 us -> 86.2 us  [finish(): pl.pallas_call(functools.partial(finish_kernel, devices=devices), in_spec...]
    pallas_call x1, Pallas kernels: 160 us -> 152 us  [ffn(): pl.pallas_call(functools.partial(ffn_kernel, devices=devices), grid=(tile...]
  transfers between devices with their start and end apart: 5 -> 5, of which waited for: 2 -> 2; matrix products, arithmetic and copies ran while one was open for 3% -> 3% of each run, Pallas kernels for 45% -> 44%
where the time goes in v6:
time: 746 us; the launch traced here: 735 us
  Pallas kernels  629 us (84%)
  waiting for transfers between devices  43.9 us (6%)
  other arithmetic  19.9 us (3%)
  local copies, waits for them, and re-layouts  15.5 us (2%)
  between operations  14.4 us (2%)
  starting transfers between devices  12.8 us (2%)
    pallas_call x1, Pallas kernels, ffn(): pl.pallas_call(functools.partial(ffn_kernel, devices=devices), grid=(tile...  152 us
    pallas_call x1, Pallas kernels, spread(): pl.pallas_call(spread_kernel, in_specs=[anywhere, anywhere, anywhere, vme...  143 us
    pallas_call x1, Pallas kernels, attend_back(): pl.pallas_call(functools.partial(attend_back_kernel, pair=pair), grid_spe...  116 us
    pallas_call x1, Pallas kernels, finish(): pl.pallas_call(functools.partial(finish_kernel, devices=devices), in_spec...  86.2 us
    pallas_call x1, Pallas kernels, attend(): pl.pallas_call(functools.partial(attend_kernel, pair=pair), grid_spec=plt...  68.6 us
    all_to_all x1, waiting for transfers between devices, sequence_body(): lax.all_to_all(sent, ('dp', 'tensor'), split_axis=0, concat_axis=0, tiled...  31.2 us
    pallas_call x1, Pallas kernels, project(): pl.pallas_call(project_kernel, grid=(L // ROWS,), in_specs=[row(width), p...  24.4 us
    pallas_call x1, Pallas kernels, attend_other(): pl.pallas_call(functools.partial(attend_other_kernel, pair=pair), grid_sp...  21.5 us
  transfers between devices with their start and end apart: 5, of which 2 were waited for; matrix products, arithmetic and copies ran while one was open for 3% of the time, Pallas kernels for 44%

profile of v6, /device:TPU:0, one launch (start us, length us, event | category | flops | bytes accessed | tf_op | source)
XLA Modules:
  0.0 735.2 jit_solution(4992654504785833374)
XLA Ops:
  7.2 0.0 all-gather.2.cloned.1.call-start
  7.2 0.7 convert_bitcast_fusion.1
  7.9 0.1 copy.35
  8.0 0.8 copy.36
  8.8 0.8 copy.37
  9.5 0.1 pad.16.clone
  9.6 1.6 pad_maximum_fusion.1.small_ref
  11.2 0.7 fusion.3.extra_ref
  11.9 2.0 pad_maximum_fusion.big_ref
  13.8 143.0 %spread.1 = (bf16[2,1024,1024]{2,1,0:T(8,128)(2,1)}, bf16[2,1024,512]{2,1,0:T(8,128)(2,1)}, bf16[2,1024,512]{2,1,0:T(8,128)(2,1)}, bf16[16,2,2,64,512]{4,3,2,1,0...) custom-call(bf16[2,1024,1024]{2,1,0:T(8,128)(2,1)} %tok_ref.1, bf16[2,1024,512]{2,1,0:T(8,128)(2,1)} %ck_ref.1, ...), custom_call_target="tpu_custom_call" | custom-call | bytes 314572800 | tf_op jit(solution)/shard_map/spread/pallas_call | solution.py:1414
  156.9 0.0 all-gather.2.cloned.1.call-update
  156.9 1.0 slice.46
  157.9 0.2 slice_reduce_fusion
  158.1 0.1 reshape_squeeze.11
  158.2 0.6 reshape.72.table
  158.8 5.1 pick_rows.1
  164.0 5.4 all-to-all-start
  169.3 0.0 reduce-scatter.2.cloned.1.call-start
  169.4 0.0 copy-start.4
  169.4 0.0 copy-start.2
  169.4 0.0 copy-start.3
  169.4 4.2 dynamic-slice_bitcast_fusion.1
  173.6 1.7 collective-permute-start
  175.4 0.6 dynamic_slice.16
  175.9 0.1 copy.34
  176.0 0.1 reshape_squeeze.10
  176.1 0.1 copy.33
  176.2 0.1 reshape_squeeze.9
  176.3 1.3 pad_add_fusion.meta
  177.6 0.2 fusion.4
  177.7 0.6 fusion.9
  178.4 24.4 %project.1 = (bf16[2048,1024]{1,0:T(8,128)(2,1)}, bf16[2048,3072]{1,0:T(8,128)(2,1)}) custom-call(bf16[2048,1024]{1,0:T(8,128)(2,1)} %bitcast.24, f32[1,1024]{1,0:T(1,128)} %get-tuple-element.91.gain_ref, bf16[1024,3200]{1,0:T(8,128)(2,1)} %get-tuple-element.52.w_ref), custom_call_target="tpu_custom_call" | custom-call | flops 12884901888 | bytes 27262976 | tf_op jit(solution)/shard_map/project/pallas_call | solution.py:709
  202.8 68.6 %attend.1 = (f32[2048,1024]{1,0:T(8,128)}, f32[2048,1024]{1,0:T(8,128)}) custom-call(s32[130]{0:T(256)} %pad_add_fusion.meta, bf16[2048,3072]{1,0:T(8,128)(2,1)} %get-tuple-element.53.q_ref.k_ref.v_ref, bf16[2048,3072]{1,0:T(8,128)(2,1)} %get-tuple-element.53.q_ref.k_ref.v_ref, bf16[2048,3072]{1,0:T(8,128)(2,1)} %get-tuple-element.53.q_ref.k_ref.v_ref, ...), custom_call_target="tpu_custom_call" | custom-call | flops 40265318400 | bytes 31457280 | tf_op jit(solution)/shard_map/attend/pallas_call | solution.py:625
  271.4 4.9 maximum_select_fusion.g_ref
  276.3 31.2 %all-to-all-done = bf16[32,128,512]{2,1,0:T(8,128)(2,1)} async-done(((bf16[32,128,512]{2,1,0:T(8,128)(2,1)}), bf16[32,128,512]{2,1,0:T(8,128)(2,1)}, u32[]{:S(2)}, u32[]{:S(2)}) %all-to-all-start) | async-done | bytes 4194336 | tf_op jit(solution)/shard_map/all_to_all | solution.py:1477
  307.4 21.5 %attend_other.1 = (bf16[2048,1024]{1,0:T(8,128)(2,1)}, f32[2048,1024]{1,0:T(8,128)}) custom-call(s32[130]{0:T(256)} %pad_add_fusion.meta, bf16[2048,3072]{1,0:T(8,128)(2,1)} %get-tuple-element.53.q_ref.k_ref.v_ref, bf16[16,2,2,64,512]{4,3,2,1,0:T(8,128)(2,1)} %bitcast.8.pk_ref.pv_ref, bf16[16,2,2,64,512]{4,3,2,1,0:T(8,128)(2,1)} %bitcast.8.pk_ref.pv_ref, ...), custom_call_target="tpu_custom_call" | custom-call | flops 2147483648 | bytes 31457280 | tf_op jit(solution)/shard_map/attend_other/pallas_call | solution.py:648
  329.0 12.7 %all-gather.2.cloned.1.call-done.w_ref.wg0.wg1.wu0.wu1.wd0.wd1.wo_ref = bf16[1024,9472]{1,0:T(8,128)(2,1)} async-done(((bf16[64,9472]{1,0:T(8,128)(2,1)}), bf16[1024,9472]{1,0:T(8,128)(2,1)}) %all-gather.2.cloned.1.call-update) | async-done | bytes 19398672 | tf_op jit(solution)/shard_map/all_gather | solution.py:1470
  341.6 11.5 %mix.1 = (f32[2048,1024]{1,0:T(8,128)}, bf16[2048,1024]{1,0:T(8,128)(2,1)}) custom-call(bf16[2048,1024]{1,0:T(8,128)(2,1)} %bitcast.25, bf16[2048,1024]{1,0:T(8,128)(2,1)} %get-tuple-element.59.ctx_ref, f32[1,1024]{1,0:T(1,128)} %get-tuple-element.90.gain_ref, bf16[1024,9472]{1,0:T(8,128)(2,1)} %all-gather.2.cloned.1.call-done.w_ref.wg0.wg1.wu0.wu1.wd0.wd1.wo_ref), custom_call_target="tpu_custom_call" | custom-call | flops 4294967296 | bytes 23068672 | tf_op jit(solution)/shard_map/mix/pallas_call | solution.py:731
  353.1 152.4 %ffn.1 = (bf16[512,4224]{1,0:T(8,128)(2,1)}, f32[1,1024]{1,0:T(1,128)}, bf16[2048,1024]{1,0:T(8,128)(2,1)}, f32[2048,1024]{1,0:T(8,128)}, bf16[2048,1024]{1,0:T(8,128)(2,1)}, /*index=5*/bf16[2048,1024]{1,0:T(8,128)(2,1)}) custom-call(bf16[2048,1024]{1,0:T(8,128)(2,1)} %get-tuple-element.61.n_ref, bf16[2048,1024]{1,0:T(8,128)(2,1)} %maximum_select_fusion.g_ref, ...), custom_call_target="tpu_custom_call" | custom-call | flops 106300440576 | bytes 62914560 | tf_op jit(solution)/shard_map/ffn/pallas_call | solution.py:940
  505.5 0.0 reduce-scatter.2.cloned.1.call-update
  505.5 5.6 all-to-all-start.1
  511.2 115.9 %attend_back.1 = (bf16[2048,1024]{1,0:T(8,128)(2,1)}, bf16[2048,1024]{1,0:T(8,128)(2,1)}, bf16[2048,1024]{1,0:T(8,128)(2,1)}) custom-call(s32[130]{0:T(256)} %pad_add_fusion.meta, bf16[2048,3072]{1,0:T(8,128)(2,1)} %get-tuple-element.53.q_ref.k_ref.v_ref, bf16[2048,3072]{1,0:T(8,128)(2,1)} %get-tuple-element.53.q_ref.k_ref.v_ref, ...), custom_call_target="tpu_custom_call" | custom-call | flops 47815065600 | bytes 41943040 | tf_op jit(solution)/shard_map/attend_back/pallas_call | solution.py:673
  627.1 86.2 %finish.1 = (bf16[2,1024,1024]{2,1,0:T(8,128)(2,1)}, f32[2,1024]{1,0:T(2,128)}, f32[64,2048]{1,0:T(8,128)}) custom-call(bf16[2048,1024]{1,0:T(8,128)(2,1)} %bitcast.26, f32[2048,1024]{1,0:T(8,128)} %get-tuple-element.68.gm_ref, bf16[2048,1024]{1,0:T(8,128)(2,1)} %get-tuple-element.69.n_ref, bf16[2048,1024]{1,0:T(8,128)(2,1)} %get-tuple-element.59.ctx_ref, ...), custom_call_target="tpu_custom_call" | custom-call | flops 30064771072 | bytes 83886080 | tf_op jit(solution)/shard_map/finish/pallas_call | solution.py:1207
  713.3 6.7 convert_element_type.22
  720.0 0.6 fusion.8
  720.6 0.8 slice_bitcast_fusion
  721.4 2.1 convert_bitcast_fusion
  723.5 4.6 copy.39
  (13 shorter events, 0.0 us)
Async XLA Ops:
  7.2 334.5 %all-gather.2.cloned.1.call-start = ((), (), s32[]{:S(2)}) async-start(), calls=%async_computation.3 | async-start | bytes 20611072 | tf_op jit(solution)/shard_map/all_gather | solution.py:1470
  164.0 143.5 %all-to-all-start = ((bf16[32,128,512]{2,1,0:T(8,128)(2,1)}), bf16[32,128,512]{2,1,0:T(8,128)(2,1)}, u32[]{:S(2)}, u32[]{:S(2)}) async-start(bf16[32,128,512]{2,1,0:T(8,128)(2,1)} %pick_rows.1), calls=%async_computation | async-start | bytes 8388608 | tf_op jit(solution)/shard_map/all_to_all | solution.py:1477
  169.3 552.1 %reduce-scatter.2.cloned.1.call-start = ((), (), s32[]{:S(2)}) async-start(), calls=%async_computation.4 | async-start | bytes 4866048 | tf_op jit(solution)/shard_map/reduce_scatter | solution.py:1493
  169.4 6.0 copy-start.4
  169.4 6.5 copy-start.2
  169.4 6.5 copy-start.3
  173.6 97.7 %collective-permute-start = (bf16[1024,1024]{1,0:T(8,128)(2,1)}, bf16[1024,1024]{1,0:T(8,128)(2,1)}, u32[]{:S(2)}, u32[]{:S(2)}) collective-permute-start(bf16[1024,1024]{1,0:T(8,128)(2,1)} %get-tuple-element.80), channel_id=1, source_target_pairs={{0,1},{1,0},{2,3},{3,2},{4,5},{5,4},{6,7},{7,6},{8,9},{9,8},{10,11... | collective-permute-start | bytes 6291464 | tf_op jit(solution)/shard_map/ppermute | solution.py:1440
  505.5 121.5 %all-to-all-start.1 = ((bf16[2,1024,1024]{2,1,0:T(8,128)(2,1)}), bf16[2,1024,1024]{2,1,0:T(8,128)(2,1)}, u32[]{:S(2)}, u32[]{:S(2)}) async-start(bf16[2,1024,1024]{2,1,0:T(8,128)(2,1)} %bitcast.22), calls=%async_computation.1 | async-start | bytes 8388608 | tf_op jit(solution)/shard_map/all_to_all | solution.py:1497
  713.3 6.7 copy-start.1
  713.3 7.3 copy-start
Sparse Core Ops, SparseCore 0:
  157.0 184.5 all-gather.1
  505.7 96.1 reduce-scatter.1

commit v7 on v6

--- a/solution.py
+++ b/solution.py
@@ -741,8 +741,6 @@
 
 
 RING = 8
-RIGHT = RING // 2
-LEFT = RING - 1 - RIGHT
 
 
 def ring_place(p):
@@ -1261,7 +1259,7 @@
 def spread_kernel(
     tok_ref, ck_ref, cv_ref, small_ref, extra_ref, big_ref,
     x_ref, ok_ref, ov_ref, held_ref, first_ref, second_ref,
-    tok_buf, k_buf, v_buf, local_sem, x_send, x_recv, all_send, all_recv, ring_send, ring_recv, pair_send, pair_recv,
+    tok_buf, k_buf, v_buf, local_sem, x_send, x_recv, all_send, all_recv, ring_send, ring_recv, line_send, line_recv, pair_send, pair_recv,
 ):
     me = lax.axis_index("dp")
     spot = lax.axis_index("tensor")
@@ -1270,11 +1268,6 @@
     rows, cols = small_ref.shape[0], small_ref.shape[1] // 3
     core = me % 2
     z, y = me // 4, (me // 2) % 2
-    place = z + y * (7 - 2 * z)
-
-    def at_place(p):
-        yy = p // 4
-        return (p + yy * (7 - 2 * p)) * 4 + yy * 2
 
     def target(dp, tensor):
         return (dp, tensor)
@@ -1349,31 +1342,51 @@
     for copy in weight_copies:
         copy.wait_recv()
 
-    def block(p, c):
-        return first_ref.at[pl.ds(pl.multiple_of((at_place(p) + c) * rows, rows), rows), :]
-
-    ahead = (place + 1) % RING
-    behind = (place + RING - 1) % RING
-
-    def hop(s, direction):
-        p = (place + RING - (s - 1)) % RING if direction == 0 else (place + s - 1) % RING
-        to = ahead if direction == 0 else behind
+    def block(zz, yy, c):
+        return first_ref.at[pl.ds(pl.multiple_of((zz * 4 + yy * 2 + c) * rows, rows), rows), :]
+
+    def along(s, direction):
+        zz = z - (s - 1) if direction == 0 else z + (s - 1)
+        to = z + 1 if direction == 0 else z - 1
         k = (s - 1) * 2 + direction
-        return remote(block(p, core), block(p, core), ring_send.at[k], ring_recv.at[k], target(at_place(to) + core, spot))
-
-    def to_pair(i, p):
-        return remote(block(p, core), block(p, core), pair_send.at[i], pair_recv.at[i], target(at_place(place) + 1 - core, spot))
-
-    hops = [hop(1, 0), hop(1, 1)]
-    for copy in hops:
-        copy.start()
-    pairs = [to_pair(0, place)]
-    pairs[0].start()
+        held = block(zz, y, core)
+        return remote(held, held, ring_send.at[k], ring_recv.at[k], target(to * 4 + y * 2 + core, spot))
+
+    def sends(s, direction):
+        return (z < 3) & (z - (s - 1) >= 0) if direction == 0 else (z > 0) & (z + (s - 1) <= 3)
+
+    def gets(s, direction):
+        return z - s >= 0 if direction == 0 else z + s <= 3
+
+    def to_line(zz):
+        held = block(zz, y, core)
+        return remote(held, held, line_send.at[zz], line_recv.at[zz], target(z * 4 + (1 - y) * 2 + core, spot))
+
+    def to_pair(zz, yy):
+        held = block(zz, yy, core)
+        k = zz * 2 + yy
+        return remote(held, held, pair_send.at[k], pair_recv.at[k], target(me + 1 - 2 * core, spot))
+
+    for direction in range(2):
+
+        @pl.when(sends(1, direction))
+        def _():
+            along(1, direction).start()
+
+    to_line(z).start()
+    to_pair(z, y).start()
     copies = []
-    for d in range(1, devices):
-        for copy in to_device(d, (me + d) % devices):
-            copy.start()
-            copies.append(copy)
+    order = [8, 4, 12, 6, 10, 2, 14, 9, 5, 13, 1, 7, 11, 3, 15]
+    assert sorted(order) == list(range(1, devices))
+
+    def some(count):
+        for d in order[:count]:
+            for copy in to_device(d, (me + d) % devices):
+                copy.start()
+                copies.append(copy)
+        del order[:count]
+
+    some(3)
     chunk = pl.ds(pl.multiple_of(me * CBLOCK, CBLOCK), CBLOCK)
     kept = [
         pltpu.make_async_copy(ck_ref.at[:, chunk, :], held_ref.at[me, :, 0], local_sem.at[10]),
@@ -1384,22 +1397,42 @@
     for load, store in zip(loads, stores):
         load.wait()
         store.start()
-    for s in range(1, RIGHT + 1):
+    for s in range(1, 4):
         for direction in range(2):
-            if direction == 1 and s > LEFT:
-                continue
-            hops[(s - 1) * 2 + direction].wait_recv()
-            p = (place + RING - s) % RING if direction == 0 else (place + s) % RING
-            if s < (RIGHT if direction == 0 else LEFT):
-                nxt = hop(s + 1, direction)
-                nxt.start()
-                hops.append(nxt)
-            pair = to_pair(len(pairs), p)
-            pair.start()
-            pairs.append(pair)
-    for copy in weight_copies + hops:
+
+            @pl.when(gets(s, direction))
+            def _():
+                along(s, direction).wait_recv()
+                zz = z - s if direction == 0 else z + s
+                if s < 3:
+
+                    @pl.when(sends(s + 1, direction))
+                    def _():
+                        along(s + 1, direction).start()
+
+                to_line(zz).start()
+                to_pair(zz, y).start()
+
+        some(2)
+    for zz in range(4):
+        to_line(zz).wait_recv()
+        to_pair(zz, 1 - y).start()
+        some(1)
+    some(devices)
+    for s in range(1, 4):
+        for direction in range(2):
+
+            @pl.when(sends(s, direction))
+            def _():
+                along(s, direction).wait_send()
+
+    for zz in range(4):
+        to_line(zz).wait_send()
+        for yy in range(2):
+            to_pair(zz, yy).wait()
+    for copy in weight_copies:
         copy.wait_send()
-    for copy in pairs + x_copies + copies:
+    for copy in x_copies + copies:
         copy.wait()
     for copy in stores + own_cols + kept:
         copy.wait()
@@ -1428,7 +1461,7 @@
             pltpu.VMEM((CACHE_LEN, cols), BF16),
             pltpu.VMEM((CACHE_LEN, cols), BF16),
             dma((12,)), dma((10,)), dma((10,)), dma((2, devices)), dma((2, devices)),
-            dma((RING - 1,)), dma((RING - 1,)), dma((RING,)), dma((RING,)),
+            dma((6,)), dma((6,)), dma((4,)), dma((4,)), dma((8,)), dma((8,)),
         ],
         compiler_params=pltpu.CompilerParams(collective_id=0, has_side_effects=True, vmem_limit_bytes=60 * MIB),
         cost_estimate=pl.CostEstimate(flops=0, bytes_accessed=300 * MIB, transcendentals=0),

time: 746 us -> 725 us (0.972)
  Pallas kernels: 629 us -> 614 us
    pallas_call x1, Pallas kernels: 143 us -> 130 us  [spread(): pl.pallas_call(spread_kernel, in_specs=[anywhere, anywhere, anywhere, vme...]
where the time goes in v7:
time: 725 us; the launch traced here: 720 us
  Pallas kernels  614 us (85%)
  waiting for transfers between devices  43.7 us (6%)
  other arithmetic  19.9 us (3%)
  local copies, waits for them, and re-layouts  15.5 us (2%)
  between operations  14.4 us (2%)
  starting transfers between devices  12.2 us (2%)
    pallas_call x1, Pallas kernels, ffn(): pl.pallas_call(functools.partial(ffn_kernel, devices=devices), grid=(tile...  152 us
    pallas_call x1, Pallas kernels, spread(): pl.pallas_call(spread_kernel, in_specs=[anywhere, anywhere, anywhere, vme...  130 us
    pallas_call x1, Pallas kernels, attend_back(): pl.pallas_call(functools.partial(attend_back_kernel, pair=pair), grid_spe...  116 us
    pallas_call x1, Pallas kernels, finish(): pl.pallas_call(functools.partial(finish_kernel, devices=devices), in_spec...  84.7 us
    pallas_call x1, Pallas kernels, attend(): pl.pallas_call(functools.partial(attend_kernel, pair=pair), grid_spec=plt...  68.6 us
    all_to_all x1, waiting for transfers between devices, sequence_body(): lax.all_to_all(sent, ('dp', 'tensor'), split_axis=0, concat_axis=0, tiled...  30.9 us
    pallas_call x1, Pallas kernels, project(): pl.pallas_call(project_kernel, grid=(L // ROWS,), in_specs=[row(width), p...  24.4 us
    pallas_call x1, Pallas kernels, attend_other(): pl.pallas_call(functools.partial(attend_other_kernel, pair=pair), grid_sp...  21.5 us
  transfers between devices with their start and end apart: 5, of which 2 were waited for; matrix products, arithmetic and copies ran while one was open for 3% of the time, Pallas kernels for 44%

profile of v7, /device:TPU:0, one launch (start us, length us, event | category | flops | bytes accessed | tf_op | source)
XLA Modules:
  0.0 719.9 jit_solution(1131033507624133776)
XLA Ops:
  7.2 0.0 all-gather.2.cloned.1.call-start
  7.2 0.7 convert_bitcast_fusion.1
  7.9 0.1 copy.35
  8.0 0.8 copy.36
  8.8 0.8 copy.37
  9.5 0.1 pad.16.clone
  9.6 1.6 pad_maximum_fusion.1.small_ref
  11.2 0.7 fusion.3.extra_ref
  11.9 2.0 pad_maximum_fusion.big_ref
  13.8 129.9 %spread.1 = (bf16[2,1024,1024]{2,1,0:T(8,128)(2,1)}, bf16[2,1024,512]{2,1,0:T(8,128)(2,1)}, bf16[2,1024,512]{2,1,0:T(8,128)(2,1)}, bf16[16,2,2,64,512]{4,3,2,1,0...) custom-call(bf16[2,1024,1024]{2,1,0:T(8,128)(2,1)} %tok_ref.1, bf16[2,1024,512]{2,1,0:T(8,128)(2,1)} %ck_ref.1, ...), custom_call_target="tpu_custom_call" | custom-call | bytes 314572800 | tf_op jit(solution)/shard_map/spread/pallas_call | solution.py:1447
  143.7 0.0 all-gather.2.cloned.1.call-update
  143.7 1.0 slice.46
  144.7 0.2 slice_reduce_fusion
  144.9 0.1 reshape_squeeze.11
  145.0 0.6 reshape.72.table
  145.6 5.3 pick_rows.1
  150.9 4.5 all-to-all-start
  155.4 0.3 reduce-scatter.2.cloned.1.call-start
  155.8 0.0 copy-start.4
  155.8 0.0 copy-start.2
  155.8 0.0 copy-start.3
  155.8 4.2 dynamic-slice_bitcast_fusion.1
  160.0 1.7 collective-permute-start
  161.7 0.6 dynamic_slice.16
  162.3 0.1 copy.34
  162.4 0.1 reshape_squeeze.10
  162.5 0.1 copy.33
  162.6 0.1 reshape_squeeze.9
  162.7 1.3 pad_add_fusion.meta
  164.0 0.2 fusion.4
  164.1 0.6 fusion.9
  164.8 24.4 %project.1 = (bf16[2048,1024]{1,0:T(8,128)(2,1)}, bf16[2048,3072]{1,0:T(8,128)(2,1)}) custom-call(bf16[2048,1024]{1,0:T(8,128)(2,1)} %bitcast.24, f32[1,1024]{1,0:T(1,128)} %get-tuple-element.91.gain_ref, bf16[1024,3200]{1,0:T(8,128)(2,1)} %get-tuple-element.52.w_ref), custom_call_target="tpu_custom_call" | custom-call | flops 12884901888 | bytes 27262976 | tf_op jit(solution)/shard_map/project/pallas_call | solution.py:709
  189.1 68.6 %attend.1 = (f32[2048,1024]{1,0:T(8,128)}, f32[2048,1024]{1,0:T(8,128)}) custom-call(s32[130]{0:T(256)} %pad_add_fusion.meta, bf16[2048,3072]{1,0:T(8,128)(2,1)} %get-tuple-element.53.q_ref.k_ref.v_ref, bf16[2048,3072]{1,0:T(8,128)(2,1)} %get-tuple-element.53.q_ref.k_ref.v_ref, bf16[2048,3072]{1,0:T(8,128)(2,1)} %get-tuple-element.53.q_ref.k_ref.v_ref, ...), custom_call_target="tpu_custom_call" | custom-call | flops 40265318400 | bytes 31457280 | tf_op jit(solution)/shard_map/attend/pallas_call | solution.py:625
  257.7 4.9 maximum_select_fusion.g_ref
  262.6 30.9 %all-to-all-done = bf16[32,128,512]{2,1,0:T(8,128)(2,1)} async-done(((bf16[32,128,512]{2,1,0:T(8,128)(2,1)}), bf16[32,128,512]{2,1,0:T(8,128)(2,1)}, u32[]{:S(2)}, u32[]{:S(2)}) %all-to-all-start) | async-done | bytes 4194336 | tf_op jit(solution)/shard_map/all_to_all | solution.py:1510
  293.5 21.5 %attend_other.1 = (bf16[2048,1024]{1,0:T(8,128)(2,1)}, f32[2048,1024]{1,0:T(8,128)}) custom-call(s32[130]{0:T(256)} %pad_add_fusion.meta, bf16[2048,3072]{1,0:T(8,128)(2,1)} %get-tuple-element.53.q_ref.k_ref.v_ref, bf16[16,2,2,64,512]{4,3,2,1,0:T(8,128)(2,1)} %bitcast.8.pk_ref.pv_ref, bf16[16,2,2,64,512]{4,3,2,1,0:T(8,128)(2,1)} %bitcast.8.pk_ref.pv_ref, ...), custom_call_target="tpu_custom_call" | custom-call | flops 2147483648 | bytes 31457280 | tf_op jit(solution)/shard_map/attend_other/pallas_call | solution.py:648
  315.0 12.7 %all-gather.2.cloned.1.call-done.w_ref.wg0.wg1.wu0.wu1.wd0.wd1.wo_ref = bf16[1024,9472]{1,0:T(8,128)(2,1)} async-done(((bf16[64,9472]{1,0:T(8,128)(2,1)}), bf16[1024,9472]{1,0:T(8,128)(2,1)}) %all-gather.2.cloned.1.call-update) | async-done | bytes 19398672 | tf_op jit(solution)/shard_map/all_gather | solution.py:1503
  327.8 11.5 %mix.1 = (f32[2048,1024]{1,0:T(8,128)}, bf16[2048,1024]{1,0:T(8,128)(2,1)}) custom-call(bf16[2048,1024]{1,0:T(8,128)(2,1)} %bitcast.25, bf16[2048,1024]{1,0:T(8,128)(2,1)} %get-tuple-element.59.ctx_ref, f32[1,1024]{1,0:T(1,128)} %get-tuple-element.90.gain_ref, bf16[1024,9472]{1,0:T(8,128)(2,1)} %all-gather.2.cloned.1.call-done.w_ref.wg0.wg1.wu0.wu1.wd0.wd1.wo_ref), custom_call_target="tpu_custom_call" | custom-call | flops 4294967296 | bytes 23068672 | tf_op jit(solution)/shard_map/mix/pallas_call | solution.py:731
  339.3 152.5 %ffn.1 = (bf16[512,4224]{1,0:T(8,128)(2,1)}, f32[1,1024]{1,0:T(1,128)}, bf16[2048,1024]{1,0:T(8,128)(2,1)}, f32[2048,1024]{1,0:T(8,128)}, bf16[2048,1024]{1,0:T(8,128)(2,1)}, /*index=5*/bf16[2048,1024]{1,0:T(8,128)(2,1)}) custom-call(bf16[2048,1024]{1,0:T(8,128)(2,1)} %get-tuple-element.61.n_ref, bf16[2048,1024]{1,0:T(8,128)(2,1)} %maximum_select_fusion.g_ref, ...), custom_call_target="tpu_custom_call" | custom-call | flops 106300440576 | bytes 62914560 | tf_op jit(solution)/shard_map/ffn/pallas_call | solution.py:938
  491.8 0.0 reduce-scatter.2.cloned.1.call-update
  491.8 5.6 all-to-all-start.1
  497.4 115.9 %attend_back.1 = (bf16[2048,1024]{1,0:T(8,128)(2,1)}, bf16[2048,1024]{1,0:T(8,128)(2,1)}, bf16[2048,1024]{1,0:T(8,128)(2,1)}) custom-call(s32[130]{0:T(256)} %pad_add_fusion.meta, bf16[2048,3072]{1,0:T(8,128)(2,1)} %get-tuple-element.53.q_ref.k_ref.v_ref, bf16[2048,3072]{1,0:T(8,128)(2,1)} %get-tuple-element.53.q_ref.k_ref.v_ref, ...), custom_call_target="tpu_custom_call" | custom-call | flops 47815065600 | bytes 41943040 | tf_op jit(solution)/shard_map/attend_back/pallas_call | solution.py:673
  613.3 84.7 %finish.1 = (bf16[2,1024,1024]{2,1,0:T(8,128)(2,1)}, f32[2,1024]{1,0:T(2,128)}, f32[64,2048]{1,0:T(8,128)}) custom-call(bf16[2048,1024]{1,0:T(8,128)(2,1)} %bitcast.26, f32[2048,1024]{1,0:T(8,128)} %get-tuple-element.68.gm_ref, bf16[2048,1024]{1,0:T(8,128)(2,1)} %get-tuple-element.69.n_ref, bf16[2048,1024]{1,0:T(8,128)(2,1)} %get-tuple-element.59.ctx_ref, ...), custom_call_target="tpu_custom_call" | custom-call | flops 30064771072 | bytes 83886080 | tf_op jit(solution)/shard_map/finish/pallas_call | solution.py:1205
  698.0 6.7 convert_element_type.22
  704.7 0.6 fusion.8
  705.3 0.8 slice_bitcast_fusion
  706.1 2.1 convert_bitcast_fusion
  708.2 4.6 copy.39
  (13 shorter events, 0.0 us)
Async XLA Ops:
  7.2 320.6 %all-gather.2.cloned.1.call-start = ((), (), s32[]{:S(2)}) async-start(), calls=%async_computation.3 | async-start | bytes 20611072 | tf_op jit(solution)/shard_map/all_gather | solution.py:1503
  150.9 142.6 %all-to-all-start = ((bf16[32,128,512]{2,1,0:T(8,128)(2,1)}), bf16[32,128,512]{2,1,0:T(8,128)(2,1)}, u32[]{:S(2)}, u32[]{:S(2)}) async-start(bf16[32,128,512]{2,1,0:T(8,128)(2,1)} %pick_rows.1), calls=%async_computation | async-start | bytes 8388608 | tf_op jit(solution)/shard_map/all_to_all | solution.py:1510
  155.4 550.7 %reduce-scatter.2.cloned.1.call-start = ((), (), s32[]{:S(2)}) async-start(), calls=%async_computation.4 | async-start | bytes 4866048 | tf_op jit(solution)/shard_map/reduce_scatter | solution.py:1526
  155.8 6.0 copy-start.4
  155.8 6.6 copy-start.2
  155.8 6.6 copy-start.3
  160.0 97.7 %collective-permute-start = (bf16[1024,1024]{1,0:T(8,128)(2,1)}, bf16[1024,1024]{1,0:T(8,128)(2,1)}, u32[]{:S(2)}, u32[]{:S(2)}) collective-permute-start(bf16[1024,1024]{1,0:T(8,128)(2,1)} %get-tuple-element.80), channel_id=1, source_target_pairs={{0,1},{1,0},{2,3},{3,2},{4,5},{5,4},{6,7},{7,6},{8,9},{9,8},{10,11... | collective-permute-start | bytes 6291464 | tf_op jit(solution)/shard_map/ppermute | solution.py:1473
  491.8 121.5 %all-to-all-start.1 = ((bf16[2,1024,1024]{2,1,0:T(8,128)(2,1)}), bf16[2,1024,1024]{2,1,0:T(8,128)(2,1)}, u32[]{:S(2)}, u32[]{:S(2)}) async-start(bf16[2,1024,1024]{2,1,0:T(8,128)(2,1)} %bitcast.22), calls=%async_computation.1 | async-start | bytes 8388608 | tf_op jit(solution)/shard_map/all_to_all | solution.py:1530
  698.0 6.7 copy-start.1
  698.0 7.3 %copy-start = (f32[64,2048]{1,0:T(8,128)S(1)}, f32[64,2048]{1,0:T(8,128)}, u32[]{:S(2)}) copy-start(f32[64,2048]{1,0:T(8,128)} %get-tuple-element.77) | copy-start | bytes 1572868
Sparse Core Ops, SparseCore 0:
  143.9 183.8 all-gather.1
  491.9 95.9 reduce-scatter.1

commit v8 on v7

--- a/solution.py
+++ b/solution.py
@@ -900,19 +900,22 @@
             copy.start()
         return carry
 
-    @pl.when(tile == tiles - 1)
+    @pl.when(tile == tiles - 2)
     def _():
         wo_copy.start()
         fetch(0).start()
+
+    @pl.when(tile == tiles - 1)
+    def _():
         gg_ref[...] = jnp.zeros_like(gg_ref)
         to_peer(tile - 2).wait()
         settle(tile - 2)
         wo_copy.wait()
-        lax.fori_loop(0, 4, unmix, 0)
+        lax.fori_loop(0, 3, unmix, 0)
         to_pair(tile).wait()
         join(tile)
         to_peer(tile).start()
-        lax.fori_loop(4, L // UT, unmix, 0)
+        lax.fori_loop(3, L // UT, unmix, 0)
         to_peer(tile - 1).wait()
         settle(tile - 1)
         to_peer(tile).wait()
@@ -1413,7 +1416,7 @@
                 to_line(zz).start()
                 to_pair(zz, y).start()
 
-        some(2)
+        some(3)
     for zz in range(4):
         to_line(zz).wait_recv()
         to_pair(zz, 1 - y).start()

time: 725 us -> 722 us (level)
    pallas_call x1, Pallas kernels: 84.7 us -> 94 us  [finish(): pl.pallas_call(functools.partial(finish_kernel, devices=devices), in_spec...]
where the time goes in v8:
time: 722 us; the launch traced here: 718 us
  Pallas kernels  611 us (85%)
  waiting for transfers between devices  46.9 us (6%)
  other arithmetic  19.9 us (3%)
  local copies, waits for them, and re-layouts  15.3 us (2%)
  between operations  14.4 us (2%)
  starting transfers between devices  11.2 us (2%)
    pallas_call x1, Pallas kernels, ffn(): pl.pallas_call(functools.partial(ffn_kernel, devices=devices), grid=(tile...  153 us
    pallas_call x1, Pallas kernels, spread(): pl.pallas_call(spread_kernel, in_specs=[anywhere, anywhere, anywhere, vme...  128 us
    pallas_call x1, Pallas kernels, attend_back(): pl.pallas_call(functools.partial(attend_back_kernel, pair=pair), grid_spe...  109 us
    pallas_call x1, Pallas kernels, finish(): pl.pallas_call(functools.partial(finish_kernel, devices=devices), in_spec...  94 us
    pallas_call x1, Pallas kernels, attend(): pl.pallas_call(functools.partial(attend_kernel, pair=pair), grid_spec=plt...  64.6 us
    all_to_all x1, waiting for transfers between devices, sequence_body(): lax.all_to_all(sent, ('dp', 'tensor'), split_axis=0, concat_axis=0, tiled...  35.4 us
    pallas_call x1, Pallas kernels, project(): pl.pallas_call(project_kernel, grid=(L // ROWS,), in_specs=[row(width), p...  24.3 us
    pallas_call x1, Pallas kernels, attend_other(): pl.pallas_call(functools.partial(attend_other_kernel, pair=pair), grid_sp...  21.1 us
  transfers between devices with their start and end apart: 5, of which 2 were waited for; matrix products, arithmetic and copies ran while one was open for 3% of the time, Pallas kernels for 44%

profile of v8, /device:TPU:0, one launch (start us, length us, event | category | flops | bytes accessed | tf_op | source)
XLA Modules:
  0.0 718.5 jit_solution(7497513892964852538)
XLA Ops:
  7.2 0.0 all-gather.2.cloned.1.call-start
  7.2 0.7 convert_bitcast_fusion.1
  7.9 0.1 copy.35
  8.0 0.8 copy.36
  8.8 0.8 copy.37
  9.5 0.1 pad.16.clone
  9.6 1.6 pad_maximum_fusion.1.small_ref
  11.2 0.7 fusion.3.extra_ref
  11.9 2.0 pad_maximum_fusion.big_ref
  13.8 128.0 %spread.1 = (bf16[2,1024,1024]{2,1,0:T(8,128)(2,1)}, bf16[2,1024,512]{2,1,0:T(8,128)(2,1)}, bf16[2,1024,512]{2,1,0:T(8,128)(2,1)}, bf16[16,2,2,64,512]{4,3,2,1,0...) custom-call(bf16[2,1024,1024]{2,1,0:T(8,128)(2,1)} %tok_ref.1, bf16[2,1024,512]{2,1,0:T(8,128)(2,1)} %ck_ref.1, ...), custom_call_target="tpu_custom_call" | custom-call | bytes 314572800 | tf_op jit(solution)/shard_map/spread/pallas_call | solution.py:1450
  141.8 0.0 all-gather.2.cloned.1.call-update
  141.8 1.0 slice.46
  142.8 0.2 slice_reduce_fusion
  143.0 0.1 reshape_squeeze.11
  143.1 0.6 reshape.72.table
  143.7 5.6 pick_rows.1
  149.4 3.6 all-to-all-start
  153.0 0.3 reduce-scatter.2.cloned.1.call-start
  153.4 0.0 copy-start.4
  153.4 0.0 copy-start.2
  153.4 0.0 copy-start.3
  153.4 4.1 dynamic-slice_bitcast_fusion.1
  157.5 1.6 collective-permute-start
  159.0 0.6 dynamic_slice.16
  159.6 0.1 copy.34
  159.7 0.1 reshape_squeeze.10
  159.8 0.1 copy.33
  159.9 0.1 reshape_squeeze.9
  160.0 1.3 pad_add_fusion.meta
  161.3 0.2 fusion.4
  161.4 0.6 fusion.9
  162.1 24.3 %project.1 = (bf16[2048,1024]{1,0:T(8,128)(2,1)}, bf16[2048,3072]{1,0:T(8,128)(2,1)}) custom-call(bf16[2048,1024]{1,0:T(8,128)(2,1)} %bitcast.24, f32[1,1024]{1,0:T(1,128)} %get-tuple-element.91.gain_ref, bf16[1024,3200]{1,0:T(8,128)(2,1)} %get-tuple-element.52.w_ref), custom_call_target="tpu_custom_call" | custom-call | flops 12884901888 | bytes 27262976 | tf_op jit(solution)/shard_map/project/pallas_call | solution.py:709
  186.4 64.6 %attend.1 = (f32[2048,1024]{1,0:T(8,128)}, f32[2048,1024]{1,0:T(8,128)}) custom-call(s32[130]{0:T(256)} %pad_add_fusion.meta, bf16[2048,3072]{1,0:T(8,128)(2,1)} %get-tuple-element.53.q_ref.k_ref.v_ref, bf16[2048,3072]{1,0:T(8,128)(2,1)} %get-tuple-element.53.q_ref.k_ref.v_ref, bf16[2048,3072]{1,0:T(8,128)(2,1)} %get-tuple-element.53.q_ref.k_ref.v_ref, ...), custom_call_target="tpu_custom_call" | custom-call | flops 40265318400 | bytes 31457280 | tf_op jit(solution)/shard_map/attend/pallas_call | solution.py:625
  251.0 4.9 maximum_select_fusion.g_ref
  255.9 35.4 %all-to-all-done = bf16[32,128,512]{2,1,0:T(8,128)(2,1)} async-done(((bf16[32,128,512]{2,1,0:T(8,128)(2,1)}), bf16[32,128,512]{2,1,0:T(8,128)(2,1)}, u32[]{:S(2)}, u32[]{:S(2)}) %all-to-all-start) | async-done | bytes 4194336 | tf_op jit(solution)/shard_map/all_to_all | solution.py:1513
  291.2 21.1 %attend_other.1 = (bf16[2048,1024]{1,0:T(8,128)(2,1)}, f32[2048,1024]{1,0:T(8,128)}) custom-call(s32[130]{0:T(256)} %pad_add_fusion.meta, bf16[2048,3072]{1,0:T(8,128)(2,1)} %get-tuple-element.53.q_ref.k_ref.v_ref, bf16[16,2,2,64,512]{4,3,2,1,0:T(8,128)(2,1)} %bitcast.8.pk_ref.pv_ref, bf16[16,2,2,64,512]{4,3,2,1,0:T(8,128)(2,1)} %bitcast.8.pk_ref.pv_ref, ...), custom_call_target="tpu_custom_call" | custom-call | flops 2147483648 | bytes 31457280 | tf_op jit(solution)/shard_map/attend_other/pallas_call | solution.py:648
  312.3 11.5 %all-gather.2.cloned.1.call-done.w_ref.wg0.wg1.wu0.wu1.wd0.wd1.wo_ref = bf16[1024,9472]{1,0:T(8,128)(2,1)} async-done(((bf16[64,9472]{1,0:T(8,128)(2,1)}), bf16[1024,9472]{1,0:T(8,128)(2,1)}) %all-gather.2.cloned.1.call-update) | async-done | bytes 19398672 | tf_op jit(solution)/shard_map/all_gather | solution.py:1506
  323.8 11.5 %mix.1 = (f32[2048,1024]{1,0:T(8,128)}, bf16[2048,1024]{1,0:T(8,128)(2,1)}) custom-call(bf16[2048,1024]{1,0:T(8,128)(2,1)} %bitcast.25, bf16[2048,1024]{1,0:T(8,128)(2,1)} %get-tuple-element.59.ctx_ref, f32[1,1024]{1,0:T(1,128)} %get-tuple-element.90.gain_ref, bf16[1024,9472]{1,0:T(8,128)(2,1)} %all-gather.2.cloned.1.call-done.w_ref.wg0.wg1.wu0.wu1.wd0.wd1.wo_ref), custom_call_target="tpu_custom_call" | custom-call | flops 4294967296 | bytes 23068672 | tf_op jit(solution)/shard_map/mix/pallas_call | solution.py:731
  335.3 152.5 %ffn.1 = (bf16[512,4224]{1,0:T(8,128)(2,1)}, f32[1,1024]{1,0:T(1,128)}, bf16[2048,1024]{1,0:T(8,128)(2,1)}, f32[2048,1024]{1,0:T(8,128)}, bf16[2048,1024]{1,0:T(8,128)(2,1)}, /*index=5*/bf16[2048,1024]{1,0:T(8,128)(2,1)}) custom-call(bf16[2048,1024]{1,0:T(8,128)(2,1)} %get-tuple-element.61.n_ref, bf16[2048,1024]{1,0:T(8,128)(2,1)} %maximum_select_fusion.g_ref, ...), custom_call_target="tpu_custom_call" | custom-call | flops 106300440576 | bytes 62914560 | tf_op jit(solution)/shard_map/ffn/pallas_call | solution.py:941
  487.8 0.0 reduce-scatter.2.cloned.1.call-update
  487.9 5.6 all-to-all-start.1
  493.5 109.1 %attend_back.1 = (bf16[2048,1024]{1,0:T(8,128)(2,1)}, bf16[2048,1024]{1,0:T(8,128)(2,1)}, bf16[2048,1024]{1,0:T(8,128)(2,1)}) custom-call(s32[130]{0:T(256)} %pad_add_fusion.meta, bf16[2048,3072]{1,0:T(8,128)(2,1)} %get-tuple-element.53.q_ref.k_ref.v_ref, bf16[2048,3072]{1,0:T(8,128)(2,1)} %get-tuple-element.53.q_ref.k_ref.v_ref, ...), custom_call_target="tpu_custom_call" | custom-call | flops 47815065600 | bytes 41943040 | tf_op jit(solution)/shard_map/attend_back/pallas_call | solution.py:673
  602.6 94.0 %finish.1 = (bf16[2,1024,1024]{2,1,0:T(8,128)(2,1)}, f32[2,1024]{1,0:T(2,128)}, f32[64,2048]{1,0:T(8,128)}) custom-call(bf16[2048,1024]{1,0:T(8,128)(2,1)} %bitcast.26, f32[2048,1024]{1,0:T(8,128)} %get-tuple-element.68.gm_ref, bf16[2048,1024]{1,0:T(8,128)(2,1)} %get-tuple-element.69.n_ref, bf16[2048,1024]{1,0:T(8,128)(2,1)} %get-tuple-element.59.ctx_ref, ...), custom_call_target="tpu_custom_call" | custom-call | flops 30064771072 | bytes 83886080 | tf_op jit(solution)/shard_map/finish/pallas_call | solution.py:1208
  696.6 6.7 convert_element_type.22
  703.3 0.6 fusion.8
  703.9 0.8 slice_bitcast_fusion
  704.7 2.1 convert_bitcast_fusion
  706.8 4.6 copy.39
  (13 shorter events, 0.0 us)
Async XLA Ops:
  7.2 316.6 %all-gather.2.cloned.1.call-start = ((), (), s32[]{:S(2)}) async-start(), calls=%async_computation.3 | async-start | bytes 20611072 | tf_op jit(solution)/shard_map/all_gather | solution.py:1506
  149.4 141.8 %all-to-all-start = ((bf16[32,128,512]{2,1,0:T(8,128)(2,1)}), bf16[32,128,512]{2,1,0:T(8,128)(2,1)}, u32[]{:S(2)}, u32[]{:S(2)}) async-start(bf16[32,128,512]{2,1,0:T(8,128)(2,1)} %pick_rows.1), calls=%async_computation | async-start | bytes 8388608 | tf_op jit(solution)/shard_map/all_to_all | solution.py:1513
  153.0 551.7 %reduce-scatter.2.cloned.1.call-start = ((), (), s32[]{:S(2)}) async-start(), calls=%async_computation.4 | async-start | bytes 4866048 | tf_op jit(solution)/shard_map/reduce_scatter | solution.py:1529
  153.4 5.7 copy-start.4
  153.4 6.3 copy-start.2
  153.4 6.2 copy-start.3
  157.5 93.5 %collective-permute-start = (bf16[1024,1024]{1,0:T(8,128)(2,1)}, bf16[1024,1024]{1,0:T(8,128)(2,1)}, u32[]{:S(2)}, u32[]{:S(2)}) collective-permute-start(bf16[1024,1024]{1,0:T(8,128)(2,1)} %get-tuple-element.80), channel_id=1, source_target_pairs={{0,1},{1,0},{2,3},{3,2},{4,5},{5,4},{6,7},{7,6},{8,9},{9,8},{10,11... | collective-permute-start | bytes 6291464 | tf_op jit(solution)/shard_map/ppermute | solution.py:1476
  487.9 114.7 %all-to-all-start.1 = ((bf16[2,1024,1024]{2,1,0:T(8,128)(2,1)}), bf16[2,1024,1024]{2,1,0:T(8,128)(2,1)}, u32[]{:S(2)}, u32[]{:S(2)}) async-start(bf16[2,1024,1024]{2,1,0:T(8,128)(2,1)} %bitcast.22), calls=%async_computation.1 | async-start | bytes 8388608 | tf_op jit(solution)/shard_map/all_to_all | solution.py:1533
  696.6 6.7 copy-start.1
  696.6 7.3 %copy-start = (f32[64,2048]{1,0:T(8,128)S(1)}, f32[64,2048]{1,0:T(8,128)}, u32[]{:S(2)}) copy-start(f32[64,2048]{1,0:T(8,128)} %get-tuple-element.77) | copy-start | bytes 1572868
Sparse Core Ops, SparseCore 0:
  142.0 181.7 all-gather.1
  488.0 96.1 reduce-scatter.1

commit v9 on v8

--- a/solution.py
+++ b/solution.py
@@ -727,10 +727,11 @@
 
 def mix(x, context, gain, weights):
     width = x.shape[1]
-    row = pl.BlockSpec((ROWS, width), lambda i: (i, 0))
+    rows = ROWS // 2
+    row = pl.BlockSpec((rows, width), lambda i: (i, 0))
     return pl.pallas_call(
         mix_kernel,
-        grid=(L // ROWS,),
+        grid=(L // rows,),
         in_specs=[row, row, pl.BlockSpec((1, width), lambda i: (0, 0)), pl.BlockSpec((width, width), lambda i: (0, 0))],
         out_specs=[row, row],
         out_shape=[jax.ShapeDtypeStruct((L, width), F32), jax.ShapeDtypeStruct((L, width), BF16)],

time: 722 us -> 722 us (level)
  no operation moved by 1% of the time
where the time goes in v9:
time: 722 us; the launch traced here: 718 us
  Pallas kernels  611 us (85%)
  waiting for transfers between devices  46.9 us (6%)
  other arithmetic  19.9 us (3%)
  local copies, waits for them, and re-layouts  15.3 us (2%)
  between operations  14.4 us (2%)
  starting transfers between devices  11.2 us (2%)
    pallas_call x1, Pallas kernels, ffn(): pl.pallas_call(functools.partial(ffn_kernel, devices=devices), grid=(tile...  152 us
    pallas_call x1, Pallas kernels, spread(): pl.pallas_call(spread_kernel, in_specs=[anywhere, anywhere, anywhere, vme...  128 us
    pallas_call x1, Pallas kernels, attend_back(): pl.pallas_call(functools.partial(attend_back_kernel, pair=pair), grid_spe...  109 us
    pallas_call x1, Pallas kernels, finish(): pl.pallas_call(functools.partial(finish_kernel, devices=devices), in_spec...  92.9 us
    pallas_call x1, Pallas kernels, attend(): pl.pallas_call(functools.partial(attend_kernel, pair=pair), grid_spec=plt...  64.6 us
    all_to_all x1, waiting for transfers between devices, sequence_body(): lax.all_to_all(sent, ('dp', 'tensor'), split_axis=0, concat_axis=0, tiled...  35.4 us
    pallas_call x1, Pallas kernels, project(): pl.pallas_call(project_kernel, grid=(L // ROWS,), in_specs=[row(width), p...  24.3 us
    pallas_call x1, Pallas kernels, attend_other(): pl.pallas_call(functools.partial(attend_other_kernel, pair=pair), grid_sp...  21.1 us
  transfers between devices with their start and end apart: 5, of which 2 were waited for; matrix products, arithmetic and copies ran while one was open for 3% of the time, Pallas kernels for 44%

profile of v9, /device:TPU:0, one launch (start us, length us, event | category | flops | bytes accessed | tf_op | source)
XLA Modules:
  0.0 718.4 jit_solution(4102682467496917857)
XLA Ops:
  7.2 0.0 all-gather.2.cloned.1.call-start
  7.2 0.7 convert_bitcast_fusion.1
  7.9 0.1 copy.35
  8.0 0.8 copy.36
  8.8 0.8 copy.37
  9.5 0.1 pad.16.clone
  9.6 1.6 pad_maximum_fusion.1.small_ref
  11.2 0.7 fusion.3.extra_ref
  11.9 2.0 pad_maximum_fusion.big_ref
  13.8 128.0 %spread.1 = (bf16[2,1024,1024]{2,1,0:T(8,128)(2,1)}, bf16[2,1024,512]{2,1,0:T(8,128)(2,1)}, bf16[2,1024,512]{2,1,0:T(8,128)(2,1)}, bf16[16,2,2,64,512]{4,3,2,1,0...) custom-call(bf16[2,1024,1024]{2,1,0:T(8,128)(2,1)} %tok_ref.1, bf16[2,1024,512]{2,1,0:T(8,128)(2,1)} %ck_ref.1, ...), custom_call_target="tpu_custom_call" | custom-call | bytes 314572800 | tf_op jit(solution)/shard_map/spread/pallas_call | solution.py:1451
  141.8 0.0 all-gather.2.cloned.1.call-update
  141.8 1.0 slice.46
  142.8 0.2 slice_reduce_fusion
  143.0 0.1 reshape_squeeze.11
  143.1 0.6 reshape.72.table
  143.7 5.6 pick_rows.1
  149.4 3.6 all-to-all-start
  153.0 0.3 reduce-scatter.2.cloned.1.call-start
  153.4 0.0 copy-start.4
  153.4 0.0 copy-start.2
  153.4 0.0 copy-start.3
  153.4 4.1 dynamic-slice_bitcast_fusion.1
  157.5 1.6 collective-permute-start
  159.0 0.6 dynamic_slice.16
  159.6 0.1 copy.34
  159.7 0.1 reshape_squeeze.10
  159.8 0.1 copy.33
  159.9 0.1 reshape_squeeze.9
  160.0 1.3 pad_add_fusion.meta
  161.3 0.2 fusion.4
  161.4 0.6 fusion.9
  162.1 24.3 %project.1 = (bf16[2048,1024]{1,0:T(8,128)(2,1)}, bf16[2048,3072]{1,0:T(8,128)(2,1)}) custom-call(bf16[2048,1024]{1,0:T(8,128)(2,1)} %bitcast.24, f32[1,1024]{1,0:T(1,128)} %get-tuple-element.91.gain_ref, bf16[1024,3200]{1,0:T(8,128)(2,1)} %get-tuple-element.52.w_ref), custom_call_target="tpu_custom_call" | custom-call | flops 12884901888 | bytes 27262976 | tf_op jit(solution)/shard_map/project/pallas_call | solution.py:709
  186.4 64.6 %attend.1 = (f32[2048,1024]{1,0:T(8,128)}, f32[2048,1024]{1,0:T(8,128)}) custom-call(s32[130]{0:T(256)} %pad_add_fusion.meta, bf16[2048,3072]{1,0:T(8,128)(2,1)} %get-tuple-element.53.q_ref.k_ref.v_ref, bf16[2048,3072]{1,0:T(8,128)(2,1)} %get-tuple-element.53.q_ref.k_ref.v_ref, bf16[2048,3072]{1,0:T(8,128)(2,1)} %get-tuple-element.53.q_ref.k_ref.v_ref, ...), custom_call_target="tpu_custom_call" | custom-call | flops 40265318400 | bytes 31457280 | tf_op jit(solution)/shard_map/attend/pallas_call | solution.py:625
  251.0 4.9 maximum_select_fusion.g_ref
  255.9 35.4 %all-to-all-done = bf16[32,128,512]{2,1,0:T(8,128)(2,1)} async-done(((bf16[32,128,512]{2,1,0:T(8,128)(2,1)}), bf16[32,128,512]{2,1,0:T(8,128)(2,1)}, u32[]{:S(2)}, u32[]{:S(2)}) %all-to-all-start) | async-done | bytes 4194336 | tf_op jit(solution)/shard_map/all_to_all | solution.py:1514
  291.2 21.1 %attend_other.1 = (bf16[2048,1024]{1,0:T(8,128)(2,1)}, f32[2048,1024]{1,0:T(8,128)}) custom-call(s32[130]{0:T(256)} %pad_add_fusion.meta, bf16[2048,3072]{1,0:T(8,128)(2,1)} %get-tuple-element.53.q_ref.k_ref.v_ref, bf16[16,2,2,64,512]{4,3,2,1,0:T(8,128)(2,1)} %bitcast.8.pk_ref.pv_ref, bf16[16,2,2,64,512]{4,3,2,1,0:T(8,128)(2,1)} %bitcast.8.pk_ref.pv_ref, ...), custom_call_target="tpu_custom_call" | custom-call | flops 2147483648 | bytes 31457280 | tf_op jit(solution)/shard_map/attend_other/pallas_call | solution.py:648
  312.3 11.5 %all-gather.2.cloned.1.call-done.w_ref.wg0.wg1.wu0.wu1.wd0.wd1.wo_ref = bf16[1024,9472]{1,0:T(8,128)(2,1)} async-done(((bf16[64,9472]{1,0:T(8,128)(2,1)}), bf16[1024,9472]{1,0:T(8,128)(2,1)}) %all-gather.2.cloned.1.call-update) | async-done | bytes 19398672 | tf_op jit(solution)/shard_map/all_gather | solution.py:1507
  323.8 12.5 %mix.1 = (f32[2048,1024]{1,0:T(8,128)}, bf16[2048,1024]{1,0:T(8,128)(2,1)}) custom-call(bf16[2048,1024]{1,0:T(8,128)(2,1)} %bitcast.25, bf16[2048,1024]{1,0:T(8,128)(2,1)} %get-tuple-element.59.ctx_ref, f32[1,1024]{1,0:T(1,128)} %get-tuple-element.90.gain_ref, bf16[1024,9472]{1,0:T(8,128)(2,1)} %all-gather.2.cloned.1.call-done.w_ref.wg0.wg1.wu0.wu1.wd0.wd1.wo_ref), custom_call_target="tpu_custom_call" | custom-call | flops 4294967296 | bytes 23068672 | tf_op jit(solution)/shard_map/mix/pallas_call | solution.py:732
  336.3 152.5 %ffn.1 = (bf16[512,4224]{1,0:T(8,128)(2,1)}, f32[1,1024]{1,0:T(1,128)}, bf16[2048,1024]{1,0:T(8,128)(2,1)}, f32[2048,1024]{1,0:T(8,128)}, bf16[2048,1024]{1,0:T(8,128)(2,1)}, /*index=5*/bf16[2048,1024]{1,0:T(8,128)(2,1)}) custom-call(bf16[2048,1024]{1,0:T(8,128)(2,1)} %get-tuple-element.61.n_ref, bf16[2048,1024]{1,0:T(8,128)(2,1)} %maximum_select_fusion.g_ref, ...), custom_call_target="tpu_custom_call" | custom-call | flops 106300440576 | bytes 62914560 | tf_op jit(solution)/shard_map/ffn/pallas_call | solution.py:942
  488.8 0.0 reduce-scatter.2.cloned.1.call-update
  488.8 5.6 all-to-all-start.1
  494.5 109.1 %attend_back.1 = (bf16[2048,1024]{1,0:T(8,128)(2,1)}, bf16[2048,1024]{1,0:T(8,128)(2,1)}, bf16[2048,1024]{1,0:T(8,128)(2,1)}) custom-call(s32[130]{0:T(256)} %pad_add_fusion.meta, bf16[2048,3072]{1,0:T(8,128)(2,1)} %get-tuple-element.53.q_ref.k_ref.v_ref, bf16[2048,3072]{1,0:T(8,128)(2,1)} %get-tuple-element.53.q_ref.k_ref.v_ref, ...), custom_call_target="tpu_custom_call" | custom-call | flops 47815065600 | bytes 41943040 | tf_op jit(solution)/shard_map/attend_back/pallas_call | solution.py:673
  603.5 92.9 %finish.1 = (bf16[2,1024,1024]{2,1,0:T(8,128)(2,1)}, f32[2,1024]{1,0:T(2,128)}, f32[64,2048]{1,0:T(8,128)}) custom-call(bf16[2048,1024]{1,0:T(8,128)(2,1)} %bitcast.26, f32[2048,1024]{1,0:T(8,128)} %get-tuple-element.68.gm_ref, bf16[2048,1024]{1,0:T(8,128)(2,1)} %get-tuple-element.69.n_ref, bf16[2048,1024]{1,0:T(8,128)(2,1)} %get-tuple-element.59.ctx_ref, ...), custom_call_target="tpu_custom_call" | custom-call | flops 30064771072 | bytes 83886080 | tf_op jit(solution)/shard_map/finish/pallas_call | solution.py:1209
  696.5 6.7 convert_element_type.22
  703.2 0.6 fusion.8
  703.8 0.8 slice_bitcast_fusion
  704.6 2.1 convert_bitcast_fusion
  706.7 4.6 copy.39
  (13 shorter events, 0.0 us)
Async XLA Ops:
  7.2 316.6 %all-gather.2.cloned.1.call-start = ((), (), s32[]{:S(2)}) async-start(), calls=%async_computation.3 | async-start | bytes 20611072 | tf_op jit(solution)/shard_map/all_gather | solution.py:1507
  149.4 141.8 %all-to-all-start = ((bf16[32,128,512]{2,1,0:T(8,128)(2,1)}), bf16[32,128,512]{2,1,0:T(8,128)(2,1)}, u32[]{:S(2)}, u32[]{:S(2)}) async-start(bf16[32,128,512]{2,1,0:T(8,128)(2,1)} %pick_rows.1), calls=%async_computation | async-start | bytes 8388608 | tf_op jit(solution)/shard_map/all_to_all | solution.py:1514
  153.0 551.6 %reduce-scatter.2.cloned.1.call-start = ((), (), s32[]{:S(2)}) async-start(), calls=%async_computation.4 | async-start | bytes 4866048 | tf_op jit(solution)/shard_map/reduce_scatter | solution.py:1530
  153.4 5.7 copy-start.4
  153.4 6.3 copy-start.2
  153.4 6.2 copy-start.3
  157.5 93.5 %collective-permute-start = (bf16[1024,1024]{1,0:T(8,128)(2,1)}, bf16[1024,1024]{1,0:T(8,128)(2,1)}, u32[]{:S(2)}, u32[]{:S(2)}) collective-permute-start(bf16[1024,1024]{1,0:T(8,128)(2,1)} %get-tuple-element.80), channel_id=1, source_target_pairs={{0,1},{1,0},{2,3},{3,2},{4,5},{5,4},{6,7},{7,6},{8,9},{9,8},{10,11... | collective-permute-start | bytes 6291464 | tf_op jit(solution)/shard_map/ppermute | solution.py:1477
  488.8 114.7 %all-to-all-start.1 = ((bf16[2,1024,1024]{2,1,0:T(8,128)(2,1)}), bf16[2,1024,1024]{2,1,0:T(8,128)(2,1)}, u32[]{:S(2)}, u32[]{:S(2)}) async-start(bf16[2,1024,1024]{2,1,0:T(8,128)(2,1)} %bitcast.22), calls=%async_computation.1 | async-start | bytes 8388608 | tf_op jit(solution)/shard_map/all_to_all | solution.py:1534
  696.5 6.7 copy-start.1
  696.5 7.3 %copy-start = (f32[64,2048]{1,0:T(8,128)S(1)}, f32[64,2048]{1,0:T(8,128)}, u32[]{:S(2)}) copy-start(f32[64,2048]{1,0:T(8,128)} %get-tuple-element.77) | copy-start | bytes 1572868
Sparse Core Ops, SparseCore 0:
  142.0 181.7 all-gather.1
  489.0 96.1 reduce-scatter.1
